TPU v7x, 256 devices: a whole 4x4x8 slice. The times are simulated.
256 devices in a mesh: ctx: 64 (over z, y, core), head: 4 (over x).
Axes of the slice: x: 4, y: 4, z: 8, core: 2. Of those that a mesh axis runs over, the one named last changes fastest.
Arguments:
- queries: bfloat16 [65536, 1024], P('ctx', 'head'), may hold values from -6 to 6
- key_rows: bfloat16 [65536, 128], P('ctx'), may hold values from -6 to 6
- value_rows: bfloat16 [65536, 128], P('ctx'), may hold values from -6 to 6
- out_grad: bfloat16 [65536, 1024], P('ctx', 'head'), may hold values from -6 to 6
- block_lists: int32 [512, 8], P('ctx'), may hold values from -1 to 511, as said below
Outputs:
- attended: bfloat16 [65536, 1024], P('ctx', 'head')
- query_grad: bfloat16 [65536, 1024], P('ctx', 'head')
- key_grad: bfloat16 [65536, 128], P(('ctx', 'head'))
- value_grad: bfloat16 [65536, 128], P(('ctx', 'head'))
Inputs may be any that keep to these rules, and one draw needn't show every extreme that they name: `block_lists`: entry 0 of row b is the position block of row b's own tokens. Every other entry is -1 or a block lying wholly before it whose rows belong to another index of ctx; the blocks of one row are distinct. Over the 8 rows of one index of ctx, at most 1 entries name blocks of any one other index, and in every draw some index has exactly 1 entries on one other.
All inputs are finite; a program needn't handle non-finite values.
Results may differ from a plain program's by a relative error of at most 0.022.
Values may be sent and summed in bfloat16 or wider, within the bound.
A program may use at most 128 MiB of HBM per device.

v0:
```python
import math

import jax
import jax.numpy as jnp
from jax import lax
from jax.sharding import PartitionSpec as P

HD = 128
BLK = 128
SEL = 8
QB = 8


NEG_FILL = -1e30


def block_home(block, half_blocks, pair_count):
    stretch_idx = block // half_blocks
    early_side = stretch_idx < pair_count
    owner_dev = jnp.where(early_side, stretch_idx, 2 * pair_count - 1 - stretch_idx)
    local_blk = block % half_blocks + jnp.where(early_side, 0, half_blocks)
    return (owner_dev, local_blk)


def entry_slots(list_rows, half_blocks, pair_count):
    extras = list_rows[:, 1:].reshape(-1)
    usable = extras >= 0
    owner_dev, local_blk = block_home(jnp.maximum(extras, 0), half_blocks, pair_count)
    onehot_own = (
        (owner_dev[:, None] == jnp.arange(pair_count, dtype=jnp.int32)[None, :]) & usable[:, None]
    ).astype(jnp.int32)
    running = jnp.cumsum(onehot_own, axis=0)
    rank_in = jnp.sum(onehot_own * running, axis=1) - 1
    return (owner_dev, local_blk, rank_in, usable)


def head_exchange(x, head_idx, count):
    ahead = x[(head_idx + jnp.arange(count, dtype=jnp.int32)) % count]
    got = [ahead[0]]
    for k in range(1, count):
        got.append(lax.ppermute(ahead[k], "head", [(j, (j + k) % count) for j in range(count)]))
    order = (head_idx - jnp.arange(count, dtype=jnp.int32)) % count
    return jnp.stack(got)[order]


def on_device(queries, key_rows, value_rows, out_grad, block_lists):
    pair_count = lax.axis_size("ctx")
    head_count = lax.axis_size("head")
    half_blocks = QB // 2
    capacity = (QB * (SEL - 1) + pair_count - 2) // (pair_count - 1)
    total_slots = pair_count * capacity
    device = lax.axis_index("ctx")
    head_idx = lax.axis_index("head")
    score_scale = 1.0 / math.sqrt(HD)
    rows_here = QB // head_count
    extras = SEL - 1
    entry_count = QB * extras
    my_entries = rows_here * extras
    part_rows = 2 * BLK // head_count
    owner_dev, local_blk, rank_in, usable = entry_slots(block_lists, half_blocks, pair_count)
    slot_idx = jnp.where(usable, owner_dev * capacity + rank_in, total_slots)
    req_table = (
        jnp.full((total_slots + 1,), -1, jnp.int32).at[slot_idx].set(local_blk)[:total_slots]
    )
    requested = lax.all_to_all(
        req_table.reshape(pair_count, capacity), "ctx", split_axis=0, concat_axis=0, tiled=True
    )
    rows_in, cols_in = queries.shape
    inputs_split = jnp.stack(
        [
            queries.reshape(head_count, rows_in // head_count, cols_in),
            out_grad.reshape(head_count, rows_in // head_count, cols_in),
        ],
        axis=1,
    )
    inputs_rows = head_exchange(inputs_split, head_idx, head_count)
    inputs_rows = jnp.transpose(inputs_rows, (1, 2, 0, 3)).reshape(2, rows_in // head_count, head_count * cols_in)
    q_rows = inputs_rows[0]
    g_rows = inputs_rows[1]
    heads_all = q_rows.shape[1] // HD
    kv_blocks = jnp.stack([key_rows.reshape(QB, BLK, HD), value_rows.reshape(QB, BLK, HD)], axis=1)
    kv_parts = kv_blocks.reshape(QB, head_count, part_rows, HD)
    my_part = lax.dynamic_index_in_dim(kv_parts, head_idx, axis=1, keepdims=False)
    send_parts = my_part[jnp.maximum(requested, 0)]
    fetched_part = lax.all_to_all(send_parts, "ctx", split_axis=0, concat_axis=0, tiled=True).reshape(
        total_slots, part_rows, HD
    )
    entry_slot = jnp.where(usable, slot_idx, 0).reshape(head_count, my_entries)
    share = fetched_part[entry_slot]
    got = head_exchange(share, head_idx, head_count)
    remote_kv = jnp.transpose(got, (1, 0, 2, 3)).reshape(rows_here, extras, 2, BLK, HD)
    first_row = head_idx * rows_here
    own_kv = lax.dynamic_slice_in_dim(kv_blocks, first_row, rows_here, axis=0)
    kv_tiles = jnp.concatenate([own_kv[:, None], remote_kv], axis=1)
    key_tile = kv_tiles[:, :, 0]
    value_tile = kv_tiles[:, :, 1]
    my_lists = lax.dynamic_slice_in_dim(block_lists, first_row, rows_here, axis=0)
    local_ids = first_row + jnp.arange(rows_here, dtype=jnp.int32)
    own_block = jnp.where(
        local_ids < half_blocks,
        device * half_blocks + local_ids,
        (2 * pair_count - 1 - device) * half_blocks + local_ids - half_blocks,
    )
    offsets = jnp.arange(BLK, dtype=jnp.int32)
    query_pos = own_block[:, None] * BLK + offsets[None, :]
    key_pos = jnp.maximum(my_lists, 0)[:, :, None] * BLK + offsets[None, None, :]
    visible = (my_lists >= 0)[:, None, :, None] & (
        key_pos[:, None, :, :] <= query_pos[:, :, None, None]
    )
    q_blocks = q_rows.reshape(rows_here, BLK, heads_all, HD)
    g_blocks = g_rows.reshape(rows_here, BLK, heads_all, HD)
    scores = (
        jnp.einsum("qihd,qsjd->qhisj", q_blocks, key_tile, preferred_element_type=jnp.float32)
        * score_scale
    )
    scores = jnp.where(visible[:, None], scores, NEG_FILL)
    row_max = jnp.max(scores, axis=(3, 4), keepdims=True)
    weights = jnp.exp(scores - row_max)
    row_total = jnp.sum(weights, axis=(3, 4), keepdims=True)
    summed = jnp.einsum(
        "qhisj,qsjd->qihd",
        weights.astype(jnp.bfloat16),
        value_tile,
        preferred_element_type=jnp.float32,
    )
    attended = (summed / jnp.transpose(row_total[..., 0, 0], (0, 2, 1))[..., None]).astype(
        jnp.bfloat16
    )
    log_total = row_max + jnp.log(row_total)
    probability = jnp.exp(scores - log_total)
    row_delta = jnp.sum(g_blocks.astype(jnp.float32) * attended.astype(jnp.float32), axis=3)
    grad_p = jnp.einsum(
        "qihd,qsjd->qhisj", g_blocks, value_tile, preferred_element_type=jnp.float32
    )
    grad_s = (probability * (grad_p - jnp.transpose(row_delta, (0, 2, 1))[..., None, None])).astype(
        jnp.bfloat16
    )
    query_grad = (
        jnp.einsum("qhisj,qsjd->qihd", grad_s, key_tile, preferred_element_type=jnp.float32)
        * score_scale
    ).astype(jnp.bfloat16)
    key_part = (
        jnp.einsum("qhisj,qihd->qsjd", grad_s, q_blocks, preferred_element_type=jnp.float32)
        * score_scale
    )
    value_part = jnp.einsum(
        "qhisj,qihd->qsjd",
        probability.astype(jnp.bfloat16),
        g_blocks,
        preferred_element_type=jnp.float32,
    )
    grad_tiles = jnp.stack([key_part, value_part], axis=2)
    remote_grad = grad_tiles[:, 1:].astype(jnp.bfloat16).reshape(my_entries, head_count, part_rows, HD)
    back = head_exchange(jnp.transpose(remote_grad, (1, 0, 2, 3)), head_idx, head_count).reshape(
        entry_count, part_rows, HD
    )
    slot_entry = (
        jnp.full((total_slots + 1,), entry_count, jnp.int32)
        .at[slot_idx]
        .set(jnp.arange(entry_count, dtype=jnp.int32))[:total_slots]
    )
    back = jnp.concatenate([back, jnp.zeros((1, part_rows, HD), back.dtype)], axis=0)
    outgoing_part = back[slot_entry]
    returned = lax.all_to_all(
        outgoing_part.reshape(pair_count, capacity, part_rows, HD),
        "ctx",
        split_axis=0,
        concat_axis=0,
        tiled=True,
    ).astype(jnp.float32)
    target = jnp.where(requested >= 0, requested, QB).reshape(-1)
    returned_sum = (
        jnp.zeros((QB + 1, part_rows, HD), jnp.float32)
        .at[target]
        .add(returned.reshape(-1, part_rows, HD))[:QB]
    )
    routed = head_exchange(returned_sum.reshape(head_count, rows_here, part_rows, HD), head_idx, head_count)
    routed = jnp.transpose(routed, (1, 0, 2, 3)).reshape(rows_here, 2, BLK, HD)
    final = grad_tiles[:, 0] + routed
    out_rows = rows_here * BLK
    out_cols = heads_all * HD // head_count
    outputs_split = jnp.transpose(
        jnp.stack([attended, query_grad]).reshape(2, out_rows, head_count, out_cols), (2, 0, 1, 3)
    )
    outputs_rows = head_exchange(outputs_split, head_idx, head_count)
    return (
        outputs_rows[:, 0].reshape(head_count * out_rows, out_cols),
        outputs_rows[:, 1].reshape(head_count * out_rows, out_cols),
        final[:, 0].reshape(rows_here * BLK, HD).astype(jnp.bfloat16),
        final[:, 1].reshape(rows_here * BLK, HD).astype(jnp.bfloat16),
    )

def solution(mesh):
    return jax.shard_map(
        on_device,
        mesh=mesh,
        in_specs=(
            P("ctx", "head"),
            P("ctx", None),
            P("ctx", None),
            P("ctx", "head"),
            P("ctx", None),
        ),
        out_specs=(
            P("ctx", "head"),
            P("ctx", "head"),
            P(("ctx", "head"), None),
            P(("ctx", "head"), None),
        ),
        check_vma=False,
    )
```

profile of v0, /device:TPU:8, one launch (start us, length us, event | category | flops | bytes accessed | tf_op | source)
XLA Modules:
  0.0 166.7 jit_solution(5275876774082835907)
XLA Ops:
  0.7 0.8 compare_and_fusion.1
  1.5 0.8 fusion.44
  3.3 0.8 scatter_custom_fusion
  4.7 12.1 %all-to-all-start = ((s32[64,1,1]{2,1,0:T(1,128)}), s32[64,1,1]{2,1,0:T(1,128)S(1)}, u32[]{:S(2)}, u32[]{:S(2)}) async-start(s32[64,1,1]{2,1,0:T(1,128)} %copy.79), calls=%async_computation | async-start | bytes 65536 | tf_op jit(solution)/shard_map/all_to_all | solution.py:65
  16.9 1.3 pad_maximum_fusion.1
  18.2 1.1 pad_maximum_fusion.6
  19.9 5.5 %all-to-all-done = s32[64,1,1]{2,1,0:T(1,128)S(1)} async-done(((s32[64,1,1]{2,1,0:T(1,128)}), s32[64,1,1]{2,1,0:T(1,128)S(1)}, u32[]{:S(2)}, u32[]{:S(2)}) %all-to-all-start) | async-done | bytes 288 | tf_op jit(solution)/shard_map/all_to_all | solution.py:65
  25.4 2.7 %fusion.69 = (s32[64]{0:T(128)}, s32[64]{0:T(128)S(1)}) fusion(s32[64,1,1]{2,1,0:T(1,128)S(1)} %all-to-all-done), kind=kLoop, calls=%fused_computation.158 | loop fusion | flops 64 | bytes 768 | tf_op jit(solution)/shard_map/all_to_all | solution.py:65
  28.1 1.7 gather_fusion
  29.8 5.5 %all-to-all-start.1 = ((bf16[64,1,64,128]{3,2,1,0:T(8,128)(2,1)}), bf16[64,1,64,128]{3,2,1,0:T(8,128)(2,1)S(1)}, u32[]{:S(2)}, u32[]{:S(2)}) async-start(bf16[64,1,64,128]{3,2,1,0:T(8,128)(2,1)} %bitcast.8), calls=%async_computation.1 | async-start | bytes 2097152 | tf_op jit(solution)/shard_map/all_to_all | solution.py:85
  35.3 0.9 fusion.73
  36.2 2.8 %collective-permute-start.5 = (bf16[2,256,256]{2,1,0:T(8,128)(2,1)}, bf16[2,256,256]{2,1,0:T(8,128)(2,1)S(1)}, u32[]{:S(2)}, u32[]{:S(2)}) collective-permute-start(bf16[2,256,256]{2,1,0:T(8,128)(2,1)} %get-tuple-element.21), channel_id=1, source_target_pairs={{0,3},{1,0},{2,1},{3,2},{4,7},{5,4},{6,5},{7,6},{8,11},{9,8},{10,9... | collective-permute-start | bytes 786440 | tf_op jit(solution)/shard_map/ppermute | solution.py:41
  39.0 0.8 collective-permute-start.4
  39.8 0.9 collective-permute-start.3
  42.5 1.3 scatter_custom_fusion.1
  44.3 6.5 %collective-permute-done.5 = bf16[2,256,256]{2,1,0:T(8,128)(2,1)S(1)} collective-permute-done((bf16[2,256,256]{2,1,0:T(8,128)(2,1)}, bf16[2,256,256]{2,1,0:T(8,128)(2,1)S(1)}, u32[]{:S(2)}, u32[]{:S(2)}) %collective-permute-start.5) | collective-permute-done | bytes 262176 | tf_op jit(solution)/shard_map/ppermute | solution.py:41
  50.8 3.6 %collective-permute-done.3 = bf16[2,256,256]{2,1,0:T(8,128)(2,1)S(1)} collective-permute-done((bf16[2,256,256]{2,1,0:T(8,128)(2,1)S(1)}, bf16[2,256,256]{2,1,0:T(8,128)(2,1)S(1)}, u32[]{:S(2)}, u32[]{:S(2)}) %collective-permute-start.3) | collective-permute-done | bytes 262176 | tf_op jit(solution)/shard_map/ppermute | solution.py:41
  54.4 1.1 pad_maximum_fusion.2
  55.5 0.7 gather_fusion.5
  56.2 8.0 %all-to-all-done.1 = bf16[64,1,64,128]{3,2,1,0:T(8,128)(2,1)S(1)} async-done(((bf16[64,1,64,128]{3,2,1,0:T(8,128)(2,1)}), bf16[64,1,64,128]{3,2,1,0:T(8,128)(2,1)S(1)}, u32[]{:S(2)}, u32[]{:S(2)}) %all-to-all-start.1) | async-done | bytes 1048608 | tf_op jit(solution)/shard_map/all_to_all | solution.py:85
  64.2 0.8 gather_fusion.1
  65.8 0.9 fusion.75
  66.7 2.8 %collective-permute-start.2 = (bf16[14,64,128]{2,1,0:T(8,128)(2,1)}, bf16[14,64,128]{2,1,0:T(8,128)(2,1)}, u32[]{:S(2)}, u32[]{:S(2)}) collective-permute-start(bf16[14,64,128]{2,1,0:T(8,128)(2,1)} %get-tuple-element.29), channel_id=1, source_target_pairs={{0,3},{1,0},{2,1},{3,2},{4,7},{5,4},{6,5},{7,6},{8,11},{9,8},{10,9... | collective-permute-start | bytes 688136 | tf_op jit(solution)/shard_map/ppermute | solution.py:41
  69.4 0.8 collective-permute-start.1
  70.2 0.9 collective-permute-start
  72.4 1.1 copy.89
  73.5 5.0 %collective-permute-done.2 = bf16[14,64,128]{2,1,0:T(8,128)(2,1)} collective-permute-done((bf16[14,64,128]{2,1,0:T(8,128)(2,1)}, bf16[14,64,128]{2,1,0:T(8,128)(2,1)}, u32[]{:S(2)}, u32[]{:S(2)}) %collective-permute-start.2) | collective-permute-done | bytes 229408 | tf_op jit(solution)/shard_map/ppermute | solution.py:41
  78.6 1.1 collective-permute-done.1
  79.7 2.5 %collective-permute-done = bf16[14,64,128]{2,1,0:T(8,128)(2,1)} collective-permute-done((bf16[14,64,128]{2,1,0:T(8,128)(2,1)}, bf16[14,64,128]{2,1,0:T(8,128)(2,1)}, u32[]{:S(2)}, u32[]{:S(2)}) %collective-permute-start) | collective-permute-done | bytes 229408 | tf_op jit(solution)/shard_map/ppermute | solution.py:41
  82.2 1.3 pad_maximum_fusion.4
  83.5 0.8 gather_fusion.3
  84.5 1.3 fusion.5
  85.8 1.8 %fusion.2 = f32[2,8,128]{2,1,0:T(8,128)S(1)} fusion(f32[2,8,128,128,8]{3,2,4,1,0:T(8,128)S(1)} %get-tuple-element.40, f32[2,8,128]{2,1,0:T(8,128)S(1)} %get-tuple-element.39, pred[2,128,8,128]{1,3,2,0:T(8,128)(4,1)S(1)} %compare_and_fusion), kind=kLoop, calls=%fused_computation.22 | loop fusion | flops 8386560 | bytes 8667136 | tf_op jit(solution)/shard_map/reduce_sum | solution.py:119
  87.6 3.0 %multiply_reduce_fusion = (f32[2,128,8]{1,2,0:T(8,128)S(1)}, bf16[2,128,8,128]{1,3,2,0:T(8,128)(2,1)}) fusion(bf16[2,128,8,128]{1,3,2,0:T(8,128)(2,1)S(1)} %copy-done.6, f32[2,128,8]{1,2,0:T(8,128)S(1)} %bitcast.250, f32[2,8,128,128,8]{3,2,4,1,0:T(8,128)S(1)} %get-tuple-element.40, f32[2,8,128]{2,1,0:T(8,128)S(1)} %get-tuple-element.39, ...), kind=kOutput, calls=%fused_computation.50 | convolution fusion | flops 547878912 | bytes 10772480 | tf_op jit(solution)/shard_map/qhisj,qsjd->qihd/dot_general | solution.py:120
  90.6 2.0 %fusion.16 = f32[2,8,1,128,128]{4,3,1,0,2:T(8,128)S(1)} fusion(f32[2,8,128,128,8]{3,2,4,1,0:T(8,128)S(1)} %get-tuple-element.40, f32[2,8,128]{2,1,0:T(8,128)S(1)} %log_add_fusion, pred[2,128,8,128]{1,3,2,0:T(8,128)(4,1)S(1)} %compare_and_fusion, bf16[2,128,8,128,1]{3,2,1,0,4:T(8,128)(2,1)S(1)} %bitcast.216), kind=kOutput, calls=%fused_computation.35 | convolution fusion | flops 545259520 | bytes 10231808 | tf_op jit(solution)/shard_map/qhisj,qihd->qsjd/dot_general | solution.py:146
  92.6 2.8 %fusion.1 = bf16[2,8,128,8,128]{2,4,1,3,0:T(8,128)(2,1)S(1)} fusion(f32[2,8,128,128,8]{3,2,4,1,0:T(8,128)S(1)} %get-tuple-element.40, f32[2,8,128]{2,1,0:T(8,128)S(1)} %bitcast.251, f32[2,8,128]{2,1,0:T(8,128)S(1)} %log_add_fusion, pred[2,128,8,128]{1,3,2,0:T(8,128)(4,1)S(1)} %compare_and_fusion, bf16[2,128,8,128,1]{3,2,1,0,4:T(8,128)(2,1)S(1)} %bitcast.217, ...), kind=kOutput, calls=%fused_computation.18 | convolution fusion | flops 550502400 | bytes 14434304 | tf_op jit(solution)/shard_map/qihd,qsjd->qhisj/dot_general | solution.py:132
  95.5 1.3 fusion.21
  97.5 0.8 gather_fusion.8
  99.1 0.8 collective-permute-start.10
  99.9 0.8 collective-permute-start.9
  101.3 5.7 %collective-permute-done.11 = bf16[14,64,128]{2,1,0:T(8,128)(2,1)S(1)} collective-permute-done((bf16[14,64,128]{2,1,0:T(8,128)(2,1)S(1)}, bf16[14,64,128]{2,1,0:T(8,128)(2,1)S(1)}, u32[]{:S(2)}, u32[]{:S(2)}) %collective-permute-start.11) | collective-permute-done | bytes 229408 | tf_op jit(solution)/shard_map/ppermute | solution.py:41
  107.0 2.1 %collective-permute-done.10 = bf16[14,64,128]{2,1,0:T(8,128)(2,1)S(1)} collective-permute-done((bf16[14,64,128]{2,1,0:T(8,128)(2,1)S(1)}, bf16[14,64,128]{2,1,0:T(8,128)(2,1)S(1)}, u32[]{:S(2)}, u32[]{:S(2)}) %collective-permute-start.10) | collective-permute-done | bytes 229408 | tf_op jit(solution)/shard_map/ppermute | solution.py:41
  109.1 3.6 %collective-permute-done.9 = bf16[14,64,128]{2,1,0:T(8,128)(2,1)S(1)} collective-permute-done((bf16[14,64,128]{2,1,0:T(8,128)(2,1)S(1)}, bf16[14,64,128]{2,1,0:T(8,128)(2,1)S(1)}, u32[]{:S(2)}, u32[]{:S(2)}) %collective-permute-start.9) | collective-permute-done | bytes 229408 | tf_op jit(solution)/shard_map/ppermute | solution.py:41
  112.8 1.0 gather_fusion.9
  113.8 1.8 %gather_fusion.10 = bf16[64,64,128]{2,1,0:T(8,128)(2,1)} fusion(bf16[57,64,128]{2,1,0:T(8,128)(2,1)S(1)} %concatenate.8, s32[1024]{0:T(1024)} %pad_clamp_fusion), kind=kCustom, calls=%fused_computation.10 | custom fusion | bytes 2097408 | tf_op jit(solution)/shard_map/gather | solution.py:163
  115.6 6.6 %all-to-all-start.2 = ((bf16[64,1,64,128]{3,2,1,0:T(8,128)(2,1)}), bf16[64,1,64,128]{3,2,1,0:T(8,128)(2,1)}, u32[]{:S(2)}, u32[]{:S(2)}) async-start(bf16[64,1,64,128]{3,2,1,0:T(8,128)(2,1)} %bitcast.78), calls=%async_computation.2 | async-start | bytes 2097152 | tf_op jit(solution)/shard_map/all_to_all | solution.py:164
  122.3 3.1 %fusion.23 = bf16[2,128,8,128]{1,3,2,0:T(8,128)(2,1)S(1)} fusion(bf16[2,8,128,8,128]{2,4,1,3,0:T(8,128)(2,1)} %copy-done.1, bf16[2,1,2,128,128]{4,3,1,0,2:T(8,128)(2,1)S(1)} %copy_bitcast_fusion, bf16[2,7,2,128,128]{4,3,2,1,0:T(8,128)(2,1)} %bitcast.230), kind=kOutput, calls=%fused_computation.42 | convolution fusion | flops 538443776 | bytes 5767168 | tf_op jit(solution)/shard_map/qhisj,qsjd->qihd/dot_general | solution.py:139
  126.1 0.9 copy.94
  127.7 1.1 maximum_bitcast_fusion
  128.8 0.7 gather_fusion.6
  129.6 0.9 collective-permute-start.8
  131.1 0.8 collective-permute-start.6
  131.9 7.0 %collective-permute-done.8 = bf16[2,256,256]{2,1,0:T(8,128)(2,1)S(1)} collective-permute-done((bf16[2,256,256]{2,1,0:T(8,128)(2,1)S(1)}, bf16[2,256,256]{2,1,0:T(8,128)(2,1)S(1)}, u32[]{:S(2)}, u32[]{:S(2)}) %collective-permute-start.8) | collective-permute-done | bytes 262176 | tf_op jit(solution)/shard_map/ppermute | solution.py:41
  138.9 2.4 %collective-permute-done.7 = bf16[2,256,256]{2,1,0:T(8,128)(2,1)S(1)} collective-permute-done((bf16[2,256,256]{2,1,0:T(8,128)(2,1)S(1)}, bf16[2,256,256]{2,1,0:T(8,128)(2,1)S(1)}, u32[]{:S(2)}, u32[]{:S(2)}) %collective-permute-start.7) | collective-permute-done | bytes 262176 | tf_op jit(solution)/shard_map/ppermute | solution.py:41
  141.3 4.4 %collective-permute-done.6 = bf16[2,256,256]{2,1,0:T(8,128)(2,1)S(1)} collective-permute-done((bf16[2,256,256]{2,1,0:T(8,128)(2,1)S(1)}, bf16[2,256,256]{2,1,0:T(8,128)(2,1)S(1)}, u32[]{:S(2)}, u32[]{:S(2)}) %collective-permute-start.6) | collective-permute-done | bytes 262176 | tf_op jit(solution)/shard_map/ppermute | solution.py:41
  145.9 1.7 %gather_fusion.7 = bf16[4,2,256,256]{3,2,1,0:T(8,128)(2,1)} fusion(bf16[4,2,256,256]{3,2,1,0:T(8,128)(2,1)S(1)} %pad_maximum_fusion.3, s32[1024]{0:T(1024)} %pad_clamp_fusion.1), kind=kCustom, calls=%fused_computation.7 | custom fusion | bytes 2097168 | tf_op jit(solution)/shard_map/gather | solution.py:43
  147.6 3.4 %all-to-all-done.2 = bf16[64,1,64,128]{3,2,1,0:T(8,128)(2,1)} async-done(((bf16[64,1,64,128]{3,2,1,0:T(8,128)(2,1)}), bf16[64,1,64,128]{3,2,1,0:T(8,128)(2,1)}, u32[]{:S(2)}, u32[]{:S(2)}) %all-to-all-start.2) | async-done | bytes 1048608 | tf_op jit(solution)/shard_map/all_to_all | solution.py:164
  151.0 1.5 bitcast_convert_fusion
  152.5 3.8 %scatter_fusion = f32[9,64,128]{2,1,0:T(8,128)S(1)} fusion(f32[9,64,128]{2,1,0:T(8,128)S(1)} %broadcast_in_dim.30, s32[64]{0:T(128)S(1)} %fusion.56, f32[64,64,128]{2,1,0:T(8,128)S(1)} %bitcast_convert_fusion), kind=kCustom, calls=%fused_computation.15 | custom fusion | flops 524288 | bytes 6291712 | tf_op jit(solution)/shard_map/scatter-add | solution.py:175
  157.0 0.9 collective-permute-start.14
  158.4 0.8 collective-permute-start.12
  159.3 2.2 %fusion.70 = (bf16[4,1,256,256]{3,2,1,0:T(8,128)(2,1)}, bf16[4,1,256,256]{3,2,1,0:T(8,128)(2,1)}) fusion(bf16[4,2,256,256]{3,2,1,0:T(8,128)(2,1)} %gather_fusion.7), kind=kLoop, calls=%fused_computation.159 | loop fusion | bytes 2097152 | tf_op jit(solution)/shard_map/slice | solution.py:188
  161.5 2.2 %collective-permute-done.13 = f32[2,64,128]{2,1,0:T(8,128)S(1)} collective-permute-done((f32[2,64,128]{2,1,0:T(8,128)S(1)}, f32[2,64,128]{2,1,0:T(8,128)S(1)}, u32[]{:S(2)}, u32[]{:S(2)}) %collective-permute-start.13) | collective-permute-done | bytes 65568 | tf_op jit(solution)/shard_map/ppermute | solution.py:41
  165.1 1.0 fusion.37
  (97 shorter events, 14.4 us)
Async XLA Ops:
  0.6 40.5 %copy-start.7 = (s32[8,8]{1,0:T(8,128)S(1)}, s32[8,8]{1,0:T(8,128)}, u32[]{:S(2)}) copy-start(s32[8,8]{1,0:T(8,128)} %param.9) | copy-start | bytes 772
  0.6 41.7 %copy-start.2 = (bf16[1024,128]{1,0:T(8,128)(2,1)S(1)}, bf16[1024,128]{1,0:T(8,128)(2,1)}, u32[]{:S(2)}) copy-start(bf16[1024,128]{1,0:T(8,128)(2,1)} %param.6) | copy-start | bytes 786436
  0.7 41.7 %copy-start.3 = (bf16[1024,128]{1,0:T(8,128)(2,1)S(1)}, bf16[1024,128]{1,0:T(8,128)(2,1)}, u32[]{:S(2)}) copy-start(bf16[1024,128]{1,0:T(8,128)(2,1)} %param.7) | copy-start | bytes 786436
  4.7 20.7 %all-to-all-start = ((s32[64,1,1]{2,1,0:T(1,128)}), s32[64,1,1]{2,1,0:T(1,128)S(1)}, u32[]{:S(2)}, u32[]{:S(2)}) async-start(s32[64,1,1]{2,1,0:T(1,128)} %copy.79), calls=%async_computation | async-start | bytes 65536 | tf_op jit(solution)/shard_map/all_to_all | solution.py:65
  19.3 46.5 %copy-start.8 = (s32[1024]{0:T(1024)}, s32[1024]{0:T(1024)S(1)}, u32[]{:S(2)}) copy-start(s32[1024]{0:T(1024)S(1)} %pad_clamp_fusion.2) | copy-start | bytes 12292
  29.8 34.4 %all-to-all-start.1 = ((bf16[64,1,64,128]{3,2,1,0:T(8,128)(2,1)}), bf16[64,1,64,128]{3,2,1,0:T(8,128)(2,1)S(1)}, u32[]{:S(2)}, u32[]{:S(2)}) async-start(bf16[64,1,64,128]{3,2,1,0:T(8,128)(2,1)} %bitcast.8), calls=%async_computation.1 | async-start | bytes 2097152 | tf_op jit(solution)/shard_map/all_to_all | solution.py:85
  36.2 14.6 %collective-permute-start.5 = (bf16[2,256,256]{2,1,0:T(8,128)(2,1)}, bf16[2,256,256]{2,1,0:T(8,128)(2,1)S(1)}, u32[]{:S(2)}, u32[]{:S(2)}) collective-permute-start(bf16[2,256,256]{2,1,0:T(8,128)(2,1)} %get-tuple-element.21), channel_id=1, source_target_pairs={{0,3},{1,0},{2,1},{3,2},{4,7},{5,4},{6,5},{7,6},{8,11},{9,8},{10,9... | collective-permute-start | bytes 786440 | tf_op jit(solution)/shard_map/ppermute | solution.py:41
  39.0 11.8 %collective-permute-start.4 = (bf16[2,256,256]{2,1,0:T(8,128)(2,1)}, bf16[2,256,256]{2,1,0:T(8,128)(2,1)S(1)}, u32[]{:S(2)}, u32[]{:S(2)}) collective-permute-start(bf16[2,256,256]{2,1,0:T(8,128)(2,1)} %get-tuple-element.19), channel_id=1, source_target_pairs={{0,2},{1,3},{2,0},{3,1},{4,6},{5,7},{6,4},{7,5},{8,10},{9,11},{10,... | collective-permute-start | bytes 786440 | tf_op jit(solution)/shard_map/ppermute | solution.py:41
  39.8 14.6 %collective-permute-start.3 = (bf16[2,256,256]{2,1,0:T(8,128)(2,1)S(1)}, bf16[2,256,256]{2,1,0:T(8,128)(2,1)S(1)}, u32[]{:S(2)}, u32[]{:S(2)}) collective-permute-start(bf16[2,256,256]{2,1,0:T(8,128)(2,1)S(1)} %get-tuple-element.20), channel_id=1, source_target_pairs={{0,1},{1,2},{2,3},{3,0},{4,5},{5,6},{6,7},{7,4},{8,9},{9,10},{10,1... | collective-permute-start | bytes 786440 | tf_op jit(solution)/shard_map/ppermute | solution.py:41
  66.7 11.9 %collective-permute-start.2 = (bf16[14,64,128]{2,1,0:T(8,128)(2,1)}, bf16[14,64,128]{2,1,0:T(8,128)(2,1)}, u32[]{:S(2)}, u32[]{:S(2)}) collective-permute-start(bf16[14,64,128]{2,1,0:T(8,128)(2,1)} %get-tuple-element.29), channel_id=1, source_target_pairs={{0,3},{1,0},{2,1},{3,2},{4,7},{5,4},{6,5},{7,6},{8,11},{9,8},{10,9... | collective-permute-start | bytes 688136 | tf_op jit(solution)/shard_map/ppermute | solution.py:41
  69.4 10.3 %collective-permute-start.1 = (bf16[14,64,128]{2,1,0:T(8,128)(2,1)}, bf16[14,64,128]{2,1,0:T(8,128)(2,1)}, u32[]{:S(2)}, u32[]{:S(2)}) collective-permute-start(bf16[14,64,128]{2,1,0:T(8,128)(2,1)} %get-tuple-element.27), channel_id=1, source_target_pairs={{0,2},{1,3},{2,0},{3,1},{4,6},{5,7},{6,4},{7,5},{8,10},{9,11},{10,... | collective-permute-start | bytes 688136 | tf_op jit(solution)/shard_map/ppermute | solution.py:41
  70.2 12.0 %collective-permute-start = (bf16[14,64,128]{2,1,0:T(8,128)(2,1)}, bf16[14,64,128]{2,1,0:T(8,128)(2,1)}, u32[]{:S(2)}, u32[]{:S(2)}) collective-permute-start(bf16[14,64,128]{2,1,0:T(8,128)(2,1)} %get-tuple-element.28), channel_id=1, source_target_pairs={{0,1},{1,2},{2,3},{3,0},{4,5},{5,6},{6,7},{7,4},{8,9},{9,10},{10,1... | collective-permute-start | bytes 688136 | tf_op jit(solution)/shard_map/ppermute | solution.py:41
  84.5 8.1 %copy-start.4 = (bf16[14,4,64,128]{3,2,1,0:T(8,128)(2,1)}, bf16[14,4,64,128]{3,2,1,0:T(8,128)(2,1)S(1)}, u32[]{:S(2)}) copy-start(bf16[14,4,64,128]{3,2,1,0:T(8,128)(2,1)S(1)} %copy.80) | copy-start | bytes 2752516
  84.5 3.2 %copy-start.6 = (bf16[2,128,8,128]{1,3,2,0:T(8,128)(2,1)S(1)}, bf16[2,128,8,128]{1,3,2,0:T(8,128)(2,1)}, u32[]{:S(2)}) copy-start(bf16[2,128,8,128]{1,3,2,0:T(8,128)(2,1)} %copy.89) | copy-start | bytes 1572868
  92.6 4.1 %copy-start = (f32[2,8,1,128,128]{4,3,1,0,2:T(8,128)}, f32[2,8,1,128,128]{4,3,1,0,2:T(8,128)S(1)}, u32[]{:S(2)}) copy-start(f32[2,8,1,128,128]{4,3,1,0,2:T(8,128)S(1)} %fusion.16) | copy-start | bytes 3145732
  95.5 2.0 %copy-start.1 = (bf16[2,8,128,8,128]{2,4,1,3,0:T(8,128)(2,1)}, bf16[2,8,128,8,128]{2,4,1,3,0:T(8,128)(2,1)S(1)}, u32[]{:S(2)}) copy-start(bf16[2,8,128,8,128]{2,4,1,3,0:T(8,128)(2,1)S(1)} %fusion.1) | copy-start | bytes 12582916
  95.5 5.2 %copy-start.10 = (s32[65]{0:T(128)S(1)}, s32[65]{0:T(128)}, u32[]{:S(2)}) copy-start(s32[65]{0:T(128)} %scatter_custom_fusion.1) | copy-start | bytes 784
  98.4 8.6 %collective-permute-start.11 = (bf16[14,64,128]{2,1,0:T(8,128)(2,1)S(1)}, bf16[14,64,128]{2,1,0:T(8,128)(2,1)S(1)}, u32[]{:S(2)}, u32[]{:S(2)}) collective-permute-start(bf16[14,64,128]{2,1,0:T(8,128)(2,1)S(1)} %get-tuple-element.25), channel_id=1, source_target_pairs={{0,3},{1,0},{2,1},{3,2},{4,7},{5,4},{6,5},{7,6},{8,11},{9,8},{10,9... | collective-permute-start | bytes 688136 | tf_op jit(solution)/shard_map/ppermute | solution.py:41
  99.1 10.0 %collective-permute-start.10 = (bf16[14,64,128]{2,1,0:T(8,128)(2,1)S(1)}, bf16[14,64,128]{2,1,0:T(8,128)(2,1)S(1)}, u32[]{:S(2)}, u32[]{:S(2)}) collective-permute-start(bf16[14,64,128]{2,1,0:T(8,128)(2,1)S(1)} %get-tuple-element.23), channel_id=1, source_target_pairs={{0,2},{1,3},{2,0},{3,1},{4,6},{5,7},{6,4},{7,5},{8,10},{9,11},{10,... | collective-permute-start | bytes 688136 | tf_op jit(solution)/shard_map/ppermute | solution.py:41
  99.9 12.8 %collective-permute-start.9 = (bf16[14,64,128]{2,1,0:T(8,128)(2,1)S(1)}, bf16[14,64,128]{2,1,0:T(8,128)(2,1)S(1)}, u32[]{:S(2)}, u32[]{:S(2)}) collective-permute-start(bf16[14,64,128]{2,1,0:T(8,128)(2,1)S(1)} %get-tuple-element.24), channel_id=1, source_target_pairs={{0,1},{1,2},{2,3},{3,0},{4,5},{5,6},{6,7},{7,4},{8,9},{9,10},{10,1... | collective-permute-start | bytes 688136 | tf_op jit(solution)/shard_map/ppermute | solution.py:41
  112.8 14.2 %copy-start.5 = (bf16[2,128,8,128]{1,3,2,0:T(8,128)(2,1)S(1)}, bf16[2,128,8,128]{1,3,2,0:T(8,128)(2,1)}, u32[]{:S(2)}) copy-start(bf16[2,128,8,128]{1,3,2,0:T(8,128)(2,1)} %get-tuple-element.42) | copy-start | bytes 1572868
  115.6 35.3 %all-to-all-start.2 = ((bf16[64,1,64,128]{3,2,1,0:T(8,128)(2,1)}), bf16[64,1,64,128]{3,2,1,0:T(8,128)(2,1)}, u32[]{:S(2)}, u32[]{:S(2)}) async-start(bf16[64,1,64,128]{3,2,1,0:T(8,128)(2,1)} %bitcast.78), calls=%async_computation.2 | async-start | bytes 2097152 | tf_op jit(solution)/shard_map/all_to_all | solution.py:164
  125.4 6.5 %copy-start.9 = (s32[64]{0:T(128)S(1)}, s32[64]{0:T(128)}, u32[]{:S(2)}) copy-start(s32[64]{0:T(128)} %get-tuple-element.4) | copy-start | bytes 772
  129.6 9.3 %collective-permute-start.8 = (bf16[2,256,256]{2,1,0:T(8,128)(2,1)S(1)}, bf16[2,256,256]{2,1,0:T(8,128)(2,1)S(1)}, u32[]{:S(2)}, u32[]{:S(2)}) collective-permute-start(bf16[2,256,256]{2,1,0:T(8,128)(2,1)S(1)} %get-tuple-element.15), channel_id=1, source_target_pairs={{0,3},{1,0},{2,1},{3,2},{4,7},{5,4},{6,5},{7,6},{8,11},{9,8},{10,9... | collective-permute-start | bytes 786440 | tf_op jit(solution)/shard_map/ppermute | solution.py:41
  130.6 10.7 %collective-permute-start.7 = (bf16[2,256,256]{2,1,0:T(8,128)(2,1)S(1)}, bf16[2,256,256]{2,1,0:T(8,128)(2,1)S(1)}, u32[]{:S(2)}, u32[]{:S(2)}) collective-permute-start(bf16[2,256,256]{2,1,0:T(8,128)(2,1)S(1)} %get-tuple-element.13), channel_id=1, source_target_pairs={{0,2},{1,3},{2,0},{3,1},{4,6},{5,7},{6,4},{7,5},{8,10},{9,11},{10,... | collective-permute-start | bytes 786440 | tf_op jit(solution)/shard_map/ppermute | solution.py:41
  131.1 14.6 %collective-permute-start.6 = (bf16[2,256,256]{2,1,0:T(8,128)(2,1)S(1)}, bf16[2,256,256]{2,1,0:T(8,128)(2,1)S(1)}, u32[]{:S(2)}, u32[]{:S(2)}) collective-permute-start(bf16[2,256,256]{2,1,0:T(8,128)(2,1)S(1)} %get-tuple-element.14), channel_id=1, source_target_pairs={{0,1},{1,2},{2,3},{3,0},{4,5},{5,6},{6,7},{7,4},{8,9},{9,10},{10,1... | collective-permute-start | bytes 786440 | tf_op jit(solution)/shard_map/ppermute | solution.py:41
  157.0 4.5 %collective-permute-start.14 = (f32[2,64,128]{2,1,0:T(8,128)S(1)}, f32[2,64,128]{2,1,0:T(8,128)S(1)}, u32[]{:S(2)}, u32[]{:S(2)}) collective-permute-start(f32[2,64,128]{2,1,0:T(8,128)S(1)} %get-tuple-element.33), channel_id=1, source_target_pairs={{0,3},{1,0},{2,1},{3,2},{4,7},{5,4},{6,5},{7,6},{8,11},{9,8},{10,9... | collective-permute-start | bytes 196616 | tf_op jit(solution)/shard_map/ppermute | solution.py:41
  157.9 5.8 %collective-permute-start.13 = (f32[2,64,128]{2,1,0:T(8,128)S(1)}, f32[2,64,128]{2,1,0:T(8,128)S(1)}, u32[]{:S(2)}, u32[]{:S(2)}) collective-permute-start(f32[2,64,128]{2,1,0:T(8,128)S(1)} %get-tuple-element.31), channel_id=1, source_target_pairs={{0,2},{1,3},{2,0},{3,1},{4,6},{5,7},{6,4},{7,5},{8,10},{9,11},{10,... | collective-permute-start | bytes 196616 | tf_op jit(solution)/shard_map/ppermute | solution.py:41
  158.4 5.9 %collective-permute-start.12 = (f32[2,64,128]{2,1,0:T(8,128)S(1)}, f32[2,64,128]{2,1,0:T(8,128)S(1)}, u32[]{:S(2)}, u32[]{:S(2)}) collective-permute-start(f32[2,64,128]{2,1,0:T(8,128)S(1)} %get-tuple-element.32), channel_id=1, source_target_pairs={{0,1},{1,2},{2,3},{3,0},{4,5},{5,6},{6,7},{7,4},{8,9},{9,10},{10,1... | collective-permute-start | bytes 196616 | tf_op jit(solution)/shard_map/ppermute | solution.py:41
where the time goes:
time: 167 us
  waiting for transfers between devices  63.7 us (38%)
  starting transfers between devices  40 us (24%)
  local copies, waits for them, and re-layouts  26.9 us (16%)
  other arithmetic  21.4 us (13%)
  matrix products  13.5 us (8%)
    ppermute x15, waiting for transfers between devices, head_exchange(): lax.ppermute(ahead[k], 'head', [(j, (j + k) % count) for j in range(count)])  46.8 us
    ppermute x15, starting transfers between devices, head_exchange(): lax.ppermute(ahead[k], 'head', [(j, (j + k) % count) for j in range(count)])  15.7 us
    all_to_all x1, starting transfers between devices, on_device(): lax.all_to_all(req_table.reshape(pair_count, capacity), 'ctx', split_axis...  12.1 us
    all_to_all x1, waiting for transfers between devices, on_device(): lax.all_to_all(send_parts, 'ctx', split_axis=0, concat_axis=0, tiled=True)  8 us
    all_to_all x1, starting transfers between devices, on_device(): lax.all_to_all(outgoing_part.reshape(pair_count, capacity, part_rows, HD)...  6.64 us
    all_to_all x1, starting transfers between devices, on_device(): lax.all_to_all(send_parts, 'ctx', split_axis=0, concat_axis=0, tiled=True)  5.55 us
    all_to_all x1, waiting for transfers between devices, on_device(): lax.all_to_all(req_table.reshape(pair_count, capacity), 'ctx', split_axis...  5.47 us
    gather x5, local copies, waits for them, and re-layouts, head_exchange(): return jnp.stack(got)[order]  4.97 us
  transfers between devices with their start and end apart: 18, of which 16 were waited for; matrix products, arithmetic and copies ran while one was open for 14% of the time, Pallas kernels for 0%

commit v1 on v0

--- a/solution.py
+++ b/solution.py
@@ -62,9 +62,13 @@
     req_table = (
         jnp.full((total_slots + 1,), -1, jnp.int32).at[slot_idx].set(local_blk)[:total_slots]
     )
-    requested = lax.all_to_all(
-        req_table.reshape(pair_count, capacity), "ctx", split_axis=0, concat_axis=0, tiled=True
-    )
+    all_lists = lax.all_gather(block_lists, "ctx", axis=0, tiled=True)
+    all_extras = all_lists[:, 1:].reshape(pair_count, entry_count)
+    all_owner, all_local = block_home(jnp.maximum(all_extras, 0), half_blocks, pair_count)
+    asks_me = (all_extras >= 0) & (all_owner == device)
+    ask_rank = jnp.cumsum(asks_me.astype(jnp.int32), axis=1) - 1
+    hit = asks_me[:, :, None] & (ask_rank[:, :, None] == jnp.arange(capacity, dtype=jnp.int32)[None, None, :])
+    requested = jnp.sum(jnp.where(hit, all_local[:, :, None] + 1, 0), axis=1) - 1
     rows_in, cols_in = queries.shape
     inputs_split = jnp.stack(
         [

time: 167 us -> 196 us (1.17)
  blocking collectives: 0 us -> 47 us
  starting transfers between devices: 40 us -> 29.8 us
  waiting for transfers between devices: 63.7 us -> 58.5 us
  other arithmetic: 21.4 us -> 19.4 us
    all_gather x0 -> x1, blocking collectives: none -> 47 us  [on_device(): all_lists = lax.all_gather(block_lists, 'ctx', axis=0, tiled=True)]
    all_to_all x1 -> x0, starting transfers between devices: 12.1 us -> none  [on_device(): lax.all_to_all(req_table.reshape(pair_count, capacity), 'ctx', split_axis...]
    all_to_all x1 -> x0, waiting for transfers between devices: 5.47 us -> none  [on_device(): lax.all_to_all(req_table.reshape(pair_count, capacity), 'ctx', split_axis...]
    all_to_all x1 -> x0, other arithmetic: 2.72 us -> none  [on_device(): lax.all_to_all(req_table.reshape(pair_count, capacity), 'ctx', split_axis...]
  transfers between devices with their start and end apart: 18 -> 17, of which waited for: 16 -> 15; matrix products, arithmetic and copies ran while one was open for 14% -> 10% of each run, Pallas kernels for 0% -> 0%
where the time goes in v1:
time: 196 us; the launch traced here: 195 us
  waiting for transfers between devices  58.5 us (30%)
  blocking collectives  47 us (24%)
  starting transfers between devices  29.8 us (15%)
  local copies, waits for them, and re-layouts  25.3 us (13%)
  other arithmetic  19.4 us (10%)
  matrix products  13.5 us (7%)
    ppermute x15, waiting for transfers between devices, head_exchange(): lax.ppermute(ahead[k], 'head', [(j, (j + k) % count) for j in range(count)])  47.6 us
    all_gather x1, blocking collectives, on_device(): all_lists = lax.all_gather(block_lists, 'ctx', axis=0, tiled=True)  47 us
    ppermute x15, starting transfers between devices, head_exchange(): lax.ppermute(ahead[k], 'head', [(j, (j + k) % count) for j in range(count)])  15.8 us
    all_to_all x1, waiting for transfers between devices, on_device(): lax.all_to_all(send_parts, 'ctx', split_axis=0, concat_axis=0, tiled=True)  7.56 us
    all_to_all x1, starting transfers between devices, on_device(): lax.all_to_all(send_parts, 'ctx', split_axis=0, concat_axis=0, tiled=True)  7.34 us
    all_to_all x1, starting transfers between devices, on_device(): lax.all_to_all(outgoing_part.reshape(pair_count, capacity, part_rows, HD)...  6.7 us
    gather x5, local copies, waits for them, and re-layouts, head_exchange(): return jnp.stack(got)[order]  4.72 us
  transfers between devices with their start and end apart: 17, of which 15 were waited for; matrix products, arithmetic and copies ran while one was open for 10% of the time, Pallas kernels for 0%

profile of v1, /device:TPU:8, one launch (start us, length us, event | category | flops | bytes accessed | tf_op | source)
XLA Modules:
  0.0 194.9 jit_solution(6086102832559587527)
XLA Ops:
  0.7 0.9 fusion.55
  1.5 0.8 maximum_shift-right-logical_fusion
  2.8 47.0 %all_gather.3 = s32[512,8]{1,0:T(8,128)S(1)} all-gather(s32[8,8]{1,0:T(8,128)} %param.9), channel_id=1, replica_groups=mesh['ctx'=64,'head'=4] {'ctx'}, dimensions={0}, use_global_device_ids=true | all-gather | bytes 16640 | tf_op jit(solution)/shard_map/all_gather | solution.py:65
  52.1 0.7 scatter_custom_fusion
  53.4 1.1 pad_maximum_fusion.6
  54.5 1.7 gather_fusion
  56.2 7.3 %all-to-all-start = ((bf16[64,1,64,128]{3,2,1,0:T(8,128)(2,1)}), bf16[64,1,64,128]{3,2,1,0:T(8,128)(2,1)S(1)}, u32[]{:S(2)}, u32[]{:S(2)}) async-start(bf16[64,1,64,128]{3,2,1,0:T(8,128)(2,1)} %bitcast.5), calls=%async_computation | async-start | bytes 2097152 | tf_op jit(solution)/shard_map/all_to_all | solution.py:89
  64.3 0.8 fusion.80
  65.1 2.8 %collective-permute-start.5 = (bf16[2,256,256]{2,1,0:T(8,128)(2,1)S(1)}, bf16[2,256,256]{2,1,0:T(8,128)(2,1)S(1)}, u32[]{:S(2)}, u32[]{:S(2)}) collective-permute-start(bf16[2,256,256]{2,1,0:T(8,128)(2,1)S(1)} %get-tuple-element.15), channel_id=1, source_target_pairs={{0,3},{1,0},{2,1},{3,2},{4,7},{5,4},{6,5},{7,6},{8,11},{9,8},{10,9... | collective-permute-start | bytes 786440 | tf_op jit(solution)/shard_map/ppermute | solution.py:41
  67.8 0.8 collective-permute-start.4
  68.6 0.9 collective-permute-start.3
  70.6 0.8 copy_bitcast_fusion
  72.1 7.2 %collective-permute-done.5 = bf16[2,256,256]{2,1,0:T(8,128)(2,1)S(1)} collective-permute-done((bf16[2,256,256]{2,1,0:T(8,128)(2,1)S(1)}, bf16[2,256,256]{2,1,0:T(8,128)(2,1)S(1)}, u32[]{:S(2)}, u32[]{:S(2)}) %collective-permute-start.5) | collective-permute-done | bytes 262176 | tf_op jit(solution)/shard_map/ppermute | solution.py:41
  79.3 3.7 %collective-permute-done.3 = bf16[2,256,256]{2,1,0:T(8,128)(2,1)S(1)} collective-permute-done((bf16[2,256,256]{2,1,0:T(8,128)(2,1)S(1)}, bf16[2,256,256]{2,1,0:T(8,128)(2,1)S(1)}, u32[]{:S(2)}, u32[]{:S(2)}) %collective-permute-start.3) | collective-permute-done | bytes 262176 | tf_op jit(solution)/shard_map/ppermute | solution.py:41
  83.0 1.1 pad_maximum_fusion.2
  84.7 7.6 %all-to-all-done = bf16[64,1,64,128]{3,2,1,0:T(8,128)(2,1)S(1)} async-done(((bf16[64,1,64,128]{3,2,1,0:T(8,128)(2,1)}), bf16[64,1,64,128]{3,2,1,0:T(8,128)(2,1)S(1)}, u32[]{:S(2)}, u32[]{:S(2)}) %all-to-all-start) | async-done | bytes 1048608 | tf_op jit(solution)/shard_map/all_to_all | solution.py:89
  92.3 0.8 gather_fusion.1
  93.1 0.8 gather_fusion.2
  94.0 0.9 fusion.82
  94.8 2.8 %collective-permute-start.2 = (bf16[14,64,128]{2,1,0:T(8,128)(2,1)}, bf16[14,64,128]{2,1,0:T(8,128)(2,1)}, u32[]{:S(2)}, u32[]{:S(2)}) collective-permute-start(bf16[14,64,128]{2,1,0:T(8,128)(2,1)} %get-tuple-element.23), channel_id=1, source_target_pairs={{0,3},{1,0},{2,1},{3,2},{4,7},{5,4},{6,5},{7,6},{8,11},{9,8},{10,9... | collective-permute-start | bytes 688136 | tf_op jit(solution)/shard_map/ppermute | solution.py:41
  97.6 0.8 collective-permute-start.1
  98.4 0.9 collective-permute-start
  100.6 1.1 copy.66
  101.7 5.0 %collective-permute-done.2 = bf16[14,64,128]{2,1,0:T(8,128)(2,1)} collective-permute-done((bf16[14,64,128]{2,1,0:T(8,128)(2,1)}, bf16[14,64,128]{2,1,0:T(8,128)(2,1)}, u32[]{:S(2)}, u32[]{:S(2)}) %collective-permute-start.2) | collective-permute-done | bytes 229408 | tf_op jit(solution)/shard_map/ppermute | solution.py:41
  106.8 1.1 collective-permute-done.1
  107.9 2.5 %collective-permute-done = bf16[14,64,128]{2,1,0:T(8,128)(2,1)} collective-permute-done((bf16[14,64,128]{2,1,0:T(8,128)(2,1)}, bf16[14,64,128]{2,1,0:T(8,128)(2,1)}, u32[]{:S(2)}, u32[]{:S(2)}) %collective-permute-start) | collective-permute-done | bytes 229408 | tf_op jit(solution)/shard_map/ppermute | solution.py:41
  110.4 1.3 pad_maximum_fusion.4
  111.7 0.7 gather_fusion.3
  112.6 1.3 fusion.5
  113.9 1.8 fusion.2
  115.7 3.0 %multiply_reduce_fusion = (f32[2,128,8]{1,2,0:T(8,128)S(1)}, bf16[2,128,8,128]{1,3,2,0:T(8,128)(2,1)}) fusion(bf16[2,128,8,128]{1,3,2,0:T(8,128)(2,1)S(1)} %copy-done.5, f32[2,128,8]{1,2,0:T(8,128)S(1)} %bitcast.248, f32[2,8,128,128,8]{3,2,4,1,0:T(8,128)S(1)} %get-tuple-element.35, f32[2,8,128]{2,1,0:T(8,128)S(1)} %get-tuple-element.34, ...), kind=kOutput, calls=%fused_computation.49 | convolution fusion | flops 547878912 | bytes 10772480 | tf_op jit(solution)/shard_map/qhisj,qsjd->qihd/dot_general | solution.py:124
  118.7 2.0 %fusion.16 = f32[2,8,1,128,128]{4,3,1,0,2:T(8,128)S(1)} fusion(f32[2,8,128,128,8]{3,2,4,1,0:T(8,128)S(1)} %get-tuple-element.35, f32[2,8,128]{2,1,0:T(8,128)S(1)} %log_add_fusion, pred[2,128,8,128]{1,3,2,0:T(8,128)(4,1)S(1)} %compare_and_fusion, bf16[2,128,8,128,1]{3,2,1,0,4:T(8,128)(2,1)S(1)} %bitcast.214), kind=kOutput, calls=%fused_computation.34 | convolution fusion | flops 545259520 | bytes 10231808 | tf_op jit(solution)/shard_map/qhisj,qihd->qsjd/dot_general | solution.py:150
  120.7 2.8 %fusion.1 = bf16[2,8,128,8,128]{2,4,1,3,0:T(8,128)(2,1)S(1)} fusion(f32[2,8,128,128,8]{3,2,4,1,0:T(8,128)S(1)} %get-tuple-element.35, f32[2,8,128]{2,1,0:T(8,128)S(1)} %bitcast.249, f32[2,8,128]{2,1,0:T(8,128)S(1)} %log_add_fusion, pred[2,128,8,128]{1,3,2,0:T(8,128)(4,1)S(1)} %compare_and_fusion, bf16[2,128,8,128,1]{3,2,1,0,4:T(8,128)(2,1)S(1)} %bitcast.215, ...), kind=kOutput, calls=%fused_computation.17 | convolution fusion | flops 550502400 | bytes 14434304 | tf_op jit(solution)/shard_map/qihd,qsjd->qhisj/dot_general | solution.py:136
  123.5 1.3 fusion.21
  125.6 0.8 gather_fusion.8
  126.5 0.7 collective-permute-start.11
  127.2 0.8 collective-permute-start.10
  127.9 0.9 collective-permute-start.9
  129.4 5.7 %collective-permute-done.11 = bf16[14,64,128]{2,1,0:T(8,128)(2,1)S(1)} collective-permute-done((bf16[14,64,128]{2,1,0:T(8,128)(2,1)S(1)}, bf16[14,64,128]{2,1,0:T(8,128)(2,1)S(1)}, u32[]{:S(2)}, u32[]{:S(2)}) %collective-permute-start.11) | collective-permute-done | bytes 229408 | tf_op jit(solution)/shard_map/ppermute | solution.py:41
  135.0 2.2 %collective-permute-done.10 = bf16[14,64,128]{2,1,0:T(8,128)(2,1)S(1)} collective-permute-done((bf16[14,64,128]{2,1,0:T(8,128)(2,1)S(1)}, bf16[14,64,128]{2,1,0:T(8,128)(2,1)S(1)}, u32[]{:S(2)}, u32[]{:S(2)}) %collective-permute-start.10) | collective-permute-done | bytes 229408 | tf_op jit(solution)/shard_map/ppermute | solution.py:41
  137.2 3.6 %collective-permute-done.9 = bf16[14,64,128]{2,1,0:T(8,128)(2,1)S(1)} collective-permute-done((bf16[14,64,128]{2,1,0:T(8,128)(2,1)S(1)}, bf16[14,64,128]{2,1,0:T(8,128)(2,1)S(1)}, u32[]{:S(2)}, u32[]{:S(2)}) %collective-permute-start.9) | collective-permute-done | bytes 229408 | tf_op jit(solution)/shard_map/ppermute | solution.py:41
  140.9 1.0 gather_fusion.9
  141.9 1.8 gather_fusion.10
  143.7 6.7 %all-to-all-start.1 = ((bf16[64,1,64,128]{3,2,1,0:T(8,128)(2,1)}), bf16[64,1,64,128]{3,2,1,0:T(8,128)(2,1)}, u32[]{:S(2)}, u32[]{:S(2)}) async-start(bf16[64,1,64,128]{3,2,1,0:T(8,128)(2,1)} %bitcast.78), calls=%async_computation.1 | async-start | bytes 2097152 | tf_op jit(solution)/shard_map/all_to_all | solution.py:168
  150.4 3.1 %fusion.23 = bf16[2,128,8,128]{1,3,2,0:T(8,128)(2,1)S(1)} fusion(bf16[2,8,128,8,128]{2,4,1,3,0:T(8,128)(2,1)} %copy-done.1, bf16[2,1,2,128,128]{4,3,1,0,2:T(8,128)(2,1)S(1)} %copy_bitcast_fusion, bf16[2,7,2,128,128]{4,3,2,1,0:T(8,128)(2,1)} %bitcast.228), kind=kOutput, calls=%fused_computation.41 | convolution fusion | flops 538443776 | bytes 5767168 | tf_op jit(solution)/shard_map/qhisj,qsjd->qihd/dot_general | solution.py:143
  154.2 0.9 copy.71
  155.8 1.1 maximum_bitcast_fusion
  157.0 0.7 gather_fusion.6
  157.8 0.9 collective-permute-start.8
  159.3 0.8 collective-permute-start.6
  160.1 6.9 %collective-permute-done.8 = bf16[2,256,256]{2,1,0:T(8,128)(2,1)S(1)} collective-permute-done((bf16[2,256,256]{2,1,0:T(8,128)(2,1)S(1)}, bf16[2,256,256]{2,1,0:T(8,128)(2,1)S(1)}, u32[]{:S(2)}, u32[]{:S(2)}) %collective-permute-start.8) | collective-permute-done | bytes 262176 | tf_op jit(solution)/shard_map/ppermute | solution.py:41
  167.1 2.4 %collective-permute-done.7 = bf16[2,256,256]{2,1,0:T(8,128)(2,1)S(1)} collective-permute-done((bf16[2,256,256]{2,1,0:T(8,128)(2,1)S(1)}, bf16[2,256,256]{2,1,0:T(8,128)(2,1)S(1)}, u32[]{:S(2)}, u32[]{:S(2)}) %collective-permute-start.7) | collective-permute-done | bytes 262176 | tf_op jit(solution)/shard_map/ppermute | solution.py:41
  169.4 4.4 %collective-permute-done.6 = bf16[2,256,256]{2,1,0:T(8,128)(2,1)S(1)} collective-permute-done((bf16[2,256,256]{2,1,0:T(8,128)(2,1)S(1)}, bf16[2,256,256]{2,1,0:T(8,128)(2,1)S(1)}, u32[]{:S(2)}, u32[]{:S(2)}) %collective-permute-start.6) | collective-permute-done | bytes 262176 | tf_op jit(solution)/shard_map/ppermute | solution.py:41
  174.0 1.7 gather_fusion.7
  175.7 3.4 %all-to-all-done.1 = bf16[64,1,64,128]{3,2,1,0:T(8,128)(2,1)} async-done(((bf16[64,1,64,128]{3,2,1,0:T(8,128)(2,1)}), bf16[64,1,64,128]{3,2,1,0:T(8,128)(2,1)}, u32[]{:S(2)}, u32[]{:S(2)}) %all-to-all-start.1) | async-done | bytes 1048608 | tf_op jit(solution)/shard_map/all_to_all | solution.py:168
  179.1 1.5 bitcast_convert_fusion
  180.6 3.8 %scatter_fusion = f32[9,64,128]{2,1,0:T(8,128)S(1)} fusion(f32[9,64,128]{2,1,0:T(8,128)S(1)} %broadcast_in_dim.29, s32[64]{0:T(128)S(1)} %fusion.65, f32[64,64,128]{2,1,0:T(8,128)S(1)} %bitcast_convert_fusion), kind=kCustom, calls=%fused_computation.14 | custom fusion | flops 524288 | bytes 6291712 | tf_op jit(solution)/shard_map/scatter-add | solution.py:179
  184.4 0.7 gather_fusion.11
  185.1 0.9 collective-permute-start.14
  186.6 0.8 collective-permute-start.12
  187.4 2.2 %fusion.77 = (bf16[4,1,256,256]{3,2,1,0:T(8,128)(2,1)}, bf16[4,1,256,256]{3,2,1,0:T(8,128)(2,1)}) fusion(bf16[4,2,256,256]{3,2,1,0:T(8,128)(2,1)} %gather_fusion.7), kind=kLoop, calls=%fused_computation.173 | loop fusion | bytes 2097152 | tf_op jit(solution)/shard_map/slice | solution.py:192
  189.7 2.2 %collective-permute-done.13 = f32[2,64,128]{2,1,0:T(8,128)S(1)} collective-permute-done((f32[2,64,128]{2,1,0:T(8,128)S(1)}, f32[2,64,128]{2,1,0:T(8,128)S(1)}, u32[]{:S(2)}, u32[]{:S(2)}) %collective-permute-start.13) | collective-permute-done | bytes 65568 | tf_op jit(solution)/shard_map/ppermute | solution.py:41
  192.6 0.7 gather_fusion.12
  193.3 1.0 fusion.42
  (108 shorter events, 13.3 us)
Async XLA Ops:
  0.6 69.4 %copy-start.8 = (s32[8,8]{1,0:T(8,128)S(1)}, s32[8,8]{1,0:T(8,128)}, u32[]{:S(2)}) copy-start(s32[8,8]{1,0:T(8,128)} %param.9) | copy-start | bytes 772
  0.6 70.0 %copy-start.2 = (bf16[1024,128]{1,0:T(8,128)(2,1)S(1)}, bf16[1024,128]{1,0:T(8,128)(2,1)}, u32[]{:S(2)}) copy-start(bf16[1024,128]{1,0:T(8,128)(2,1)} %param.6) | copy-start | bytes 786436
  0.7 62.9 %copy-start.6 = (bf16[1024,256]{1,0:T(8,128)(2,1)S(1)}, bf16[1024,256]{1,0:T(8,128)(2,1)}, u32[]{:S(2)}) copy-start(bf16[1024,256]{1,0:T(8,128)(2,1)} %param.8) | copy-start | bytes 1572868
  0.7 62.9 %copy-start.7 = (bf16[1024,256]{1,0:T(8,128)(2,1)S(1)}, bf16[1024,256]{1,0:T(8,128)(2,1)}, u32[]{:S(2)}) copy-start(bf16[1024,256]{1,0:T(8,128)(2,1)} %param.5) | copy-start | bytes 1572868
  52.1 11.4 %copy-start.11 = (s32[64]{0:T(128)}, s32[64]{0:T(128)S(1)}, u32[]{:S(2)}) copy-start(s32[64]{0:T(128)S(1)} %reduce_sum.45) | copy-start | bytes 772
  56.2 36.1 %all-to-all-start = ((bf16[64,1,64,128]{3,2,1,0:T(8,128)(2,1)}), bf16[64,1,64,128]{3,2,1,0:T(8,128)(2,1)S(1)}, u32[]{:S(2)}, u32[]{:S(2)}) async-start(bf16[64,1,64,128]{3,2,1,0:T(8,128)(2,1)} %bitcast.5), calls=%async_computation | async-start | bytes 2097152 | tf_op jit(solution)/shard_map/all_to_all | solution.py:89
  63.5 8.0 %copy-start.9 = (s32[1024]{0:T(1024)}, s32[1024]{0:T(1024)S(1)}, u32[]{:S(2)}) copy-start(s32[1024]{0:T(1024)S(1)} %pad_clamp_fusion.2) | copy-start | bytes 12292
  65.1 14.3 %collective-permute-start.5 = (bf16[2,256,256]{2,1,0:T(8,128)(2,1)S(1)}, bf16[2,256,256]{2,1,0:T(8,128)(2,1)S(1)}, u32[]{:S(2)}, u32[]{:S(2)}) collective-permute-start(bf16[2,256,256]{2,1,0:T(8,128)(2,1)S(1)} %get-tuple-element.15), channel_id=1, source_target_pairs={{0,3},{1,0},{2,1},{3,2},{4,7},{5,4},{6,5},{7,6},{8,11},{9,8},{10,9... | collective-permute-start | bytes 786440 | tf_op jit(solution)/shard_map/ppermute | solution.py:41
  67.8 11.5 %collective-permute-start.4 = (bf16[2,256,256]{2,1,0:T(8,128)(2,1)S(1)}, bf16[2,256,256]{2,1,0:T(8,128)(2,1)S(1)}, u32[]{:S(2)}, u32[]{:S(2)}) collective-permute-start(bf16[2,256,256]{2,1,0:T(8,128)(2,1)S(1)} %get-tuple-element.13), channel_id=1, source_target_pairs={{0,2},{1,3},{2,0},{3,1},{4,6},{5,7},{6,4},{7,5},{8,10},{9,11},{10,... | collective-permute-start | bytes 786440 | tf_op jit(solution)/shard_map/ppermute | solution.py:41
  68.6 14.4 %collective-permute-start.3 = (bf16[2,256,256]{2,1,0:T(8,128)(2,1)S(1)}, bf16[2,256,256]{2,1,0:T(8,128)(2,1)S(1)}, u32[]{:S(2)}, u32[]{:S(2)}) collective-permute-start(bf16[2,256,256]{2,1,0:T(8,128)(2,1)S(1)} %get-tuple-element.14), channel_id=1, source_target_pairs={{0,1},{1,2},{2,3},{3,0},{4,5},{5,6},{6,7},{7,4},{8,9},{9,10},{10,1... | collective-permute-start | bytes 786440 | tf_op jit(solution)/shard_map/ppermute | solution.py:41
  70.0 41.7 %copy-start.10 = (s32[1024]{0:T(1024)}, s32[1024]{0:T(1024)S(1)}, u32[]{:S(2)}) copy-start(s32[1024]{0:T(1024)S(1)} %pad_clamp_fusion.1) | copy-start | bytes 12292
  94.8 11.9 %collective-permute-start.2 = (bf16[14,64,128]{2,1,0:T(8,128)(2,1)}, bf16[14,64,128]{2,1,0:T(8,128)(2,1)}, u32[]{:S(2)}, u32[]{:S(2)}) collective-permute-start(bf16[14,64,128]{2,1,0:T(8,128)(2,1)} %get-tuple-element.23), channel_id=1, source_target_pairs={{0,3},{1,0},{2,1},{3,2},{4,7},{5,4},{6,5},{7,6},{8,11},{9,8},{10,9... | collective-permute-start | bytes 688136 | tf_op jit(solution)/shard_map/ppermute | solution.py:41
  97.6 10.3 %collective-permute-start.1 = (bf16[14,64,128]{2,1,0:T(8,128)(2,1)}, bf16[14,64,128]{2,1,0:T(8,128)(2,1)}, u32[]{:S(2)}, u32[]{:S(2)}) collective-permute-start(bf16[14,64,128]{2,1,0:T(8,128)(2,1)} %get-tuple-element.21), channel_id=1, source_target_pairs={{0,2},{1,3},{2,0},{3,1},{4,6},{5,7},{6,4},{7,5},{8,10},{9,11},{10,... | collective-permute-start | bytes 688136 | tf_op jit(solution)/shard_map/ppermute | solution.py:41
  98.4 12.0 %collective-permute-start = (bf16[14,64,128]{2,1,0:T(8,128)(2,1)}, bf16[14,64,128]{2,1,0:T(8,128)(2,1)}, u32[]{:S(2)}, u32[]{:S(2)}) collective-permute-start(bf16[14,64,128]{2,1,0:T(8,128)(2,1)} %get-tuple-element.22), channel_id=1, source_target_pairs={{0,1},{1,2},{2,3},{3,0},{4,5},{5,6},{6,7},{7,4},{8,9},{9,10},{10,1... | collective-permute-start | bytes 688136 | tf_op jit(solution)/shard_map/ppermute | solution.py:41
  112.5 8.2 %copy-start.3 = (bf16[14,4,64,128]{3,2,1,0:T(8,128)(2,1)}, bf16[14,4,64,128]{3,2,1,0:T(8,128)(2,1)S(1)}, u32[]{:S(2)}) copy-start(bf16[14,4,64,128]{3,2,1,0:T(8,128)(2,1)S(1)} %copy.57) | copy-start | bytes 2752516
  112.5 3.2 %copy-start.5 = (bf16[2,128,8,128]{1,3,2,0:T(8,128)(2,1)S(1)}, bf16[2,128,8,128]{1,3,2,0:T(8,128)(2,1)}, u32[]{:S(2)}) copy-start(bf16[2,128,8,128]{1,3,2,0:T(8,128)(2,1)} %copy.66) | copy-start | bytes 1572868
  120.7 4.1 %copy-start = (f32[2,8,1,128,128]{4,3,1,0,2:T(8,128)}, f32[2,8,1,128,128]{4,3,1,0,2:T(8,128)S(1)}, u32[]{:S(2)}) copy-start(f32[2,8,1,128,128]{4,3,1,0,2:T(8,128)S(1)} %fusion.16) | copy-start | bytes 3145732
  123.5 2.0 %copy-start.1 = (bf16[2,8,128,8,128]{2,4,1,3,0:T(8,128)(2,1)}, bf16[2,8,128,8,128]{2,4,1,3,0:T(8,128)(2,1)S(1)}, u32[]{:S(2)}) copy-start(bf16[2,8,128,8,128]{2,4,1,3,0:T(8,128)(2,1)S(1)} %fusion.1) | copy-start | bytes 12582916
  123.5 5.2 %copy-start.13 = (s32[64]{0:T(128)S(1)}, s32[64]{0:T(128)}, u32[]{:S(2)}) copy-start(s32[64]{0:T(128)} %get-tuple-element.38) | copy-start | bytes 772
  126.5 8.6 %collective-permute-start.11 = (bf16[14,64,128]{2,1,0:T(8,128)(2,1)S(1)}, bf16[14,64,128]{2,1,0:T(8,128)(2,1)S(1)}, u32[]{:S(2)}, u32[]{:S(2)}) collective-permute-start(bf16[14,64,128]{2,1,0:T(8,128)(2,1)S(1)} %get-tuple-element.19), channel_id=1, source_target_pairs={{0,3},{1,0},{2,1},{3,2},{4,7},{5,4},{6,5},{7,6},{8,11},{9,8},{10,9... | collective-permute-start | bytes 688136 | tf_op jit(solution)/shard_map/ppermute | solution.py:41
  127.2 10.0 %collective-permute-start.10 = (bf16[14,64,128]{2,1,0:T(8,128)(2,1)S(1)}, bf16[14,64,128]{2,1,0:T(8,128)(2,1)S(1)}, u32[]{:S(2)}, u32[]{:S(2)}) collective-permute-start(bf16[14,64,128]{2,1,0:T(8,128)(2,1)S(1)} %get-tuple-element.17), channel_id=1, source_target_pairs={{0,2},{1,3},{2,0},{3,1},{4,6},{5,7},{6,4},{7,5},{8,10},{9,11},{10,... | collective-permute-start | bytes 688136 | tf_op jit(solution)/shard_map/ppermute | solution.py:41
  127.9 12.8 %collective-permute-start.9 = (bf16[14,64,128]{2,1,0:T(8,128)(2,1)S(1)}, bf16[14,64,128]{2,1,0:T(8,128)(2,1)S(1)}, u32[]{:S(2)}, u32[]{:S(2)}) collective-permute-start(bf16[14,64,128]{2,1,0:T(8,128)(2,1)S(1)} %get-tuple-element.18), channel_id=1, source_target_pairs={{0,1},{1,2},{2,3},{3,0},{4,5},{5,6},{6,7},{7,4},{8,9},{9,10},{10,1... | collective-permute-start | bytes 688136 | tf_op jit(solution)/shard_map/ppermute | solution.py:41
  140.9 14.2 %copy-start.4 = (bf16[2,128,8,128]{1,3,2,0:T(8,128)(2,1)S(1)}, bf16[2,128,8,128]{1,3,2,0:T(8,128)(2,1)}, u32[]{:S(2)}) copy-start(bf16[2,128,8,128]{1,3,2,0:T(8,128)(2,1)} %get-tuple-element.37) | copy-start | bytes 1572868
  143.7 35.4 %all-to-all-start.1 = ((bf16[64,1,64,128]{3,2,1,0:T(8,128)(2,1)}), bf16[64,1,64,128]{3,2,1,0:T(8,128)(2,1)}, u32[]{:S(2)}, u32[]{:S(2)}) async-start(bf16[64,1,64,128]{3,2,1,0:T(8,128)(2,1)} %bitcast.78), calls=%async_computation.1 | async-start | bytes 2097152 | tf_op jit(solution)/shard_map/all_to_all | solution.py:168
  153.6 6.5 %copy-start.12 = (s32[64]{0:T(128)S(1)}, s32[64]{0:T(128)}, u32[]{:S(2)}) copy-start(s32[64]{0:T(128)} %copy-done.11) | copy-start | bytes 772
  157.8 9.3 %collective-permute-start.8 = (bf16[2,256,256]{2,1,0:T(8,128)(2,1)S(1)}, bf16[2,256,256]{2,1,0:T(8,128)(2,1)S(1)}, u32[]{:S(2)}, u32[]{:S(2)}) collective-permute-start(bf16[2,256,256]{2,1,0:T(8,128)(2,1)S(1)} %get-tuple-element.9), channel_id=1, source_target_pairs={{0,3},{1,0},{2,1},{3,2},{4,7},{5,4},{6,5},{7,6},{8,11},{9,8},{10,9... | collective-permute-start | bytes 786440 | tf_op jit(solution)/shard_map/ppermute | solution.py:41
  158.7 10.7 %collective-permute-start.7 = (bf16[2,256,256]{2,1,0:T(8,128)(2,1)S(1)}, bf16[2,256,256]{2,1,0:T(8,128)(2,1)S(1)}, u32[]{:S(2)}, u32[]{:S(2)}) collective-permute-start(bf16[2,256,256]{2,1,0:T(8,128)(2,1)S(1)} %get-tuple-element.7), channel_id=1, source_target_pairs={{0,2},{1,3},{2,0},{3,1},{4,6},{5,7},{6,4},{7,5},{8,10},{9,11},{10,... | collective-permute-start | bytes 786440 | tf_op jit(solution)/shard_map/ppermute | solution.py:41
  159.3 14.6 %collective-permute-start.6 = (bf16[2,256,256]{2,1,0:T(8,128)(2,1)S(1)}, bf16[2,256,256]{2,1,0:T(8,128)(2,1)S(1)}, u32[]{:S(2)}, u32[]{:S(2)}) collective-permute-start(bf16[2,256,256]{2,1,0:T(8,128)(2,1)S(1)} %get-tuple-element.8), channel_id=1, source_target_pairs={{0,1},{1,2},{2,3},{3,0},{4,5},{5,6},{6,7},{7,4},{8,9},{9,10},{10,1... | collective-permute-start | bytes 786440 | tf_op jit(solution)/shard_map/ppermute | solution.py:41
  185.1 4.5 %collective-permute-start.14 = (f32[2,64,128]{2,1,0:T(8,128)S(1)}, f32[2,64,128]{2,1,0:T(8,128)S(1)}, u32[]{:S(2)}, u32[]{:S(2)}) collective-permute-start(f32[2,64,128]{2,1,0:T(8,128)S(1)} %get-tuple-element.27), channel_id=1, source_target_pairs={{0,3},{1,0},{2,1},{3,2},{4,7},{5,4},{6,5},{7,6},{8,11},{9,8},{10,9... | collective-permute-start | bytes 196616 | tf_op jit(solution)/shard_map/ppermute | solution.py:41
  186.1 5.8 %collective-permute-start.13 = (f32[2,64,128]{2,1,0:T(8,128)S(1)}, f32[2,64,128]{2,1,0:T(8,128)S(1)}, u32[]{:S(2)}, u32[]{:S(2)}) collective-permute-start(f32[2,64,128]{2,1,0:T(8,128)S(1)} %get-tuple-element.25), channel_id=1, source_target_pairs={{0,2},{1,3},{2,0},{3,1},{4,6},{5,7},{6,4},{7,5},{8,10},{9,11},{10,... | collective-permute-start | bytes 196616 | tf_op jit(solution)/shard_map/ppermute | solution.py:41
  186.6 5.9 %collective-permute-start.12 = (f32[2,64,128]{2,1,0:T(8,128)S(1)}, f32[2,64,128]{2,1,0:T(8,128)S(1)}, u32[]{:S(2)}, u32[]{:S(2)}) collective-permute-start(f32[2,64,128]{2,1,0:T(8,128)S(1)} %get-tuple-element.26), channel_id=1, source_target_pairs={{0,1},{1,2},{2,3},{3,0},{4,5},{5,6},{6,7},{7,4},{8,9},{9,10},{10,1... | collective-permute-start | bytes 196616 | tf_op jit(solution)/shard_map/ppermute | solution.py:41

commit v2 on v0

--- a/solution.py
+++ b/solution.py
@@ -167,13 +167,12 @@
         split_axis=0,
         concat_axis=0,
         tiled=True,
-    ).astype(jnp.float32)
+    )
     target = jnp.where(requested >= 0, requested, QB).reshape(-1)
-    returned_sum = (
-        jnp.zeros((QB + 1, part_rows, HD), jnp.float32)
-        .at[target]
-        .add(returned.reshape(-1, part_rows, HD))[:QB]
-    )
+    pick = (jnp.arange(QB, dtype=jnp.int32)[:, None] == target[None, :]).astype(returned.dtype)
+    returned_sum = jnp.dot(
+        pick, returned.reshape(total_slots, part_rows * HD), preferred_element_type=jnp.float32
+    ).reshape(QB, part_rows, HD)
     routed = head_exchange(returned_sum.reshape(head_count, rows_here, part_rows, HD), head_idx, head_count)
     routed = jnp.transpose(routed, (1, 0, 2, 3)).reshape(rows_here, 2, BLK, HD)
     final = grad_tiles[:, 0] + routed

time: 167 us -> 173 us (1.036)
  local copies, waits for them, and re-layouts: 26.9 us -> 36.1 us
  other arithmetic: 21.4 us -> 16.2 us
  matrix products: 13.5 us -> 15.4 us
    gather x5, local copies, waits for them, and re-layouts: 3.61 us -> 7.76 us  [head_exchange(): ahead = x[(head_idx + jnp.arange(count, dtype=jnp.int32)) % count]]
    scatter-add x1 -> x0, other arithmetic: 3.75 us -> none  [on_device(): returned_sum = jnp.zeros((QB + 1, part_rows, HD), jnp.float32).at[target]...]
    all_to_all x1, waiting for transfers between devices: 3.37 us -> 0.01 us  [on_device(): lax.all_to_all(outgoing_part.reshape(pair_count, capacity, part_rows, HD)...]
    ppermute x15, waiting for transfers between devices: 46.8 us -> 49 us  [head_exchange(): lax.ppermute(ahead[k], 'head', [(j, (j + k) % count) for j in range(count)])]
    unnamed x22 -> x14, local copies, waits for them, and re-layouts: 0.57 us -> 2.49 us
    dot_general x0 -> x1, matrix products: none -> 1.91 us  [on_device(): jnp.dot(pick, returned.reshape(total_slots, part_rows * HD), preferred_el...]
  transfers between devices with their start and end apart: 18 -> 18, of which waited for: 16 -> 16; matrix products, arithmetic and copies ran while one was open for 14% -> 15% of each run, Pallas kernels for 0% -> 0%
where the time goes in v2:
time: 173 us; the launch traced here: 172 us
  waiting for transfers between devices  63 us (36%)
  starting transfers between devices  39.9 us (23%)
  local copies, waits for them, and re-layouts  36.1 us (21%)
  other arithmetic  16.2 us (9%)
  matrix products  15.4 us (9%)
    ppermute x15, waiting for transfers between devices, head_exchange(): lax.ppermute(ahead[k], 'head', [(j, (j + k) % count) for j in range(count)])  49 us
    ppermute x15, starting transfers between devices, head_exchange(): lax.ppermute(ahead[k], 'head', [(j, (j + k) % count) for j in range(count)])  15.6 us
    all_to_all x1, starting transfers between devices, on_device(): lax.all_to_all(req_table.reshape(pair_count, capacity), 'ctx', split_axis...  12.1 us
    all_to_all x1, waiting for transfers between devices, on_device(): lax.all_to_all(send_parts, 'ctx', split_axis=0, concat_axis=0, tiled=True)  8.46 us
    gather x5, local copies, waits for them, and re-layouts, head_exchange(): ahead = x[(head_idx + jnp.arange(count, dtype=jnp.int32)) % count]  7.76 us
    all_to_all x1, starting transfers between devices, on_device(): lax.all_to_all(outgoing_part.reshape(pair_count, capacity, part_rows, HD)...  6.63 us
    all_to_all x1, starting transfers between devices, on_device(): lax.all_to_all(send_parts, 'ctx', split_axis=0, concat_axis=0, tiled=True)  5.55 us
    all_to_all x1, waiting for transfers between devices, on_device(): lax.all_to_all(req_table.reshape(pair_count, capacity), 'ctx', split_axis...  5.48 us
  transfers between devices with their start and end apart: 18, of which 16 were waited for; matrix products, arithmetic and copies ran while one was open for 15% of the time, Pallas kernels for 0%

profile of v2, /device:TPU:8, one launch (start us, length us, event | category | flops | bytes accessed | tf_op | source)
XLA Modules:
  0.0 171.8 jit_solution(2963743471076943128)
XLA Ops:
  0.7 0.8 compare_and_fusion.1
  5.2 12.1 %all-to-all-start = ((s32[64,1,1]{2,1,0:T(1,128)}), s32[64,1,1]{2,1,0:T(1,128)S(1)}, u32[]{:S(2)}, u32[]{:S(2)}) async-start(s32[64,1,1]{2,1,0:T(1,128)} %copy.89), calls=%async_computation | async-start | bytes 65536 | tf_op jit(solution)/shard_map/all_to_all | solution.py:65
  17.4 1.3 pad_maximum_fusion.1
  18.7 1.1 pad_maximum_fusion.6
  20.4 5.5 %all-to-all-done = s32[64,1,1]{2,1,0:T(1,128)S(1)} async-done(((s32[64,1,1]{2,1,0:T(1,128)}), s32[64,1,1]{2,1,0:T(1,128)S(1)}, u32[]{:S(2)}, u32[]{:S(2)}) %all-to-all-start) | async-done | bytes 288 | tf_op jit(solution)/shard_map/all_to_all | solution.py:65
  25.9 2.7 %fusion.74 = (s32[64]{0:T(128)}, s32[64]{0:T(128)S(1)}) fusion(s32[64,1,1]{2,1,0:T(1,128)S(1)} %all-to-all-done), kind=kLoop, calls=%fused_computation.163 | loop fusion | flops 64 | bytes 768 | tf_op jit(solution)/shard_map/all_to_all | solution.py:65
  28.6 1.7 gather_fusion
  30.3 5.5 %all-to-all-start.1 = ((bf16[64,1,64,128]{3,2,1,0:T(8,128)(2,1)}), bf16[64,1,64,128]{3,2,1,0:T(8,128)(2,1)S(1)}, u32[]{:S(2)}, u32[]{:S(2)}) async-start(bf16[64,1,64,128]{3,2,1,0:T(8,128)(2,1)} %bitcast.8), calls=%async_computation.1 | async-start | bytes 2097152 | tf_op jit(solution)/shard_map/all_to_all | solution.py:85
  35.8 0.8 fusion.78
  36.6 2.8 %collective-permute-start.5 = (bf16[2,256,256]{2,1,0:T(8,128)(2,1)S(1)}, bf16[2,256,256]{2,1,0:T(8,128)(2,1)S(1)}, u32[]{:S(2)}, u32[]{:S(2)}) collective-permute-start(bf16[2,256,256]{2,1,0:T(8,128)(2,1)S(1)} %get-tuple-element.21), channel_id=1, source_target_pairs={{0,3},{1,0},{2,1},{3,2},{4,7},{5,4},{6,5},{7,6},{8,11},{9,8},{10,9... | collective-permute-start | bytes 786440 | tf_op jit(solution)/shard_map/ppermute | solution.py:41
  39.4 0.8 collective-permute-start.4
  40.2 0.9 collective-permute-start.3
  41.6 0.9 copy_bitcast_fusion
  42.6 0.9 scatter_custom_fusion.1
  44.0 6.9 %collective-permute-done.5 = bf16[2,256,256]{2,1,0:T(8,128)(2,1)S(1)} collective-permute-done((bf16[2,256,256]{2,1,0:T(8,128)(2,1)S(1)}, bf16[2,256,256]{2,1,0:T(8,128)(2,1)S(1)}, u32[]{:S(2)}, u32[]{:S(2)}) %collective-permute-start.5) | collective-permute-done | bytes 262176 | tf_op jit(solution)/shard_map/ppermute | solution.py:41
  50.9 3.7 %collective-permute-done.3 = bf16[2,256,256]{2,1,0:T(8,128)(2,1)S(1)} collective-permute-done((bf16[2,256,256]{2,1,0:T(8,128)(2,1)S(1)}, bf16[2,256,256]{2,1,0:T(8,128)(2,1)S(1)}, u32[]{:S(2)}, u32[]{:S(2)}) %collective-permute-start.3) | collective-permute-done | bytes 262176 | tf_op jit(solution)/shard_map/ppermute | solution.py:41
  54.5 1.1 pad_maximum_fusion.2
  56.2 8.5 %all-to-all-done.1 = bf16[64,1,64,128]{3,2,1,0:T(8,128)(2,1)S(1)} async-done(((bf16[64,1,64,128]{3,2,1,0:T(8,128)(2,1)}), bf16[64,1,64,128]{3,2,1,0:T(8,128)(2,1)S(1)}, u32[]{:S(2)}, u32[]{:S(2)}) %all-to-all-start.1) | async-done | bytes 1048608 | tf_op jit(solution)/shard_map/all_to_all | solution.py:85
  64.7 1.6 gather_fusion.1
  66.3 1.9 %gather_fusion.2 = bf16[4,14,64,128]{3,2,1,0:T(8,128)(2,1)S(1)} fusion(bf16[4,14,64,128]{3,2,1,0:T(8,128)(2,1)} %bitcast.229, s32[1024]{0:T(1024)S(1)} %pad_clamp_fusion.2), kind=kCustom, calls=%fused_computation.2 | custom fusion | bytes 1835024 | tf_op jit(solution)/shard_map/gather | solution.py:38
  68.2 0.9 fusion.80
  69.1 2.8 %collective-permute-start.2 = (bf16[14,64,128]{2,1,0:T(8,128)(2,1)}, bf16[14,64,128]{2,1,0:T(8,128)(2,1)S(1)}, u32[]{:S(2)}, u32[]{:S(2)}) collective-permute-start(bf16[14,64,128]{2,1,0:T(8,128)(2,1)} %get-tuple-element.29), channel_id=1, source_target_pairs={{0,3},{1,0},{2,1},{3,2},{4,7},{5,4},{6,5},{7,6},{8,11},{9,8},{10,9... | collective-permute-start | bytes 688136 | tf_op jit(solution)/shard_map/ppermute | solution.py:41
  71.8 0.8 collective-permute-start.1
  72.6 0.9 collective-permute-start
  74.8 1.1 copy.99
  75.9 5.0 %collective-permute-done.2 = bf16[14,64,128]{2,1,0:T(8,128)(2,1)S(1)} collective-permute-done((bf16[14,64,128]{2,1,0:T(8,128)(2,1)}, bf16[14,64,128]{2,1,0:T(8,128)(2,1)S(1)}, u32[]{:S(2)}, u32[]{:S(2)}) %collective-permute-start.2) | collective-permute-done | bytes 229408 | tf_op jit(solution)/shard_map/ppermute | solution.py:41
  81.0 1.1 collective-permute-done.1
  82.1 2.5 %collective-permute-done = bf16[14,64,128]{2,1,0:T(8,128)(2,1)} collective-permute-done((bf16[14,64,128]{2,1,0:T(8,128)(2,1)}, bf16[14,64,128]{2,1,0:T(8,128)(2,1)}, u32[]{:S(2)}, u32[]{:S(2)}) %collective-permute-start) | collective-permute-done | bytes 229408 | tf_op jit(solution)/shard_map/ppermute | solution.py:41
  84.6 1.2 pad_maximum_fusion.4
  86.6 1.3 fusion.5
  88.0 1.8 %fusion.2 = f32[2,8,128]{2,1,0:T(8,128)S(1)} fusion(f32[2,8,128,128,8]{3,2,4,1,0:T(8,128)S(1)} %get-tuple-element.40, f32[2,8,128]{2,1,0:T(8,128)S(1)} %get-tuple-element.39, pred[2,128,8,128]{1,3,2,0:T(8,128)(4,1)S(1)} %compare_and_fusion), kind=kLoop, calls=%fused_computation.21 | loop fusion | flops 8386560 | bytes 8667136 | tf_op jit(solution)/shard_map/reduce_sum | solution.py:119
  89.8 2.9 %multiply_reduce_fusion = (f32[2,128,8]{1,2,0:T(8,128)S(1)}, bf16[2,128,8,128]{1,3,2,0:T(8,128)(2,1)}) fusion(bf16[2,128,8,128]{1,3,2,0:T(8,128)(2,1)S(1)} %copy-done.3, f32[2,128,8]{1,2,0:T(8,128)S(1)} %bitcast.265, f32[2,8,128,128,8]{3,2,4,1,0:T(8,128)S(1)} %get-tuple-element.40, f32[2,8,128]{2,1,0:T(8,128)S(1)} %get-tuple-element.39, ...), kind=kOutput, calls=%fused_computation.52 | convolution fusion | flops 547878912 | bytes 10772480 | tf_op jit(solution)/shard_map/qhisj,qsjd->qihd/dot_general | solution.py:120
  92.7 2.0 %fusion.16 = f32[2,8,1,128,128]{4,3,1,0,2:T(8,128)S(1)} fusion(f32[2,8,128,128,8]{3,2,4,1,0:T(8,128)S(1)} %get-tuple-element.40, f32[2,8,128]{2,1,0:T(8,128)S(1)} %log_add_fusion, pred[2,128,8,128]{1,3,2,0:T(8,128)(4,1)S(1)} %compare_and_fusion, bf16[2,128,8,128,1]{3,2,1,0,4:T(8,128)(2,1)S(1)} %bitcast.231), kind=kOutput, calls=%fused_computation.34 | convolution fusion | flops 545259520 | bytes 10231808 | tf_op jit(solution)/shard_map/qhisj,qihd->qsjd/dot_general | solution.py:146
  94.8 2.8 %fusion.1 = bf16[2,8,128,8,128]{2,4,1,3,0:T(8,128)(2,1)S(1)} fusion(f32[2,8,128,128,8]{3,2,4,1,0:T(8,128)S(1)} %get-tuple-element.40, f32[2,8,128]{2,1,0:T(8,128)S(1)} %bitcast.266, f32[2,8,128]{2,1,0:T(8,128)S(1)} %log_add_fusion, pred[2,128,8,128]{1,3,2,0:T(8,128)(4,1)S(1)} %compare_and_fusion, bf16[2,128,8,128,1]{3,2,1,0,4:T(8,128)(2,1)S(1)} %bitcast.232, ...), kind=kOutput, calls=%fused_computation.17 | convolution fusion | flops 550502400 | bytes 14434304 | tf_op jit(solution)/shard_map/qihd,qsjd->qhisj/dot_general | solution.py:132
  97.6 2.0 %copy-done = bf16[2,8,128,8,128]{2,4,1,3,0:T(8,128)(2,1)} copy-done((bf16[2,8,128,8,128]{2,4,1,3,0:T(8,128)(2,1)}, bf16[2,8,128,8,128]{2,4,1,3,0:T(8,128)(2,1)S(1)}, u32[]{:S(2)}) %copy-start) | copy-done | bytes 4194328
  99.6 1.3 fusion.21
  100.9 1.0 copy.107
  102.0 1.9 %gather_fusion.8 = bf16[4,14,64,128]{3,2,1,0:T(8,128)(2,1)S(1)} fusion(bf16[4,14,64,128]{3,2,0,1:T(8,128)(2,1)} %bitcast.228, s32[1024]{0:T(1024)S(1)} %pad_clamp_fusion.2), kind=kCustom, calls=%fused_computation.8 | custom fusion | bytes 1835024 | tf_op jit(solution)/shard_map/gather | solution.py:38
  105.4 0.9 collective-permute-start.9
  106.3 6.2 %collective-permute-done.11 = bf16[14,64,128]{2,1,0:T(8,128)(2,1)S(1)} collective-permute-done((bf16[14,64,128]{2,1,0:T(8,128)(2,1)S(1)}, bf16[14,64,128]{2,1,0:T(8,128)(2,1)S(1)}, u32[]{:S(2)}, u32[]{:S(2)}) %collective-permute-start.11) | collective-permute-done | bytes 229408 | tf_op jit(solution)/shard_map/ppermute | solution.py:41
  112.5 2.2 %collective-permute-done.10 = bf16[14,64,128]{2,1,0:T(8,128)(2,1)S(1)} collective-permute-done((bf16[14,64,128]{2,1,0:T(8,128)(2,1)S(1)}, bf16[14,64,128]{2,1,0:T(8,128)(2,1)S(1)}, u32[]{:S(2)}, u32[]{:S(2)}) %collective-permute-start.10) | collective-permute-done | bytes 229408 | tf_op jit(solution)/shard_map/ppermute | solution.py:41
  114.7 3.5 %collective-permute-done.9 = bf16[14,64,128]{2,1,0:T(8,128)(2,1)S(1)} collective-permute-done((bf16[14,64,128]{2,1,0:T(8,128)(2,1)S(1)}, bf16[14,64,128]{2,1,0:T(8,128)(2,1)S(1)}, u32[]{:S(2)}, u32[]{:S(2)}) %collective-permute-start.9) | collective-permute-done | bytes 229408 | tf_op jit(solution)/shard_map/ppermute | solution.py:41
  118.3 1.6 gather_fusion.9
  119.9 1.2 concatenate.8
  121.2 1.7 gather_fusion.10
  122.9 6.6 %all-to-all-start.2 = ((bf16[64,1,64,128]{3,2,1,0:T(8,128)(2,1)}), bf16[64,1,64,128]{3,2,1,0:T(8,128)(2,1)}, u32[]{:S(2)}, u32[]{:S(2)}) async-start(bf16[64,1,64,128]{3,2,1,0:T(8,128)(2,1)} %bitcast.224), calls=%async_computation.2 | async-start | bytes 2097152 | tf_op jit(solution)/shard_map/all_to_all | solution.py:164
  129.5 3.1 %fusion.23 = bf16[2,128,8,128]{1,3,2,0:T(8,128)(2,1)S(1)} fusion(bf16[2,8,128,8,128]{2,4,1,3,0:T(8,128)(2,1)} %copy-done, bf16[2,1,2,128,128]{4,3,1,0,2:T(8,128)(2,1)S(1)} %copy_bitcast_fusion, bf16[2,7,2,128,128]{4,3,2,1,0:T(8,128)(2,1)} %bitcast.244), kind=kOutput, calls=%fused_computation.41 | convolution fusion | flops 538443776 | bytes 5767168 | tf_op jit(solution)/shard_map/qhisj,qsjd->qihd/dot_general | solution.py:139
  133.3 0.9 copy.104
  134.2 1.3 copy.96
  135.9 2.1 %maximum_bitcast_fusion = bf16[4,2,256,256]{3,2,1,0:T(8,128)(2,1)} fusion(bf16[1,256,4,256]{3,1,0,2:T(8,128)(2,1)} %copy.104, bf16[1,256,4,256]{3,1,0,2:T(8,128)(2,1)S(1)} %copy.103), kind=kLoop, calls=%fused_computation.50 | loop fusion | flops 524288 | bytes 2097152 | tf_op jit(solution)/shard_map/transpose | solution.py:181
  138.1 1.8 %gather_fusion.6 = bf16[4,2,256,256]{3,2,1,0:T(8,128)(2,1)S(1)} fusion(bf16[4,2,256,256]{3,2,1,0:T(8,128)(2,1)} %maximum_bitcast_fusion, s32[1024]{0:T(1024)S(1)} %pad_clamp_fusion.2), kind=kCustom, calls=%fused_computation.6 | custom fusion | bytes 2097168 | tf_op jit(solution)/shard_map/gather | solution.py:38
  140.0 0.9 collective-permute-start.8
  141.5 0.8 collective-permute-start.6
  142.3 6.9 %collective-permute-done.8 = bf16[2,256,256]{2,1,0:T(8,128)(2,1)S(1)} collective-permute-done((bf16[2,256,256]{2,1,0:T(8,128)(2,1)S(1)}, bf16[2,256,256]{2,1,0:T(8,128)(2,1)S(1)}, u32[]{:S(2)}, u32[]{:S(2)}) %collective-permute-start.8) | collective-permute-done | bytes 262176 | tf_op jit(solution)/shard_map/ppermute | solution.py:41
  149.2 2.4 %collective-permute-done.7 = bf16[2,256,256]{2,1,0:T(8,128)(2,1)S(1)} collective-permute-done((bf16[2,256,256]{2,1,0:T(8,128)(2,1)S(1)}, bf16[2,256,256]{2,1,0:T(8,128)(2,1)S(1)}, u32[]{:S(2)}, u32[]{:S(2)}) %collective-permute-start.7) | collective-permute-done | bytes 262176 | tf_op jit(solution)/shard_map/ppermute | solution.py:41
  151.6 4.4 %collective-permute-done.6 = bf16[2,256,256]{2,1,0:T(8,128)(2,1)S(1)} collective-permute-done((bf16[2,256,256]{2,1,0:T(8,128)(2,1)S(1)}, bf16[2,256,256]{2,1,0:T(8,128)(2,1)S(1)}, u32[]{:S(2)}, u32[]{:S(2)}) %collective-permute-start.6) | collective-permute-done | bytes 262176 | tf_op jit(solution)/shard_map/ppermute | solution.py:41
  156.1 1.1 pad_maximum_fusion.3
  157.2 1.8 %gather_fusion.7 = bf16[4,2,256,256]{3,2,1,0:T(8,128)(2,1)S(1)} fusion(bf16[4,2,256,256]{3,2,1,0:T(8,128)(2,1)} %pad_maximum_fusion.3, s32[1024]{0:T(1024)S(1)} %pad_clamp_fusion.1), kind=kCustom, calls=%fused_computation.7 | custom fusion | bytes 2097168 | tf_op jit(solution)/shard_map/gather | solution.py:43
  159.1 1.9 %fusion.24 = f32[4,2,64,128]{3,0,2,1:T(4,128)S(1)} fusion(s32[64]{0:T(128)S(1)} %compare_select_fusion.3, s32[4,2]{0,1:T(2,128)S(1)} %multiply_add_fusion, bf16[8,8,64,128]{3,2,1,0:T(8,128)(2,1)} %bitcast.117), kind=kOutput, calls=%fused_computation.44 | convolution fusion | flops 8389120 | bytes 1311008 | tf_op jit(solution)/shard_map/dot_general | solution.py:173
  161.7 1.5 gather_fusion.11
  164.5 0.8 collective-permute-start.12
  165.3 1.0 fusion.75
  166.4 1.7 collective-permute-done.14
  168.0 1.8 %collective-permute-done.13 = f32[2,64,128]{2,1,0:T(8,128)S(1)} collective-permute-done((f32[2,64,128]{2,1,0:T(8,128)S(1)}, f32[2,64,128]{2,1,0:T(8,128)S(1)}, u32[]{:S(2)}, u32[]{:S(2)}) %collective-permute-start.13) | collective-permute-done | bytes 65568 | tf_op jit(solution)/shard_map/ppermute | solution.py:41
  (88 shorter events, 15.5 us)
Async XLA Ops:
  0.6 40.9 %copy-start.4 = (s32[8,8]{1,0:T(8,128)S(1)}, s32[8,8]{1,0:T(8,128)}, u32[]{:S(2)}) copy-start(s32[8,8]{1,0:T(8,128)} %param.9) | copy-start | bytes 772
  0.6 40.9 %copy-start.1 = (bf16[1024,128]{1,0:T(8,128)(2,1)S(1)}, bf16[1024,128]{1,0:T(8,128)(2,1)}, u32[]{:S(2)}) copy-start(bf16[1024,128]{1,0:T(8,128)(2,1)} %param.6) | copy-start | bytes 786436
  3.2 0.5 copy-start.6
  5.2 20.7 %all-to-all-start = ((s32[64,1,1]{2,1,0:T(1,128)}), s32[64,1,1]{2,1,0:T(1,128)S(1)}, u32[]{:S(2)}, u32[]{:S(2)}) async-start(s32[64,1,1]{2,1,0:T(1,128)} %copy.89), calls=%async_computation | async-start | bytes 65536 | tf_op jit(solution)/shard_map/all_to_all | solution.py:65
  30.3 34.4 %all-to-all-start.1 = ((bf16[64,1,64,128]{3,2,1,0:T(8,128)(2,1)}), bf16[64,1,64,128]{3,2,1,0:T(8,128)(2,1)S(1)}, u32[]{:S(2)}, u32[]{:S(2)}) async-start(bf16[64,1,64,128]{3,2,1,0:T(8,128)(2,1)} %bitcast.8), calls=%async_computation.1 | async-start | bytes 2097152 | tf_op jit(solution)/shard_map/all_to_all | solution.py:85
  36.6 14.3 %collective-permute-start.5 = (bf16[2,256,256]{2,1,0:T(8,128)(2,1)S(1)}, bf16[2,256,256]{2,1,0:T(8,128)(2,1)S(1)}, u32[]{:S(2)}, u32[]{:S(2)}) collective-permute-start(bf16[2,256,256]{2,1,0:T(8,128)(2,1)S(1)} %get-tuple-element.21), channel_id=1, source_target_pairs={{0,3},{1,0},{2,1},{3,2},{4,7},{5,4},{6,5},{7,6},{8,11},{9,8},{10,9... | collective-permute-start | bytes 786440 | tf_op jit(solution)/shard_map/ppermute | solution.py:41
  39.4 11.5 %collective-permute-start.4 = (bf16[2,256,256]{2,1,0:T(8,128)(2,1)S(1)}, bf16[2,256,256]{2,1,0:T(8,128)(2,1)S(1)}, u32[]{:S(2)}, u32[]{:S(2)}) collective-permute-start(bf16[2,256,256]{2,1,0:T(8,128)(2,1)S(1)} %get-tuple-element.19), channel_id=1, source_target_pairs={{0,2},{1,3},{2,0},{3,1},{4,6},{5,7},{6,4},{7,5},{8,10},{9,11},{10,... | collective-permute-start | bytes 786440 | tf_op jit(solution)/shard_map/ppermute | solution.py:41
  40.2 14.4 %collective-permute-start.3 = (bf16[2,256,256]{2,1,0:T(8,128)(2,1)S(1)}, bf16[2,256,256]{2,1,0:T(8,128)(2,1)S(1)}, u32[]{:S(2)}, u32[]{:S(2)}) collective-permute-start(bf16[2,256,256]{2,1,0:T(8,128)(2,1)S(1)} %get-tuple-element.20), channel_id=1, source_target_pairs={{0,1},{1,2},{2,3},{3,0},{4,5},{5,6},{6,7},{7,4},{8,9},{9,10},{10,1... | collective-permute-start | bytes 786440 | tf_op jit(solution)/shard_map/ppermute | solution.py:41
  69.1 11.9 %collective-permute-start.2 = (bf16[14,64,128]{2,1,0:T(8,128)(2,1)}, bf16[14,64,128]{2,1,0:T(8,128)(2,1)S(1)}, u32[]{:S(2)}, u32[]{:S(2)}) collective-permute-start(bf16[14,64,128]{2,1,0:T(8,128)(2,1)} %get-tuple-element.29), channel_id=1, source_target_pairs={{0,3},{1,0},{2,1},{3,2},{4,7},{5,4},{6,5},{7,6},{8,11},{9,8},{10,9... | collective-permute-start | bytes 688136 | tf_op jit(solution)/shard_map/ppermute | solution.py:41
  71.8 10.3 %collective-permute-start.1 = (bf16[14,64,128]{2,1,0:T(8,128)(2,1)}, bf16[14,64,128]{2,1,0:T(8,128)(2,1)}, u32[]{:S(2)}, u32[]{:S(2)}) collective-permute-start(bf16[14,64,128]{2,1,0:T(8,128)(2,1)} %get-tuple-element.27), channel_id=1, source_target_pairs={{0,2},{1,3},{2,0},{3,1},{4,6},{5,7},{6,4},{7,5},{8,10},{9,11},{10,... | collective-permute-start | bytes 688136 | tf_op jit(solution)/shard_map/ppermute | solution.py:41
  72.6 12.0 %collective-permute-start = (bf16[14,64,128]{2,1,0:T(8,128)(2,1)}, bf16[14,64,128]{2,1,0:T(8,128)(2,1)}, u32[]{:S(2)}, u32[]{:S(2)}) collective-permute-start(bf16[14,64,128]{2,1,0:T(8,128)(2,1)} %get-tuple-element.28), channel_id=1, source_target_pairs={{0,1},{1,2},{2,3},{3,0},{4,5},{5,6},{6,7},{7,4},{8,9},{9,10},{10,1... | collective-permute-start | bytes 688136 | tf_op jit(solution)/shard_map/ppermute | solution.py:41
  86.6 8.1 %copy-start.2 = (bf16[14,4,64,128]{3,2,1,0:T(8,128)(2,1)}, bf16[14,4,64,128]{3,2,1,0:T(8,128)(2,1)S(1)}, u32[]{:S(2)}) copy-start(bf16[14,4,64,128]{3,2,1,0:T(8,128)(2,1)S(1)} %copy.90) | copy-start | bytes 2752516
  86.6 3.2 %copy-start.3 = (bf16[2,128,8,128]{1,3,2,0:T(8,128)(2,1)S(1)}, bf16[2,128,8,128]{1,3,2,0:T(8,128)(2,1)}, u32[]{:S(2)}) copy-start(bf16[2,128,8,128]{1,3,2,0:T(8,128)(2,1)} %copy.99) | copy-start | bytes 1572868
  97.6 2.0 %copy-start = (bf16[2,8,128,8,128]{2,4,1,3,0:T(8,128)(2,1)}, bf16[2,8,128,8,128]{2,4,1,3,0:T(8,128)(2,1)S(1)}, u32[]{:S(2)}) copy-start(bf16[2,8,128,8,128]{2,4,1,3,0:T(8,128)(2,1)S(1)} %fusion.1) | copy-start | bytes 12582916
  104.0 8.6 %collective-permute-start.11 = (bf16[14,64,128]{2,1,0:T(8,128)(2,1)S(1)}, bf16[14,64,128]{2,1,0:T(8,128)(2,1)S(1)}, u32[]{:S(2)}, u32[]{:S(2)}) collective-permute-start(bf16[14,64,128]{2,1,0:T(8,128)(2,1)S(1)} %get-tuple-element.25), channel_id=1, source_target_pairs={{0,3},{1,0},{2,1},{3,2},{4,7},{5,4},{6,5},{7,6},{8,11},{9,8},{10,9... | collective-permute-start | bytes 688136 | tf_op jit(solution)/shard_map/ppermute | solution.py:41
  104.7 10.0 %collective-permute-start.10 = (bf16[14,64,128]{2,1,0:T(8,128)(2,1)S(1)}, bf16[14,64,128]{2,1,0:T(8,128)(2,1)S(1)}, u32[]{:S(2)}, u32[]{:S(2)}) collective-permute-start(bf16[14,64,128]{2,1,0:T(8,128)(2,1)S(1)} %get-tuple-element.23), channel_id=1, source_target_pairs={{0,2},{1,3},{2,0},{3,1},{4,6},{5,7},{6,4},{7,5},{8,10},{9,11},{10,... | collective-permute-start | bytes 688136 | tf_op jit(solution)/shard_map/ppermute | solution.py:41
  105.4 12.8 %collective-permute-start.9 = (bf16[14,64,128]{2,1,0:T(8,128)(2,1)S(1)}, bf16[14,64,128]{2,1,0:T(8,128)(2,1)S(1)}, u32[]{:S(2)}, u32[]{:S(2)}) collective-permute-start(bf16[14,64,128]{2,1,0:T(8,128)(2,1)S(1)} %get-tuple-element.24), channel_id=1, source_target_pairs={{0,1},{1,2},{2,3},{3,0},{4,5},{5,6},{6,7},{7,4},{8,9},{9,10},{10,1... | collective-permute-start | bytes 688136 | tf_op jit(solution)/shard_map/ppermute | solution.py:41
  122.9 36.2 %all-to-all-start.2 = ((bf16[64,1,64,128]{3,2,1,0:T(8,128)(2,1)}), bf16[64,1,64,128]{3,2,1,0:T(8,128)(2,1)}, u32[]{:S(2)}, u32[]{:S(2)}) async-start(bf16[64,1,64,128]{3,2,1,0:T(8,128)(2,1)} %bitcast.224), calls=%async_computation.2 | async-start | bytes 2097152 | tf_op jit(solution)/shard_map/all_to_all | solution.py:164
  129.5 12.8 %copy-start.5 = (s32[64]{0:T(128)S(1)}, s32[64]{0:T(128)}, u32[]{:S(2)}) copy-start(s32[64]{0:T(128)} %get-tuple-element.4) | copy-start | bytes 772
  140.0 9.3 %collective-permute-start.8 = (bf16[2,256,256]{2,1,0:T(8,128)(2,1)S(1)}, bf16[2,256,256]{2,1,0:T(8,128)(2,1)S(1)}, u32[]{:S(2)}, u32[]{:S(2)}) collective-permute-start(bf16[2,256,256]{2,1,0:T(8,128)(2,1)S(1)} %get-tuple-element.15), channel_id=1, source_target_pairs={{0,3},{1,0},{2,1},{3,2},{4,7},{5,4},{6,5},{7,6},{8,11},{9,8},{10,9... | collective-permute-start | bytes 786440 | tf_op jit(solution)/shard_map/ppermute | solution.py:41
  140.9 10.7 %collective-permute-start.7 = (bf16[2,256,256]{2,1,0:T(8,128)(2,1)S(1)}, bf16[2,256,256]{2,1,0:T(8,128)(2,1)S(1)}, u32[]{:S(2)}, u32[]{:S(2)}) collective-permute-start(bf16[2,256,256]{2,1,0:T(8,128)(2,1)S(1)} %get-tuple-element.13), channel_id=1, source_target_pairs={{0,2},{1,3},{2,0},{3,1},{4,6},{5,7},{6,4},{7,5},{8,10},{9,11},{10,... | collective-permute-start | bytes 786440 | tf_op jit(solution)/shard_map/ppermute | solution.py:41
  141.5 14.6 %collective-permute-start.6 = (bf16[2,256,256]{2,1,0:T(8,128)(2,1)S(1)}, bf16[2,256,256]{2,1,0:T(8,128)(2,1)S(1)}, u32[]{:S(2)}, u32[]{:S(2)}) collective-permute-start(bf16[2,256,256]{2,1,0:T(8,128)(2,1)S(1)} %get-tuple-element.14), channel_id=1, source_target_pairs={{0,1},{1,2},{2,3},{3,0},{4,5},{5,6},{6,7},{7,4},{8,9},{9,10},{10,1... | collective-permute-start | bytes 786440 | tf_op jit(solution)/shard_map/ppermute | solution.py:41
  163.2 4.8 %collective-permute-start.14 = (f32[2,64,128]{2,1,0:T(8,128)S(1)}, f32[2,64,128]{2,1,0:T(8,128)S(1)}, u32[]{:S(2)}, u32[]{:S(2)}) collective-permute-start(f32[2,64,128]{2,1,0:T(8,128)S(1)} %get-tuple-element.33), channel_id=1, source_target_pairs={{0,3},{1,0},{2,1},{3,2},{4,7},{5,4},{6,5},{7,6},{8,11},{9,8},{10,9... | collective-permute-start | bytes 196616 | tf_op jit(solution)/shard_map/ppermute | solution.py:41
  163.9 6.0 %collective-permute-start.13 = (f32[2,64,128]{2,1,0:T(8,128)S(1)}, f32[2,64,128]{2,1,0:T(8,128)S(1)}, u32[]{:S(2)}, u32[]{:S(2)}) collective-permute-start(f32[2,64,128]{2,1,0:T(8,128)S(1)} %get-tuple-element.31), channel_id=1, source_target_pairs={{0,2},{1,3},{2,0},{3,1},{4,6},{5,7},{6,4},{7,5},{8,10},{9,11},{10,... | collective-permute-start | bytes 196616 | tf_op jit(solution)/shard_map/ppermute | solution.py:41
  164.5 5.9 %collective-permute-start.12 = (f32[2,64,128]{2,1,0:T(8,128)S(1)}, f32[2,64,128]{2,1,0:T(8,128)S(1)}, u32[]{:S(2)}, u32[]{:S(2)}) collective-permute-start(f32[2,64,128]{2,1,0:T(8,128)S(1)} %get-tuple-element.32), channel_id=1, source_target_pairs={{0,1},{1,2},{2,3},{3,0},{4,5},{5,6},{6,7},{7,4},{8,9},{9,10},{10,1... | collective-permute-start | bytes 196616 | tf_op jit(solution)/shard_map/ppermute | solution.py:41

commit v3 on v0

--- a/solution.py
+++ b/solution.py
@@ -82,12 +82,16 @@
     kv_parts = kv_blocks.reshape(QB, head_count, part_rows, HD)
     my_part = lax.dynamic_index_in_dim(kv_parts, head_idx, axis=1, keepdims=False)
     send_parts = my_part[jnp.maximum(requested, 0)]
-    fetched_part = lax.all_to_all(send_parts, "ctx", split_axis=0, concat_axis=0, tiled=True).reshape(
-        total_slots, part_rows, HD
-    )
     entry_slot = jnp.where(usable, slot_idx, 0).reshape(head_count, my_entries)
-    share = fetched_part[entry_slot]
-    got = head_exchange(share, head_idx, head_count)
+    chunk_rows = part_rows // 2
+    got_chunks = []
+    for chunk in range(2):
+        sent = send_parts[:, :, chunk * chunk_rows : (chunk + 1) * chunk_rows]
+        fetched_chunk = lax.all_to_all(sent, "ctx", split_axis=0, concat_axis=0, tiled=True).reshape(
+            total_slots, chunk_rows, HD
+        )
+        got_chunks.append(head_exchange(fetched_chunk[entry_slot], head_idx, head_count))
+    got = jnp.concatenate(got_chunks, axis=2)
     remote_kv = jnp.transpose(got, (1, 0, 2, 3)).reshape(rows_here, extras, 2, BLK, HD)
     first_row = head_idx * rows_here
     own_kv = lax.dynamic_slice_in_dim(kv_blocks, first_row, rows_here, axis=0)
@@ -174,7 +178,9 @@
         .at[target]
         .add(returned.reshape(-1, part_rows, HD))[:QB]
     )
-    routed = head_exchange(returned_sum.reshape(head_count, rows_here, part_rows, HD), head_idx, head_count)
+    routed = lax.all_to_all(
+        returned_sum.reshape(head_count, rows_here, part_rows, HD), "head", split_axis=0, concat_axis=0, tiled=True
+    )
     routed = jnp.transpose(routed, (1, 0, 2, 3)).reshape(rows_here, 2, BLK, HD)
     final = grad_tiles[:, 0] + routed
     out_rows = rows_here * BLK

time: 167 us -> 181 us (1.084)
  starting transfers between devices: 40 us -> 51.4 us
  local copies, waits for them, and re-layouts: 26.9 us -> 29.4 us
    ppermute x15, waiting for transfers between devices: 46.8 us -> 27.7 us  [head_exchange(): lax.ppermute(ahead[k], 'head', [(j, (j + k) % count) for j in range(count)])]
    all_to_all x1 -> x3, waiting for transfers between devices: 8 us -> 25.7 us  [the longest x2 21.3 us: on_device(): lax.all_to_all(sent, 'ctx', split_axis=0, concat_axis=0, tiled=True)]
    all_to_all x1 -> x3, starting transfers between devices: 5.55 us -> 14.8 us  [the longest x2 11.4 us: on_device(): lax.all_to_all(sent, 'ctx', split_axis=0, concat_axis=0, tiled=True)]
    ppermute x15, starting transfers between devices: 15.7 us -> 18.5 us  [head_exchange(): lax.ppermute(ahead[k], 'head', [(j, (j + k) % count) for j in range(count)])]
  transfers between devices with their start and end apart: 18 -> 20, of which waited for: 16 -> 14; matrix products, arithmetic and copies ran while one was open for 14% -> 19% of each run, Pallas kernels for 0% -> 0%
where the time goes in v3:
time: 181 us; the launch traced here: 180 us
  waiting for transfers between devices  63.6 us (35%)
  starting transfers between devices  51.4 us (28%)
  local copies, waits for them, and re-layouts  29.4 us (16%)
  other arithmetic  21 us (12%)
  matrix products  13.5 us (7%)
    ppermute x15, waiting for transfers between devices, head_exchange(): lax.ppermute(ahead[k], 'head', [(j, (j + k) % count) for j in range(count)])  27.7 us
    all_to_all x2, waiting for transfers between devices, on_device(): lax.all_to_all(sent, 'ctx', split_axis=0, concat_axis=0, tiled=True)  21.3 us
    ppermute x15, starting transfers between devices, head_exchange(): lax.ppermute(ahead[k], 'head', [(j, (j + k) % count) for j in range(count)])  18.5 us
    all_to_all x1, starting transfers between devices, on_device(): lax.all_to_all(req_table.reshape(pair_count, capacity), 'ctx', split_axis...  12.1 us
    all_to_all x2, starting transfers between devices, on_device(): lax.all_to_all(sent, 'ctx', split_axis=0, concat_axis=0, tiled=True)  11.4 us
    all_to_all x1, waiting for transfers between devices, on_device(): lax.all_to_all(req_table.reshape(pair_count, capacity), 'ctx', split_axis...  7.1 us
    all_to_all x1, starting transfers between devices, on_device(): lax.all_to_all(outgoing_part.reshape(pair_count, capacity, part_rows, HD)...  5.94 us
    gather x5, local copies, waits for them, and re-layouts, head_exchange(): return jnp.stack(got)[order]  4.99 us
  transfers between devices with their start and end apart: 20, of which 14 were waited for; matrix products, arithmetic and copies ran while one was open for 19% of the time, Pallas kernels for 0%

profile of v3, /device:TPU:8, one launch (start us, length us, event | category | flops | bytes accessed | tf_op | source)
XLA Modules:
  0.0 180.2 jit_solution(7488517864882815796)
XLA Ops:
  0.7 1.3 pad_maximum_fusion.1
  2.7 0.9 fusion.74
  3.6 2.8 %collective-permute-start.8 = (bf16[2,256,256]{2,1,0:T(8,128)(2,1)}, bf16[2,256,256]{2,1,0:T(8,128)(2,1)S(1)}, u32[]{:S(2)}, u32[]{:S(2)}) collective-permute-start(bf16[2,256,256]{2,1,0:T(8,128)(2,1)} %get-tuple-element.23), channel_id=1, source_target_pairs={{0,3},{1,0},{2,1},{3,2},{4,7},{5,4},{6,5},{7,6},{8,11},{9,8},{10,9... | collective-permute-start | bytes 786440 | tf_op jit(solution)/shard_map/ppermute | solution.py:41
  6.3 0.8 collective-permute-start.7
  7.1 0.9 collective-permute-start.6
  8.0 0.8 compare_and_fusion.1
  8.8 0.8 fusion.44
  10.5 0.8 scatter_custom_fusion
  12.0 12.1 %all-to-all-start = ((s32[64,1,1]{2,1,0:T(1,128)}), s32[64,1,1]{2,1,0:T(1,128)S(1)}, u32[]{:S(2)}, u32[]{:S(2)}) async-start(s32[64,1,1]{2,1,0:T(1,128)} %copy.80), calls=%async_computation | async-start | bytes 65536 | tf_op jit(solution)/shard_map/all_to_all | solution.py:65
  24.1 1.1 pad_maximum_fusion.5
  25.6 7.1 %all-to-all-done = s32[64,1,1]{2,1,0:T(1,128)S(1)} async-done(((s32[64,1,1]{2,1,0:T(1,128)}), s32[64,1,1]{2,1,0:T(1,128)S(1)}, u32[]{:S(2)}, u32[]{:S(2)}) %all-to-all-start) | async-done | bytes 288 | tf_op jit(solution)/shard_map/all_to_all | solution.py:65
  32.7 2.7 %fusion.69 = (s32[64]{0:T(128)}, s32[64]{0:T(128)S(1)}) fusion(s32[64,1,1]{2,1,0:T(1,128)S(1)} %all-to-all-done), kind=kLoop, calls=%fused_computation.160 | loop fusion | flops 64 | bytes 768 | tf_op jit(solution)/shard_map/all_to_all | solution.py:65
  35.4 0.7 gather_fusion
  36.1 1.0 fusion.73
  37.2 5.5 %all-to-all-start.2 = ((bf16[64,1,32,128]{3,2,1,0:T(8,128)(2,1)}), bf16[64,1,32,128]{3,2,1,0:T(8,128)(2,1)S(1)}, u32[]{:S(2)}, u32[]{:S(2)}) async-start(bf16[64,1,32,128]{3,2,1,0:T(8,128)(2,1)} %get-tuple-element.19), calls=%async_computation.2 | async-start | bytes 1048576 | tf_op jit(solution)/shard_map/all_to_all | solution.py:90
  43.6 16.7 %all-to-all-done.2 = bf16[64,1,32,128]{3,2,1,0:T(8,128)(2,1)S(1)} async-done(((bf16[64,1,32,128]{3,2,1,0:T(8,128)(2,1)}), bf16[64,1,32,128]{3,2,1,0:T(8,128)(2,1)S(1)}, u32[]{:S(2)}, u32[]{:S(2)}) %all-to-all-start.2) | async-done | bytes 524320 | tf_op jit(solution)/shard_map/all_to_all | solution.py:90
  60.3 5.8 %all-to-all-start.1 = ((bf16[64,1,32,128]{3,2,1,0:T(8,128)(2,1)}), bf16[64,1,32,128]{3,2,1,0:T(8,128)(2,1)S(1)}, u32[]{:S(2)}, u32[]{:S(2)}) async-start(bf16[64,1,32,128]{3,2,1,0:T(8,128)(2,1)} %get-tuple-element.18), calls=%async_computation.1 | async-start | bytes 1048576 | tf_op jit(solution)/shard_map/all_to_all | solution.py:90
  66.2 1.2 scatter_custom_fusion.1
  68.7 1.3 pad_maximum_fusion.2
  72.1 1.1 copy.90
  73.8 0.8 gather_fusion.5
  75.3 2.4 %collective-permute-start.5 = (bf16[14,32,128]{2,1,0:T(8,128)(2,1)}, bf16[14,32,128]{2,1,0:T(8,128)(2,1)S(1)}, u32[]{:S(2)}, u32[]{:S(2)}) collective-permute-start(bf16[14,32,128]{2,1,0:T(8,128)(2,1)} %get-tuple-element.35), channel_id=1, source_target_pairs={{0,3},{1,0},{2,1},{3,2},{4,7},{5,4},{6,5},{7,6},{8,11},{9,8},{10,9... | collective-permute-start | bytes 344072 | tf_op jit(solution)/shard_map/ppermute | solution.py:41
  77.6 1.5 collective-permute-start.4
  79.1 4.6 %all-to-all-done.1 = bf16[64,1,32,128]{3,2,1,0:T(8,128)(2,1)S(1)} async-done(((bf16[64,1,32,128]{3,2,1,0:T(8,128)(2,1)}), bf16[64,1,32,128]{3,2,1,0:T(8,128)(2,1)S(1)}, u32[]{:S(2)}, u32[]{:S(2)}) %all-to-all-start.1) | async-done | bytes 524320 | tf_op jit(solution)/shard_map/all_to_all | solution.py:90
  84.4 0.8 gather_fusion.2
  85.2 2.4 %collective-permute-start.2 = (bf16[14,32,128]{2,1,0:T(8,128)(2,1)S(1)}, bf16[14,32,128]{2,1,0:T(8,128)(2,1)S(1)}, u32[]{:S(2)}, u32[]{:S(2)}) collective-permute-start(bf16[14,32,128]{2,1,0:T(8,128)(2,1)S(1)} %get-tuple-element.31), channel_id=1, source_target_pairs={{0,3},{1,0},{2,1},{3,2},{4,7},{5,4},{6,5},{7,6},{8,11},{9,8},{10,9... | collective-permute-start | bytes 344072 | tf_op jit(solution)/shard_map/ppermute | solution.py:41
  87.6 1.5 collective-permute-start.1
  89.8 1.1 pad_maximum_fusion.8
  90.9 0.8 gather_fusion.6
  91.7 1.0 collective-permute-done.2
  92.7 2.4 %collective-permute-done.1 = bf16[14,32,128]{2,1,0:T(8,128)(2,1)S(1)} collective-permute-done((bf16[14,32,128]{2,1,0:T(8,128)(2,1)S(1)}, bf16[14,32,128]{2,1,0:T(8,128)(2,1)S(1)}, u32[]{:S(2)}, u32[]{:S(2)}) %collective-permute-start.1) | collective-permute-done | bytes 114720 | tf_op jit(solution)/shard_map/ppermute | solution.py:41
  95.1 1.2 collective-permute-done
  96.4 0.8 gather_fusion.3
  97.4 1.3 fusion.5
  98.8 1.8 fusion.2
  100.6 2.9 %multiply_reduce_fusion = (f32[2,128,8]{1,2,0:T(8,128)S(1)}, bf16[2,128,8,128]{1,3,2,0:T(8,128)(2,1)}) fusion(bf16[2,128,8,128]{1,3,2,0:T(8,128)(2,1)S(1)} %copy-done.5, f32[2,128,8]{1,2,0:T(8,128)S(1)} %bitcast.256, f32[2,8,128,128,8]{3,2,4,1,0:T(8,128)S(1)} %get-tuple-element.42, f32[2,8,128]{2,1,0:T(8,128)S(1)} %get-tuple-element.41, ...), kind=kOutput, calls=%fused_computation.51 | convolution fusion | flops 547878912 | bytes 10772480 | tf_op jit(solution)/shard_map/qhisj,qsjd->qihd/dot_general | solution.py:124
  103.5 2.0 %fusion.16 = f32[2,8,1,128,128]{4,3,1,0,2:T(8,128)S(1)} fusion(f32[2,8,128,128,8]{3,2,4,1,0:T(8,128)S(1)} %get-tuple-element.42, f32[2,8,128]{2,1,0:T(8,128)S(1)} %log_add_fusion, pred[2,128,8,128]{1,3,2,0:T(8,128)(4,1)S(1)} %compare_and_fusion, bf16[2,128,8,128,1]{3,2,1,0,4:T(8,128)(2,1)S(1)} %bitcast.219), kind=kOutput, calls=%fused_computation.36 | convolution fusion | flops 545259520 | bytes 10231808 | tf_op jit(solution)/shard_map/qhisj,qihd->qsjd/dot_general | solution.py:150
  105.5 2.8 %fusion.1 = bf16[2,8,128,8,128]{2,4,1,3,0:T(8,128)(2,1)S(1)} fusion(f32[2,8,128,128,8]{3,2,4,1,0:T(8,128)S(1)} %get-tuple-element.42, f32[2,8,128]{2,1,0:T(8,128)S(1)} %bitcast.257, f32[2,8,128]{2,1,0:T(8,128)S(1)} %log_add_fusion, pred[2,128,8,128]{1,3,2,0:T(8,128)(4,1)S(1)} %compare_and_fusion, bf16[2,128,8,128,1]{3,2,1,0,4:T(8,128)(2,1)S(1)} %bitcast.220, ...), kind=kOutput, calls=%fused_computation.19 | convolution fusion | flops 550502400 | bytes 14434304 | tf_op jit(solution)/shard_map/qihd,qsjd->qhisj/dot_general | solution.py:136
  108.4 1.3 fusion.21
  110.4 0.8 gather_fusion.11
  111.9 1.5 collective-permute-start.13
  113.5 0.9 collective-permute-start.12
  114.9 4.9 %collective-permute-done.14 = bf16[14,64,128]{2,1,0:T(8,128)(2,1)S(1)} collective-permute-done((bf16[14,64,128]{2,1,0:T(8,128)(2,1)S(1)}, bf16[14,64,128]{2,1,0:T(8,128)(2,1)S(1)}, u32[]{:S(2)}, u32[]{:S(2)}) %collective-permute-start.14) | collective-permute-done | bytes 229408 | tf_op jit(solution)/shard_map/ppermute | solution.py:41
  119.9 2.1 %collective-permute-done.13 = bf16[14,64,128]{2,1,0:T(8,128)(2,1)S(1)} collective-permute-done((bf16[14,64,128]{2,1,0:T(8,128)(2,1)S(1)}, bf16[14,64,128]{2,1,0:T(8,128)(2,1)S(1)}, u32[]{:S(2)}, u32[]{:S(2)}) %collective-permute-start.13) | collective-permute-done | bytes 229408 | tf_op jit(solution)/shard_map/ppermute | solution.py:41
  121.9 3.0 %collective-permute-done.12 = bf16[14,64,128]{2,1,0:T(8,128)(2,1)S(1)} collective-permute-done((bf16[14,64,128]{2,1,0:T(8,128)(2,1)S(1)}, bf16[14,64,128]{2,1,0:T(8,128)(2,1)S(1)}, u32[]{:S(2)}, u32[]{:S(2)}) %collective-permute-start.12) | collective-permute-done | bytes 229408 | tf_op jit(solution)/shard_map/ppermute | solution.py:41
  125.0 1.0 gather_fusion.12
  126.1 1.8 gather_fusion.13
  127.9 5.9 %all-to-all-start.3 = ((bf16[64,1,64,128]{3,2,1,0:T(8,128)(2,1)}), bf16[64,1,64,128]{3,2,1,0:T(8,128)(2,1)}, u32[]{:S(2)}, u32[]{:S(2)}) async-start(bf16[64,1,64,128]{3,2,1,0:T(8,128)(2,1)} %bitcast.86), calls=%async_computation.3 | async-start | bytes 2097152 | tf_op jit(solution)/shard_map/all_to_all | solution.py:168
  133.8 3.1 %fusion.23 = bf16[2,128,8,128]{1,3,2,0:T(8,128)(2,1)S(1)} fusion(bf16[2,8,128,8,128]{2,4,1,3,0:T(8,128)(2,1)} %copy-done.1, bf16[2,1,2,128,128]{4,3,1,0,2:T(8,128)(2,1)S(1)} %copy_bitcast_fusion, bf16[2,7,2,128,128]{4,3,2,1,0:T(8,128)(2,1)} %bitcast.236), kind=kOutput, calls=%fused_computation.43 | convolution fusion | flops 538443776 | bytes 5767168 | tf_op jit(solution)/shard_map/qhisj,qsjd->qihd/dot_general | solution.py:143
  137.6 0.9 copy.95
  139.2 1.1 maximum_bitcast_fusion
  141.2 1.1 collective-permute-start.11
  142.3 1.4 collective-permute-start.10
  144.4 6.0 %collective-permute-done.11 = bf16[2,256,256]{2,1,0:T(8,128)(2,1)S(1)} collective-permute-done((bf16[2,256,256]{2,1,0:T(8,128)(2,1)S(1)}, bf16[2,256,256]{2,1,0:T(8,128)(2,1)S(1)}, u32[]{:S(2)}, u32[]{:S(2)}) %collective-permute-start.11) | collective-permute-done | bytes 262176 | tf_op jit(solution)/shard_map/ppermute | solution.py:41
  150.4 2.6 %collective-permute-done.10 = bf16[2,256,256]{2,1,0:T(8,128)(2,1)S(1)} collective-permute-done((bf16[2,256,256]{2,1,0:T(8,128)(2,1)S(1)}, bf16[2,256,256]{2,1,0:T(8,128)(2,1)S(1)}, u32[]{:S(2)}, u32[]{:S(2)}) %collective-permute-start.10) | collective-permute-done | bytes 262176 | tf_op jit(solution)/shard_map/ppermute | solution.py:41
  153.1 4.4 %collective-permute-done.9 = bf16[2,256,256]{2,1,0:T(8,128)(2,1)S(1)} collective-permute-done((bf16[2,256,256]{2,1,0:T(8,128)(2,1)S(1)}, bf16[2,256,256]{2,1,0:T(8,128)(2,1)S(1)}, u32[]{:S(2)}, u32[]{:S(2)}) %collective-permute-start.9) | collective-permute-done | bytes 262176 | tf_op jit(solution)/shard_map/ppermute | solution.py:41
  157.6 1.8 gather_fusion.10
  159.4 3.1 %all-to-all-done.3 = bf16[64,1,64,128]{3,2,1,0:T(8,128)(2,1)} async-done(((bf16[64,1,64,128]{3,2,1,0:T(8,128)(2,1)}), bf16[64,1,64,128]{3,2,1,0:T(8,128)(2,1)}, u32[]{:S(2)}, u32[]{:S(2)}) %all-to-all-start.3) | async-done | bytes 1048608 | tf_op jit(solution)/shard_map/all_to_all | solution.py:168
  162.5 1.5 bitcast_convert_fusion
  164.0 3.8 %scatter_fusion = f32[9,64,128]{2,1,0:T(8,128)S(1)} fusion(f32[9,64,128]{2,1,0:T(8,128)S(1)} %broadcast_in_dim.30, s32[64]{0:T(128)S(1)} %fusion.56, f32[64,64,128]{2,1,0:T(8,128)S(1)} %bitcast_convert_fusion), kind=kCustom, calls=%fused_computation.16 | custom fusion | flops 524288 | bytes 6291712 | tf_op jit(solution)/shard_map/scatter-add | solution.py:179
  168.5 3.4 %all-to-all-start.4 = ((f32[4,2,64,128]{3,2,1,0:T(8,128)}), f32[4,2,64,128]{3,2,1,0:T(8,128)S(1)}, u32[]{:S(2)}, u32[]{:S(2)}) async-start(f32[4,2,64,128]{3,2,1,0:T(8,128)} %bitcast.89), calls=%async_computation.4 | async-start | bytes 524288 | tf_op jit(solution)/shard_map/all_to_all | solution.py:181
  171.9 2.2 %fusion.70 = (bf16[4,1,256,256]{3,2,1,0:T(8,128)(2,1)}, bf16[4,1,256,256]{3,2,1,0:T(8,128)(2,1)}) fusion(bf16[4,2,256,256]{3,2,1,0:T(8,128)(2,1)} %gather_fusion.10), kind=kLoop, calls=%fused_computation.161 | loop fusion | bytes 2097152 | tf_op jit(solution)/shard_map/slice | solution.py:194
  174.1 4.4 %all-to-all-done.4 = f32[4,2,64,128]{3,2,1,0:T(8,128)S(1)} async-done(((f32[4,2,64,128]{3,2,1,0:T(8,128)}), f32[4,2,64,128]{3,2,1,0:T(8,128)S(1)}, u32[]{:S(2)}, u32[]{:S(2)}) %all-to-all-start.4) | async-done | bytes 262176 | tf_op jit(solution)/shard_map/all_to_all | solution.py:181
  178.6 1.0 fusion.37
  (110 shorter events, 16.3 us)
Async XLA Ops:
  0.6 42.2 %copy-start.10 = (s32[8,8]{1,0:T(8,128)S(1)}, s32[8,8]{1,0:T(8,128)}, u32[]{:S(2)}) copy-start(s32[8,8]{1,0:T(8,128)} %param.9) | copy-start | bytes 772
  0.6 42.8 %copy-start.2 = (bf16[1024,128]{1,0:T(8,128)(2,1)S(1)}, bf16[1024,128]{1,0:T(8,128)(2,1)}, u32[]{:S(2)}) copy-start(bf16[1024,128]{1,0:T(8,128)(2,1)} %param.6) | copy-start | bytes 786436
  0.7 42.8 %copy-start.3 = (bf16[1024,128]{1,0:T(8,128)(2,1)S(1)}, bf16[1024,128]{1,0:T(8,128)(2,1)}, u32[]{:S(2)}) copy-start(bf16[1024,128]{1,0:T(8,128)(2,1)} %param.7) | copy-start | bytes 786436
  0.7 7.3 %copy-start.11 = (s32[1024]{0:T(1024)}, s32[1024]{0:T(1024)S(1)}, u32[]{:S(2)}) copy-start(s32[1024]{0:T(1024)S(1)} %pad_clamp_fusion.2) | copy-start | bytes 12292
  3.6 64.4 %collective-permute-start.8 = (bf16[2,256,256]{2,1,0:T(8,128)(2,1)}, bf16[2,256,256]{2,1,0:T(8,128)(2,1)S(1)}, u32[]{:S(2)}, u32[]{:S(2)}) collective-permute-start(bf16[2,256,256]{2,1,0:T(8,128)(2,1)} %get-tuple-element.23), channel_id=1, source_target_pairs={{0,3},{1,0},{2,1},{3,2},{4,7},{5,4},{6,5},{7,6},{8,11},{9,8},{10,9... | collective-permute-start | bytes 786440 | tf_op jit(solution)/shard_map/ppermute | solution.py:41
  6.3 61.7 %collective-permute-start.7 = (bf16[2,256,256]{2,1,0:T(8,128)(2,1)S(1)}, bf16[2,256,256]{2,1,0:T(8,128)(2,1)}, u32[]{:S(2)}, u32[]{:S(2)}) collective-permute-start(bf16[2,256,256]{2,1,0:T(8,128)(2,1)S(1)} %get-tuple-element.21), channel_id=1, source_target_pairs={{0,2},{1,3},{2,0},{3,1},{4,6},{5,7},{6,4},{7,5},{8,10},{9,11},{10,... | collective-permute-start | bytes 786440 | tf_op jit(solution)/shard_map/ppermute | solution.py:41
  7.1 60.9 %collective-permute-start.6 = (bf16[2,256,256]{2,1,0:T(8,128)(2,1)S(1)}, bf16[2,256,256]{2,1,0:T(8,128)(2,1)}, u32[]{:S(2)}, u32[]{:S(2)}) collective-permute-start(bf16[2,256,256]{2,1,0:T(8,128)(2,1)S(1)} %get-tuple-element.22), channel_id=1, source_target_pairs={{0,1},{1,2},{2,3},{3,0},{4,5},{5,6},{6,7},{7,4},{8,9},{9,10},{10,1... | collective-permute-start | bytes 786440 | tf_op jit(solution)/shard_map/ppermute | solution.py:41
  12.0 20.7 %all-to-all-start = ((s32[64,1,1]{2,1,0:T(1,128)}), s32[64,1,1]{2,1,0:T(1,128)S(1)}, u32[]{:S(2)}, u32[]{:S(2)}) async-start(s32[64,1,1]{2,1,0:T(1,128)} %copy.80), calls=%async_computation | async-start | bytes 65536 | tf_op jit(solution)/shard_map/all_to_all | solution.py:65
  37.2 23.2 %all-to-all-start.2 = ((bf16[64,1,32,128]{3,2,1,0:T(8,128)(2,1)}), bf16[64,1,32,128]{3,2,1,0:T(8,128)(2,1)S(1)}, u32[]{:S(2)}, u32[]{:S(2)}) async-start(bf16[64,1,32,128]{3,2,1,0:T(8,128)(2,1)} %get-tuple-element.19), calls=%async_computation.2 | async-start | bytes 1048576 | tf_op jit(solution)/shard_map/all_to_all | solution.py:90
  60.3 23.4 %all-to-all-start.1 = ((bf16[64,1,32,128]{3,2,1,0:T(8,128)(2,1)}), bf16[64,1,32,128]{3,2,1,0:T(8,128)(2,1)S(1)}, u32[]{:S(2)}, u32[]{:S(2)}) async-start(bf16[64,1,32,128]{3,2,1,0:T(8,128)(2,1)} %get-tuple-element.18), calls=%async_computation.1 | async-start | bytes 1048576 | tf_op jit(solution)/shard_map/all_to_all | solution.py:90
  68.0 0.7 copy-start.7
  75.3 13.9 %collective-permute-start.5 = (bf16[14,32,128]{2,1,0:T(8,128)(2,1)}, bf16[14,32,128]{2,1,0:T(8,128)(2,1)S(1)}, u32[]{:S(2)}, u32[]{:S(2)}) collective-permute-start(bf16[14,32,128]{2,1,0:T(8,128)(2,1)} %get-tuple-element.35), channel_id=1, source_target_pairs={{0,3},{1,0},{2,1},{3,2},{4,7},{5,4},{6,5},{7,6},{8,11},{9,8},{10,9... | collective-permute-start | bytes 344072 | tf_op jit(solution)/shard_map/ppermute | solution.py:41
  77.6 11.5 %collective-permute-start.4 = (bf16[14,32,128]{2,1,0:T(8,128)(2,1)S(1)}, bf16[14,32,128]{2,1,0:T(8,128)(2,1)S(1)}, u32[]{:S(2)}, u32[]{:S(2)}) collective-permute-start(bf16[14,32,128]{2,1,0:T(8,128)(2,1)S(1)} %get-tuple-element.33), channel_id=1, source_target_pairs={{0,2},{1,3},{2,0},{3,1},{4,6},{5,7},{6,4},{7,5},{8,10},{9,11},{10,... | collective-permute-start | bytes 344072 | tf_op jit(solution)/shard_map/ppermute | solution.py:41
  79.1 10.0 %collective-permute-start.3 = (bf16[14,32,128]{2,1,0:T(8,128)(2,1)S(1)}, bf16[14,32,128]{2,1,0:T(8,128)(2,1)}, u32[]{:S(2)}, u32[]{:S(2)}) collective-permute-start(bf16[14,32,128]{2,1,0:T(8,128)(2,1)S(1)} %get-tuple-element.34), channel_id=1, source_target_pairs={{0,1},{1,2},{2,3},{3,0},{4,5},{5,6},{6,7},{7,4},{8,9},{9,10},{10,1... | collective-permute-start | bytes 344072 | tf_op jit(solution)/shard_map/ppermute | solution.py:41
  85.2 7.5 %collective-permute-start.2 = (bf16[14,32,128]{2,1,0:T(8,128)(2,1)S(1)}, bf16[14,32,128]{2,1,0:T(8,128)(2,1)S(1)}, u32[]{:S(2)}, u32[]{:S(2)}) collective-permute-start(bf16[14,32,128]{2,1,0:T(8,128)(2,1)S(1)} %get-tuple-element.31), channel_id=1, source_target_pairs={{0,3},{1,0},{2,1},{3,2},{4,7},{5,4},{6,5},{7,6},{8,11},{9,8},{10,9... | collective-permute-start | bytes 344072 | tf_op jit(solution)/shard_map/ppermute | solution.py:41
  87.6 7.5 %collective-permute-start.1 = (bf16[14,32,128]{2,1,0:T(8,128)(2,1)S(1)}, bf16[14,32,128]{2,1,0:T(8,128)(2,1)S(1)}, u32[]{:S(2)}, u32[]{:S(2)}) collective-permute-start(bf16[14,32,128]{2,1,0:T(8,128)(2,1)S(1)} %get-tuple-element.29), channel_id=1, source_target_pairs={{0,2},{1,3},{2,0},{3,1},{4,6},{5,7},{6,4},{7,5},{8,10},{9,11},{10,... | collective-permute-start | bytes 344072 | tf_op jit(solution)/shard_map/ppermute | solution.py:41
  89.1 0.6 copy-start.8
  89.1 7.2 %collective-permute-start = (bf16[14,32,128]{2,1,0:T(8,128)(2,1)S(1)}, bf16[14,32,128]{2,1,0:T(8,128)(2,1)S(1)}, u32[]{:S(2)}, u32[]{:S(2)}) collective-permute-start(bf16[14,32,128]{2,1,0:T(8,128)(2,1)S(1)} %get-tuple-element.30), channel_id=1, source_target_pairs={{0,1},{1,2},{2,3},{3,0},{4,5},{5,6},{6,7},{7,4},{8,9},{9,10},{10,1... | collective-permute-start | bytes 344072 | tf_op jit(solution)/shard_map/ppermute | solution.py:41
  89.2 0.7 copy-start.9
  97.4 8.1 %copy-start.4 = (bf16[14,4,64,128]{3,2,1,0:T(8,128)(2,1)}, bf16[14,4,64,128]{3,2,1,0:T(8,128)(2,1)S(1)}, u32[]{:S(2)}) copy-start(bf16[14,4,64,128]{3,2,1,0:T(8,128)(2,1)S(1)} %copy.81) | copy-start | bytes 2752516
  97.4 3.2 %copy-start.5 = (bf16[2,128,8,128]{1,3,2,0:T(8,128)(2,1)S(1)}, bf16[2,128,8,128]{1,3,2,0:T(8,128)(2,1)}, u32[]{:S(2)}) copy-start(bf16[2,128,8,128]{1,3,2,0:T(8,128)(2,1)} %copy.90) | copy-start | bytes 1572868
  105.5 4.1 %copy-start = (f32[2,8,1,128,128]{4,3,1,0,2:T(8,128)}, f32[2,8,1,128,128]{4,3,1,0,2:T(8,128)S(1)}, u32[]{:S(2)}) copy-start(f32[2,8,1,128,128]{4,3,1,0,2:T(8,128)S(1)} %fusion.16) | copy-start | bytes 3145732
  108.4 1.9 %copy-start.1 = (bf16[2,8,128,8,128]{2,4,1,3,0:T(8,128)(2,1)}, bf16[2,8,128,8,128]{2,4,1,3,0:T(8,128)(2,1)S(1)}, u32[]{:S(2)}) copy-start(bf16[2,8,128,8,128]{2,4,1,3,0:T(8,128)(2,1)S(1)} %fusion.1) | copy-start | bytes 12582916
  108.4 6.0 %copy-start.13 = (s32[65]{0:T(128)S(1)}, s32[65]{0:T(128)}, u32[]{:S(2)}) copy-start(s32[65]{0:T(128)} %scatter_custom_fusion.1) | copy-start | bytes 784
  111.3 8.6 %collective-permute-start.14 = (bf16[14,64,128]{2,1,0:T(8,128)(2,1)S(1)}, bf16[14,64,128]{2,1,0:T(8,128)(2,1)S(1)}, u32[]{:S(2)}, u32[]{:S(2)}) collective-permute-start(bf16[14,64,128]{2,1,0:T(8,128)(2,1)S(1)} %get-tuple-element.27), channel_id=1, source_target_pairs={{0,3},{1,0},{2,1},{3,2},{4,7},{5,4},{6,5},{7,6},{8,11},{9,8},{10,9... | collective-permute-start | bytes 688136 | tf_op jit(solution)/shard_map/ppermute | solution.py:41
  111.9 10.0 %collective-permute-start.13 = (bf16[14,64,128]{2,1,0:T(8,128)(2,1)S(1)}, bf16[14,64,128]{2,1,0:T(8,128)(2,1)S(1)}, u32[]{:S(2)}, u32[]{:S(2)}) collective-permute-start(bf16[14,64,128]{2,1,0:T(8,128)(2,1)S(1)} %get-tuple-element.25), channel_id=1, source_target_pairs={{0,2},{1,3},{2,0},{3,1},{4,6},{5,7},{6,4},{7,5},{8,10},{9,11},{10,... | collective-permute-start | bytes 688136 | tf_op jit(solution)/shard_map/ppermute | solution.py:41
  113.5 11.4 %collective-permute-start.12 = (bf16[14,64,128]{2,1,0:T(8,128)(2,1)S(1)}, bf16[14,64,128]{2,1,0:T(8,128)(2,1)S(1)}, u32[]{:S(2)}, u32[]{:S(2)}) collective-permute-start(bf16[14,64,128]{2,1,0:T(8,128)(2,1)S(1)} %get-tuple-element.26), channel_id=1, source_target_pairs={{0,1},{1,2},{2,3},{3,0},{4,5},{5,6},{6,7},{7,4},{8,9},{9,10},{10,1... | collective-permute-start | bytes 688136 | tf_op jit(solution)/shard_map/ppermute | solution.py:41
  125.0 13.4 %copy-start.6 = (bf16[2,128,8,128]{1,3,2,0:T(8,128)(2,1)S(1)}, bf16[2,128,8,128]{1,3,2,0:T(8,128)(2,1)}, u32[]{:S(2)}) copy-start(bf16[2,128,8,128]{1,3,2,0:T(8,128)(2,1)} %get-tuple-element.44) | copy-start | bytes 1572868
  127.9 34.6 %all-to-all-start.3 = ((bf16[64,1,64,128]{3,2,1,0:T(8,128)(2,1)}), bf16[64,1,64,128]{3,2,1,0:T(8,128)(2,1)}, u32[]{:S(2)}, u32[]{:S(2)}) async-start(bf16[64,1,64,128]{3,2,1,0:T(8,128)(2,1)} %bitcast.86), calls=%async_computation.3 | async-start | bytes 2097152 | tf_op jit(solution)/shard_map/all_to_all | solution.py:168
  136.9 7.5 %copy-start.12 = (s32[64]{0:T(128)S(1)}, s32[64]{0:T(128)}, u32[]{:S(2)}) copy-start(s32[64]{0:T(128)} %get-tuple-element.4) | copy-start | bytes 772
  141.2 9.3 %collective-permute-start.11 = (bf16[2,256,256]{2,1,0:T(8,128)(2,1)S(1)}, bf16[2,256,256]{2,1,0:T(8,128)(2,1)S(1)}, u32[]{:S(2)}, u32[]{:S(2)}) collective-permute-start(bf16[2,256,256]{2,1,0:T(8,128)(2,1)S(1)} %get-tuple-element.15), channel_id=1, source_target_pairs={{0,3},{1,0},{2,1},{3,2},{4,7},{5,4},{6,5},{7,6},{8,11},{9,8},{10,9... | collective-permute-start | bytes 786440 | tf_op jit(solution)/shard_map/ppermute | solution.py:41
  142.3 10.7 %collective-permute-start.10 = (bf16[2,256,256]{2,1,0:T(8,128)(2,1)S(1)}, bf16[2,256,256]{2,1,0:T(8,128)(2,1)S(1)}, u32[]{:S(2)}, u32[]{:S(2)}) collective-permute-start(bf16[2,256,256]{2,1,0:T(8,128)(2,1)S(1)} %get-tuple-element.13), channel_id=1, source_target_pairs={{0,2},{1,3},{2,0},{3,1},{4,6},{5,7},{6,4},{7,5},{8,10},{9,11},{10,... | collective-permute-start | bytes 786440 | tf_op jit(solution)/shard_map/ppermute | solution.py:41
  143.7 13.8 %collective-permute-start.9 = (bf16[2,256,256]{2,1,0:T(8,128)(2,1)S(1)}, bf16[2,256,256]{2,1,0:T(8,128)(2,1)S(1)}, u32[]{:S(2)}, u32[]{:S(2)}) collective-permute-start(bf16[2,256,256]{2,1,0:T(8,128)(2,1)S(1)} %get-tuple-element.14), channel_id=1, source_target_pairs={{0,1},{1,2},{2,3},{3,0},{4,5},{5,6},{6,7},{7,4},{8,9},{9,10},{10,1... | collective-permute-start | bytes 786440 | tf_op jit(solution)/shard_map/ppermute | solution.py:41
  168.5 10.1 %all-to-all-start.4 = ((f32[4,2,64,128]{3,2,1,0:T(8,128)}), f32[4,2,64,128]{3,2,1,0:T(8,128)S(1)}, u32[]{:S(2)}, u32[]{:S(2)}) async-start(f32[4,2,64,128]{3,2,1,0:T(8,128)} %bitcast.89), calls=%async_computation.4 | async-start | bytes 524288 | tf_op jit(solution)/shard_map/all_to_all | solution.py:181

commit v4 on v0

--- a/solution.py
+++ b/solution.py
@@ -126,8 +126,7 @@
     attended = (summed / jnp.transpose(row_total[..., 0, 0], (0, 2, 1))[..., None]).astype(
         jnp.bfloat16
     )
-    log_total = row_max + jnp.log(row_total)
-    probability = jnp.exp(scores - log_total)
+    probability = weights * (1.0 / row_total)
     row_delta = jnp.sum(g_blocks.astype(jnp.float32) * attended.astype(jnp.float32), axis=3)
     grad_p = jnp.einsum(
         "qihd,qsjd->qhisj", g_blocks, value_tile, preferred_element_type=jnp.float32

time: 167 us -> 168 us (level)
  no operation moved by 1% of the time
where the time goes in v4:
time: 168 us; the launch traced here: 167 us
  waiting for transfers between devices  64.1 us (38%)
  starting transfers between devices  40.1 us (24%)
  local copies, waits for them, and re-layouts  26.3 us (16%)
  other arithmetic  21.5 us (13%)
  matrix products  14 us (8%)
    ppermute x15, waiting for transfers between devices, head_exchange(): lax.ppermute(ahead[k], 'head', [(j, (j + k) % count) for j in range(count)])  47.5 us
    ppermute x15, starting transfers between devices, head_exchange(): lax.ppermute(ahead[k], 'head', [(j, (j + k) % count) for j in range(count)])  15.8 us
    all_to_all x1, starting transfers between devices, on_device(): lax.all_to_all(req_table.reshape(pair_count, capacity), 'ctx', split_axis...  12.1 us
    all_to_all x1, waiting for transfers between devices, on_device(): lax.all_to_all(send_parts, 'ctx', split_axis=0, concat_axis=0, tiled=True)  7.99 us
    all_to_all x1, starting transfers between devices, on_device(): lax.all_to_all(outgoing_part.reshape(pair_count, capacity, part_rows, HD)...  6.64 us
    all_to_all x1, starting transfers between devices, on_device(): lax.all_to_all(send_parts, 'ctx', split_axis=0, concat_axis=0, tiled=True)  5.55 us
    all_to_all x1, waiting for transfers between devices, on_device(): lax.all_to_all(req_table.reshape(pair_count, capacity), 'ctx', split_axis...  5.47 us
    gather x5, local copies, waits for them, and re-layouts, head_exchange(): return jnp.stack(got)[order]  4.98 us
  transfers between devices with their start and end apart: 18, of which 16 were waited for; matrix products, arithmetic and copies ran while one was open for 14% of the time, Pallas kernels for 0%

profile of v4, /device:TPU:8, one launch (start us, length us, event | category | flops | bytes accessed | tf_op | source)
XLA Modules:
  0.0 167.2 jit_solution(17492077352594018672)
XLA Ops:
  0.7 0.8 compare_and_fusion.1
  1.5 0.8 fusion.38
  3.3 0.8 scatter_custom_fusion
  4.7 12.1 %all-to-all-start = ((s32[64,1,1]{2,1,0:T(1,128)}), s32[64,1,1]{2,1,0:T(1,128)S(1)}, u32[]{:S(2)}, u32[]{:S(2)}) async-start(s32[64,1,1]{2,1,0:T(1,128)} %copy.79), calls=%async_computation | async-start | bytes 65536 | tf_op jit(solution)/shard_map/all_to_all | solution.py:65
  16.9 1.3 pad_maximum_fusion.1
  18.2 1.1 pad_maximum_fusion.6
  19.9 5.5 %all-to-all-done = s32[64,1,1]{2,1,0:T(1,128)S(1)} async-done(((s32[64,1,1]{2,1,0:T(1,128)}), s32[64,1,1]{2,1,0:T(1,128)S(1)}, u32[]{:S(2)}, u32[]{:S(2)}) %all-to-all-start) | async-done | bytes 288 | tf_op jit(solution)/shard_map/all_to_all | solution.py:65
  25.4 2.8 %fusion.63 = (s32[64]{0:T(128)}, s32[64]{0:T(128)S(1)}) fusion(s32[64,1,1]{2,1,0:T(1,128)S(1)} %all-to-all-done), kind=kLoop, calls=%fused_computation.156 | loop fusion | flops 64 | bytes 768 | tf_op jit(solution)/shard_map/all_to_all | solution.py:65
  28.2 1.7 gather_fusion
  29.8 5.5 %all-to-all-start.1 = ((bf16[64,1,64,128]{3,2,1,0:T(8,128)(2,1)}), bf16[64,1,64,128]{3,2,1,0:T(8,128)(2,1)S(1)}, u32[]{:S(2)}, u32[]{:S(2)}) async-start(bf16[64,1,64,128]{3,2,1,0:T(8,128)(2,1)} %bitcast.8), calls=%async_computation.1 | async-start | bytes 2097152 | tf_op jit(solution)/shard_map/all_to_all | solution.py:85
  35.4 0.9 fusion.67
  36.3 2.8 %collective-permute-start.5 = (bf16[2,256,256]{2,1,0:T(8,128)(2,1)}, bf16[2,256,256]{2,1,0:T(8,128)(2,1)S(1)}, u32[]{:S(2)}, u32[]{:S(2)}) collective-permute-start(bf16[2,256,256]{2,1,0:T(8,128)(2,1)} %get-tuple-element.21), channel_id=1, source_target_pairs={{0,3},{1,0},{2,1},{3,2},{4,7},{5,4},{6,5},{7,6},{8,11},{9,8},{10,9... | collective-permute-start | bytes 786440 | tf_op jit(solution)/shard_map/ppermute | solution.py:41
  39.1 0.8 collective-permute-start.4
  39.9 0.9 collective-permute-start.3
  42.6 0.7 scatter_custom_fusion.1
  43.8 7.0 %collective-permute-done.5 = bf16[2,256,256]{2,1,0:T(8,128)(2,1)S(1)} collective-permute-done((bf16[2,256,256]{2,1,0:T(8,128)(2,1)}, bf16[2,256,256]{2,1,0:T(8,128)(2,1)S(1)}, u32[]{:S(2)}, u32[]{:S(2)}) %collective-permute-start.5) | collective-permute-done | bytes 262176 | tf_op jit(solution)/shard_map/ppermute | solution.py:41
  50.9 3.6 %collective-permute-done.3 = bf16[2,256,256]{2,1,0:T(8,128)(2,1)S(1)} collective-permute-done((bf16[2,256,256]{2,1,0:T(8,128)(2,1)S(1)}, bf16[2,256,256]{2,1,0:T(8,128)(2,1)S(1)}, u32[]{:S(2)}, u32[]{:S(2)}) %collective-permute-start.3) | collective-permute-done | bytes 262176 | tf_op jit(solution)/shard_map/ppermute | solution.py:41
  54.4 1.1 pad_maximum_fusion.2
  55.5 0.7 gather_fusion.5
  56.3 8.0 %all-to-all-done.1 = bf16[64,1,64,128]{3,2,1,0:T(8,128)(2,1)S(1)} async-done(((bf16[64,1,64,128]{3,2,1,0:T(8,128)(2,1)}), bf16[64,1,64,128]{3,2,1,0:T(8,128)(2,1)S(1)}, u32[]{:S(2)}, u32[]{:S(2)}) %all-to-all-start.1) | async-done | bytes 1048608 | tf_op jit(solution)/shard_map/all_to_all | solution.py:85
  64.3 0.8 gather_fusion.1
  65.1 0.7 gather_fusion.2
  65.8 0.9 fusion.69
  66.7 2.8 %collective-permute-start.2 = (bf16[14,64,128]{2,1,0:T(8,128)(2,1)}, bf16[14,64,128]{2,1,0:T(8,128)(2,1)}, u32[]{:S(2)}, u32[]{:S(2)}) collective-permute-start(bf16[14,64,128]{2,1,0:T(8,128)(2,1)} %get-tuple-element.29), channel_id=1, source_target_pairs={{0,3},{1,0},{2,1},{3,2},{4,7},{5,4},{6,5},{7,6},{8,11},{9,8},{10,9... | collective-permute-start | bytes 688136 | tf_op jit(solution)/shard_map/ppermute | solution.py:41
  69.5 0.8 collective-permute-start.1
  70.3 0.9 collective-permute-start
  71.8 1.1 copy.89
  73.6 5.0 %collective-permute-done.2 = bf16[14,64,128]{2,1,0:T(8,128)(2,1)} collective-permute-done((bf16[14,64,128]{2,1,0:T(8,128)(2,1)}, bf16[14,64,128]{2,1,0:T(8,128)(2,1)}, u32[]{:S(2)}, u32[]{:S(2)}) %collective-permute-start.2) | collective-permute-done | bytes 229408 | tf_op jit(solution)/shard_map/ppermute | solution.py:41
  78.6 1.1 collective-permute-done.1
  79.8 2.5 %collective-permute-done = bf16[14,64,128]{2,1,0:T(8,128)(2,1)} collective-permute-done((bf16[14,64,128]{2,1,0:T(8,128)(2,1)}, bf16[14,64,128]{2,1,0:T(8,128)(2,1)}, u32[]{:S(2)}, u32[]{:S(2)}) %collective-permute-start) | collective-permute-done | bytes 229408 | tf_op jit(solution)/shard_map/ppermute | solution.py:41
  82.3 1.3 pad_maximum_fusion.4
  83.6 0.8 gather_fusion.3
  84.5 1.3 fusion.2
  85.9 1.8 %fusion.7 = f32[2,8,128]{2,1,0:T(8,128)S(1)} fusion(f32[2,8,128]{2,1,0:T(8,128)S(1)} %get-tuple-element.39, f32[2,8,128,128,8]{3,2,4,1,0:T(8,128)S(1)} %get-tuple-element.40, pred[2,128,8,128]{1,3,2,0:T(8,128)(4,1)S(1)} %compare_and_fusion), kind=kLoop, calls=%fused_computation.29 | loop fusion | flops 8386560 | bytes 8667136 | tf_op jit(solution)/shard_map/reduce_sum | solution.py:119
  87.7 2.9 %multiply_reduce_fusion = (f32[2,128,8]{1,2,0:T(8,128)S(1)}, bf16[2,128,8,128]{1,3,2,0:T(8,128)(2,1)}) fusion(bf16[2,128,8,128]{1,3,2,0:T(8,128)(2,1)S(1)} %copy-done.6, f32[2,128,8]{1,2,0:T(8,128)S(1)} %bitcast.252, f32[2,8,128]{2,1,0:T(8,128)S(1)} %get-tuple-element.39, f32[2,8,128,128,8]{3,2,4,1,0:T(8,128)S(1)} %get-tuple-element.40, ...), kind=kOutput, calls=%fused_computation.48 | convolution fusion | flops 547878912 | bytes 10772480 | tf_op jit(solution)/shard_map/qhisj,qsjd->qihd/dot_general | solution.py:120
  90.6 2.3 %fusion.12 = f32[2,8,1,128,128]{4,3,1,0,2:T(8,128)S(1)} fusion(f32[2,8,128]{2,1,0:T(8,128)S(1)} %broadcast_divide_fusion, f32[2,8,128]{2,1,0:T(8,128)S(1)} %get-tuple-element.39, f32[2,8,128,128,8]{3,2,4,1,0:T(8,128)S(1)} %get-tuple-element.40, pred[2,128,8,128]{1,3,2,0:T(8,128)(4,1)S(1)} %compare_and_fusion, bf16[2,128,8,128,1]{3,2,1,0,4:T(8,128)(2,1)S(1)} %bitcast.218), kind=kOutput, calls=%fused_computation.33 | convolution fusion | flops 547356672 | bytes 10240000 | tf_op jit(solution)/shard_map/qhisj,qihd->qsjd/dot_general | solution.py:145
  93.0 3.1 %fusion.1 = bf16[2,8,128,8,128]{2,4,1,3,0:T(8,128)(2,1)S(1)} fusion(f32[2,8,128]{2,1,0:T(8,128)S(1)} %bitcast.253, f32[2,8,128]{2,1,0:T(8,128)S(1)} %broadcast_divide_fusion, f32[2,8,128]{2,1,0:T(8,128)S(1)} %get-tuple-element.39, f32[2,8,128,128,8]{3,2,4,1,0:T(8,128)S(1)} %get-tuple-element.40, pred[2,128,8,128]{1,3,2,0:T(8,128)(4,1)S(1)} %compare_and_fusion, ...), kind=kOutput, calls=%fused_computation.18 | convolution fusion | flops 552599552 | bytes 14442496 | tf_op jit(solution)/shard_map/qihd,qsjd->qhisj/dot_general | solution.py:131
  96.0 1.3 fusion.15
  99.6 0.8 collective-permute-start.10
  100.3 0.9 collective-permute-start.9
  101.8 5.6 %collective-permute-done.11 = bf16[14,64,128]{2,1,0:T(8,128)(2,1)S(1)} collective-permute-done((bf16[14,64,128]{2,1,0:T(8,128)(2,1)S(1)}, bf16[14,64,128]{2,1,0:T(8,128)(2,1)S(1)}, u32[]{:S(2)}, u32[]{:S(2)}) %collective-permute-start.11) | collective-permute-done | bytes 229408 | tf_op jit(solution)/shard_map/ppermute | solution.py:41
  107.4 2.2 %collective-permute-done.10 = bf16[14,64,128]{2,1,0:T(8,128)(2,1)S(1)} collective-permute-done((bf16[14,64,128]{2,1,0:T(8,128)(2,1)S(1)}, bf16[14,64,128]{2,1,0:T(8,128)(2,1)S(1)}, u32[]{:S(2)}, u32[]{:S(2)}) %collective-permute-start.10) | collective-permute-done | bytes 229408 | tf_op jit(solution)/shard_map/ppermute | solution.py:41
  109.6 3.3 %collective-permute-done.9 = bf16[14,64,128]{2,1,0:T(8,128)(2,1)S(1)} collective-permute-done((bf16[14,64,128]{2,1,0:T(8,128)(2,1)S(1)}, bf16[14,64,128]{2,1,0:T(8,128)(2,1)S(1)}, u32[]{:S(2)}, u32[]{:S(2)}) %collective-permute-start.9) | collective-permute-done | bytes 229408 | tf_op jit(solution)/shard_map/ppermute | solution.py:41
  113.0 1.0 gather_fusion.9
  114.1 1.8 %gather_fusion.10 = bf16[64,64,128]{2,1,0:T(8,128)(2,1)} fusion(bf16[57,64,128]{2,1,0:T(8,128)(2,1)S(1)} %concatenate.8, s32[1024]{0:T(1024)} %pad_clamp_fusion), kind=kCustom, calls=%fused_computation.10 | custom fusion | bytes 2097408 | tf_op jit(solution)/shard_map/gather | solution.py:162
  115.9 6.6 %all-to-all-start.2 = ((bf16[64,1,64,128]{3,2,1,0:T(8,128)(2,1)}), bf16[64,1,64,128]{3,2,1,0:T(8,128)(2,1)}, u32[]{:S(2)}, u32[]{:S(2)}) async-start(bf16[64,1,64,128]{3,2,1,0:T(8,128)(2,1)} %bitcast.78), calls=%async_computation.2 | async-start | bytes 2097152 | tf_op jit(solution)/shard_map/all_to_all | solution.py:163
  122.6 3.1 %fusion.17 = bf16[2,128,8,128]{1,3,2,0:T(8,128)(2,1)S(1)} fusion(bf16[2,8,128,8,128]{2,4,1,3,0:T(8,128)(2,1)} %copy-done.1, bf16[2,1,2,128,128]{4,3,1,0,2:T(8,128)(2,1)S(1)} %copy_bitcast_fusion, bf16[2,7,2,128,128]{4,3,2,1,0:T(8,128)(2,1)} %bitcast.232), kind=kOutput, calls=%fused_computation.40 | convolution fusion | flops 538443776 | bytes 5767168 | tf_op jit(solution)/shard_map/qhisj,qsjd->qihd/dot_general | solution.py:138
  126.3 0.9 copy.94
  127.9 1.1 maximum_bitcast_fusion
  129.1 0.7 gather_fusion.6
  129.9 1.2 collective-permute-start.8
  131.4 0.8 collective-permute-start.6
  132.2 6.9 %collective-permute-done.8 = bf16[2,256,256]{2,1,0:T(8,128)(2,1)S(1)} collective-permute-done((bf16[2,256,256]{2,1,0:T(8,128)(2,1)S(1)}, bf16[2,256,256]{2,1,0:T(8,128)(2,1)S(1)}, u32[]{:S(2)}, u32[]{:S(2)}) %collective-permute-start.8) | collective-permute-done | bytes 262176 | tf_op jit(solution)/shard_map/ppermute | solution.py:41
  139.2 2.6 %collective-permute-done.7 = bf16[2,256,256]{2,1,0:T(8,128)(2,1)S(1)} collective-permute-done((bf16[2,256,256]{2,1,0:T(8,128)(2,1)S(1)}, bf16[2,256,256]{2,1,0:T(8,128)(2,1)S(1)}, u32[]{:S(2)}, u32[]{:S(2)}) %collective-permute-start.7) | collective-permute-done | bytes 262176 | tf_op jit(solution)/shard_map/ppermute | solution.py:41
  141.8 4.4 %collective-permute-done.6 = bf16[2,256,256]{2,1,0:T(8,128)(2,1)S(1)} collective-permute-done((bf16[2,256,256]{2,1,0:T(8,128)(2,1)S(1)}, bf16[2,256,256]{2,1,0:T(8,128)(2,1)S(1)}, u32[]{:S(2)}, u32[]{:S(2)}) %collective-permute-start.6) | collective-permute-done | bytes 262176 | tf_op jit(solution)/shard_map/ppermute | solution.py:41
  146.4 1.7 %gather_fusion.7 = bf16[4,2,256,256]{3,2,1,0:T(8,128)(2,1)} fusion(bf16[4,2,256,256]{3,2,1,0:T(8,128)(2,1)S(1)} %pad_maximum_fusion.3, s32[1024]{0:T(1024)} %pad_clamp_fusion.1), kind=kCustom, calls=%fused_computation.7 | custom fusion | bytes 2097168 | tf_op jit(solution)/shard_map/gather | solution.py:43
  148.1 3.1 %all-to-all-done.2 = bf16[64,1,64,128]{3,2,1,0:T(8,128)(2,1)} async-done(((bf16[64,1,64,128]{3,2,1,0:T(8,128)(2,1)}), bf16[64,1,64,128]{3,2,1,0:T(8,128)(2,1)}, u32[]{:S(2)}, u32[]{:S(2)}) %all-to-all-start.2) | async-done | bytes 1048608 | tf_op jit(solution)/shard_map/all_to_all | solution.py:163
  151.2 1.5 bitcast_convert_fusion
  152.7 3.8 %scatter_fusion = f32[9,64,128]{2,1,0:T(8,128)S(1)} fusion(f32[9,64,128]{2,1,0:T(8,128)S(1)} %broadcast_in_dim.30, s32[64]{0:T(128)S(1)} %fusion.50, f32[64,64,128]{2,1,0:T(8,128)S(1)} %bitcast_convert_fusion), kind=kCustom, calls=%fused_computation.15 | custom fusion | flops 524288 | bytes 6291712 | tf_op jit(solution)/shard_map/scatter-add | solution.py:174
  157.2 1.1 collective-permute-start.14
  158.7 0.8 collective-permute-start.12
  159.5 2.2 %fusion.64 = (bf16[4,1,256,256]{3,2,1,0:T(8,128)(2,1)}, bf16[4,1,256,256]{3,2,1,0:T(8,128)(2,1)}) fusion(bf16[4,2,256,256]{3,2,1,0:T(8,128)(2,1)} %gather_fusion.7), kind=kLoop, calls=%fused_computation.157 | loop fusion | bytes 2097152 | tf_op jit(solution)/shard_map/slice | solution.py:187
  161.8 2.4 %collective-permute-done.13 = f32[2,64,128]{2,1,0:T(8,128)S(1)} collective-permute-done((f32[2,64,128]{2,1,0:T(8,128)S(1)}, f32[2,64,128]{2,1,0:T(8,128)S(1)}, u32[]{:S(2)}, u32[]{:S(2)}) %collective-permute-start.13) | collective-permute-done | bytes 65568 | tf_op jit(solution)/shard_map/ppermute | solution.py:41
  165.6 1.0 fusion.31
  (95 shorter events, 14.0 us)
Async XLA Ops:
  0.6 40.6 %copy-start.7 = (s32[8,8]{1,0:T(8,128)S(1)}, s32[8,8]{1,0:T(8,128)}, u32[]{:S(2)}) copy-start(s32[8,8]{1,0:T(8,128)} %param.9) | copy-start | bytes 772
  0.6 41.8 %copy-start.2 = (bf16[1024,128]{1,0:T(8,128)(2,1)S(1)}, bf16[1024,128]{1,0:T(8,128)(2,1)}, u32[]{:S(2)}) copy-start(bf16[1024,128]{1,0:T(8,128)(2,1)} %param.6) | copy-start | bytes 786436
  0.7 41.8 %copy-start.3 = (bf16[1024,128]{1,0:T(8,128)(2,1)S(1)}, bf16[1024,128]{1,0:T(8,128)(2,1)}, u32[]{:S(2)}) copy-start(bf16[1024,128]{1,0:T(8,128)(2,1)} %param.7) | copy-start | bytes 786436
  4.7 20.7 %all-to-all-start = ((s32[64,1,1]{2,1,0:T(1,128)}), s32[64,1,1]{2,1,0:T(1,128)S(1)}, u32[]{:S(2)}, u32[]{:S(2)}) async-start(s32[64,1,1]{2,1,0:T(1,128)} %copy.79), calls=%async_computation | async-start | bytes 65536 | tf_op jit(solution)/shard_map/all_to_all | solution.py:65
  19.3 78.8 %copy-start.8 = (s32[1024]{0:T(1024)}, s32[1024]{0:T(1024)S(1)}, u32[]{:S(2)}) copy-start(s32[1024]{0:T(1024)S(1)} %pad_clamp_fusion.2) | copy-start | bytes 12292
  29.8 34.4 %all-to-all-start.1 = ((bf16[64,1,64,128]{3,2,1,0:T(8,128)(2,1)}), bf16[64,1,64,128]{3,2,1,0:T(8,128)(2,1)S(1)}, u32[]{:S(2)}, u32[]{:S(2)}) async-start(bf16[64,1,64,128]{3,2,1,0:T(8,128)(2,1)} %bitcast.8), calls=%async_computation.1 | async-start | bytes 2097152 | tf_op jit(solution)/shard_map/all_to_all | solution.py:85
  36.3 14.6 %collective-permute-start.5 = (bf16[2,256,256]{2,1,0:T(8,128)(2,1)}, bf16[2,256,256]{2,1,0:T(8,128)(2,1)S(1)}, u32[]{:S(2)}, u32[]{:S(2)}) collective-permute-start(bf16[2,256,256]{2,1,0:T(8,128)(2,1)} %get-tuple-element.21), channel_id=1, source_target_pairs={{0,3},{1,0},{2,1},{3,2},{4,7},{5,4},{6,5},{7,6},{8,11},{9,8},{10,9... | collective-permute-start | bytes 786440 | tf_op jit(solution)/shard_map/ppermute | solution.py:41
  39.1 11.8 %collective-permute-start.4 = (bf16[2,256,256]{2,1,0:T(8,128)(2,1)}, bf16[2,256,256]{2,1,0:T(8,128)(2,1)S(1)}, u32[]{:S(2)}, u32[]{:S(2)}) collective-permute-start(bf16[2,256,256]{2,1,0:T(8,128)(2,1)} %get-tuple-element.19), channel_id=1, source_target_pairs={{0,2},{1,3},{2,0},{3,1},{4,6},{5,7},{6,4},{7,5},{8,10},{9,11},{10,... | collective-permute-start | bytes 786440 | tf_op jit(solution)/shard_map/ppermute | solution.py:41
  39.9 14.6 %collective-permute-start.3 = (bf16[2,256,256]{2,1,0:T(8,128)(2,1)S(1)}, bf16[2,256,256]{2,1,0:T(8,128)(2,1)S(1)}, u32[]{:S(2)}, u32[]{:S(2)}) collective-permute-start(bf16[2,256,256]{2,1,0:T(8,128)(2,1)S(1)} %get-tuple-element.20), channel_id=1, source_target_pairs={{0,1},{1,2},{2,3},{3,0},{4,5},{5,6},{6,7},{7,4},{8,9},{9,10},{10,1... | collective-permute-start | bytes 786440 | tf_op jit(solution)/shard_map/ppermute | solution.py:41
  66.7 11.9 %collective-permute-start.2 = (bf16[14,64,128]{2,1,0:T(8,128)(2,1)}, bf16[14,64,128]{2,1,0:T(8,128)(2,1)}, u32[]{:S(2)}, u32[]{:S(2)}) collective-permute-start(bf16[14,64,128]{2,1,0:T(8,128)(2,1)} %get-tuple-element.29), channel_id=1, source_target_pairs={{0,3},{1,0},{2,1},{3,2},{4,7},{5,4},{6,5},{7,6},{8,11},{9,8},{10,9... | collective-permute-start | bytes 688136 | tf_op jit(solution)/shard_map/ppermute | solution.py:41
  69.5 10.3 %collective-permute-start.1 = (bf16[14,64,128]{2,1,0:T(8,128)(2,1)}, bf16[14,64,128]{2,1,0:T(8,128)(2,1)}, u32[]{:S(2)}, u32[]{:S(2)}) collective-permute-start(bf16[14,64,128]{2,1,0:T(8,128)(2,1)} %get-tuple-element.27), channel_id=1, source_target_pairs={{0,2},{1,3},{2,0},{3,1},{4,6},{5,7},{6,4},{7,5},{8,10},{9,11},{10,... | collective-permute-start | bytes 688136 | tf_op jit(solution)/shard_map/ppermute | solution.py:41
  70.3 12.0 %collective-permute-start = (bf16[14,64,128]{2,1,0:T(8,128)(2,1)}, bf16[14,64,128]{2,1,0:T(8,128)(2,1)}, u32[]{:S(2)}, u32[]{:S(2)}) collective-permute-start(bf16[14,64,128]{2,1,0:T(8,128)(2,1)} %get-tuple-element.28), channel_id=1, source_target_pairs={{0,1},{1,2},{2,3},{3,0},{4,5},{5,6},{6,7},{7,4},{8,9},{9,10},{10,1... | collective-permute-start | bytes 688136 | tf_op jit(solution)/shard_map/ppermute | solution.py:41
  84.5 8.4 %copy-start.4 = (bf16[14,4,64,128]{3,2,1,0:T(8,128)(2,1)}, bf16[14,4,64,128]{3,2,1,0:T(8,128)(2,1)S(1)}, u32[]{:S(2)}) copy-start(bf16[14,4,64,128]{3,2,1,0:T(8,128)(2,1)S(1)} %copy.80) | copy-start | bytes 2752516
  84.5 3.2 %copy-start.6 = (bf16[2,128,8,128]{1,3,2,0:T(8,128)(2,1)S(1)}, bf16[2,128,8,128]{1,3,2,0:T(8,128)(2,1)}, u32[]{:S(2)}) copy-start(bf16[2,128,8,128]{1,3,2,0:T(8,128)(2,1)} %copy.89) | copy-start | bytes 1572868
  92.9 4.4 %copy-start = (f32[2,8,1,128,128]{4,3,1,0,2:T(8,128)}, f32[2,8,1,128,128]{4,3,1,0,2:T(8,128)S(1)}, u32[]{:S(2)}) copy-start(f32[2,8,1,128,128]{4,3,1,0,2:T(8,128)S(1)} %fusion.12) | copy-start | bytes 3145732
  96.0 2.0 %copy-start.1 = (bf16[2,8,128,8,128]{2,4,1,3,0:T(8,128)(2,1)}, bf16[2,8,128,8,128]{2,4,1,3,0:T(8,128)(2,1)S(1)}, u32[]{:S(2)}) copy-start(bf16[2,8,128,8,128]{2,4,1,3,0:T(8,128)(2,1)S(1)} %fusion.1) | copy-start | bytes 12582916
  98.9 8.6 %collective-permute-start.11 = (bf16[14,64,128]{2,1,0:T(8,128)(2,1)S(1)}, bf16[14,64,128]{2,1,0:T(8,128)(2,1)S(1)}, u32[]{:S(2)}, u32[]{:S(2)}) collective-permute-start(bf16[14,64,128]{2,1,0:T(8,128)(2,1)S(1)} %get-tuple-element.25), channel_id=1, source_target_pairs={{0,3},{1,0},{2,1},{3,2},{4,7},{5,4},{6,5},{7,6},{8,11},{9,8},{10,9... | collective-permute-start | bytes 688136 | tf_op jit(solution)/shard_map/ppermute | solution.py:41
  99.6 10.0 %collective-permute-start.10 = (bf16[14,64,128]{2,1,0:T(8,128)(2,1)S(1)}, bf16[14,64,128]{2,1,0:T(8,128)(2,1)S(1)}, u32[]{:S(2)}, u32[]{:S(2)}) collective-permute-start(bf16[14,64,128]{2,1,0:T(8,128)(2,1)S(1)} %get-tuple-element.23), channel_id=1, source_target_pairs={{0,2},{1,3},{2,0},{3,1},{4,6},{5,7},{6,4},{7,5},{8,10},{9,11},{10,... | collective-permute-start | bytes 688136 | tf_op jit(solution)/shard_map/ppermute | solution.py:41
  100.3 12.6 %collective-permute-start.9 = (bf16[14,64,128]{2,1,0:T(8,128)(2,1)S(1)}, bf16[14,64,128]{2,1,0:T(8,128)(2,1)S(1)}, u32[]{:S(2)}, u32[]{:S(2)}) collective-permute-start(bf16[14,64,128]{2,1,0:T(8,128)(2,1)S(1)} %get-tuple-element.24), channel_id=1, source_target_pairs={{0,1},{1,2},{2,3},{3,0},{4,5},{5,6},{6,7},{7,4},{8,9},{9,10},{10,1... | collective-permute-start | bytes 688136 | tf_op jit(solution)/shard_map/ppermute | solution.py:41
  113.0 14.2 %copy-start.5 = (bf16[2,128,8,128]{1,3,2,0:T(8,128)(2,1)S(1)}, bf16[2,128,8,128]{1,3,2,0:T(8,128)(2,1)}, u32[]{:S(2)}) copy-start(bf16[2,128,8,128]{1,3,2,0:T(8,128)(2,1)} %get-tuple-element.42) | copy-start | bytes 1572868
  115.9 35.3 %all-to-all-start.2 = ((bf16[64,1,64,128]{3,2,1,0:T(8,128)(2,1)}), bf16[64,1,64,128]{3,2,1,0:T(8,128)(2,1)}, u32[]{:S(2)}, u32[]{:S(2)}) async-start(bf16[64,1,64,128]{3,2,1,0:T(8,128)(2,1)} %bitcast.78), calls=%async_computation.2 | async-start | bytes 2097152 | tf_op jit(solution)/shard_map/all_to_all | solution.py:163
  125.7 6.5 %copy-start.9 = (s32[64]{0:T(128)S(1)}, s32[64]{0:T(128)}, u32[]{:S(2)}) copy-start(s32[64]{0:T(128)} %get-tuple-element.4) | copy-start | bytes 772
  129.9 9.3 %collective-permute-start.8 = (bf16[2,256,256]{2,1,0:T(8,128)(2,1)S(1)}, bf16[2,256,256]{2,1,0:T(8,128)(2,1)S(1)}, u32[]{:S(2)}, u32[]{:S(2)}) collective-permute-start(bf16[2,256,256]{2,1,0:T(8,128)(2,1)S(1)} %get-tuple-element.15), channel_id=1, source_target_pairs={{0,3},{1,0},{2,1},{3,2},{4,7},{5,4},{6,5},{7,6},{8,11},{9,8},{10,9... | collective-permute-start | bytes 786440 | tf_op jit(solution)/shard_map/ppermute | solution.py:41
  131.1 10.7 %collective-permute-start.7 = (bf16[2,256,256]{2,1,0:T(8,128)(2,1)S(1)}, bf16[2,256,256]{2,1,0:T(8,128)(2,1)S(1)}, u32[]{:S(2)}, u32[]{:S(2)}) collective-permute-start(bf16[2,256,256]{2,1,0:T(8,128)(2,1)S(1)} %get-tuple-element.13), channel_id=1, source_target_pairs={{0,2},{1,3},{2,0},{3,1},{4,6},{5,7},{6,4},{7,5},{8,10},{9,11},{10,... | collective-permute-start | bytes 786440 | tf_op jit(solution)/shard_map/ppermute | solution.py:41
  131.4 14.8 %collective-permute-start.6 = (bf16[2,256,256]{2,1,0:T(8,128)(2,1)S(1)}, bf16[2,256,256]{2,1,0:T(8,128)(2,1)S(1)}, u32[]{:S(2)}, u32[]{:S(2)}) collective-permute-start(bf16[2,256,256]{2,1,0:T(8,128)(2,1)S(1)} %get-tuple-element.14), channel_id=1, source_target_pairs={{0,1},{1,2},{2,3},{3,0},{4,5},{5,6},{6,7},{7,4},{8,9},{9,10},{10,1... | collective-permute-start | bytes 786440 | tf_op jit(solution)/shard_map/ppermute | solution.py:41
  157.2 4.5 %collective-permute-start.14 = (f32[2,64,128]{2,1,0:T(8,128)S(1)}, f32[2,64,128]{2,1,0:T(8,128)S(1)}, u32[]{:S(2)}, u32[]{:S(2)}) collective-permute-start(f32[2,64,128]{2,1,0:T(8,128)S(1)} %get-tuple-element.33), channel_id=1, source_target_pairs={{0,3},{1,0},{2,1},{3,2},{4,7},{5,4},{6,5},{7,6},{8,11},{9,8},{10,9... | collective-permute-start | bytes 196616 | tf_op jit(solution)/shard_map/ppermute | solution.py:41
  158.4 5.8 %collective-permute-start.13 = (f32[2,64,128]{2,1,0:T(8,128)S(1)}, f32[2,64,128]{2,1,0:T(8,128)S(1)}, u32[]{:S(2)}, u32[]{:S(2)}) collective-permute-start(f32[2,64,128]{2,1,0:T(8,128)S(1)} %get-tuple-element.31), channel_id=1, source_target_pairs={{0,2},{1,3},{2,0},{3,1},{4,6},{5,7},{6,4},{7,5},{8,10},{9,11},{10,... | collective-permute-start | bytes 196616 | tf_op jit(solution)/shard_map/ppermute | solution.py:41
  158.7 6.1 %collective-permute-start.12 = (f32[2,64,128]{2,1,0:T(8,128)S(1)}, f32[2,64,128]{2,1,0:T(8,128)S(1)}, u32[]{:S(2)}, u32[]{:S(2)}) collective-permute-start(f32[2,64,128]{2,1,0:T(8,128)S(1)} %get-tuple-element.32), channel_id=1, source_target_pairs={{0,1},{1,2},{2,3},{3,0},{4,5},{5,6},{6,7},{7,4},{8,9},{9,10},{10,1... | collective-permute-start | bytes 196616 | tf_op jit(solution)/shard_map/ppermute | solution.py:41

commit v5 on v0

--- a/solution.py
+++ b/solution.py
@@ -34,11 +34,13 @@
     return (owner_dev, local_blk, rank_in, usable)
 
 
-def head_exchange(x, head_idx, count):
+def head_exchange(x, head_idx, count, reorder=True):
     ahead = x[(head_idx + jnp.arange(count, dtype=jnp.int32)) % count]
     got = [ahead[0]]
     for k in range(1, count):
         got.append(lax.ppermute(ahead[k], "head", [(j, (j + k) % count) for j in range(count)]))
+    if not reorder:
+        return jnp.stack(got)
     order = (head_idx - jnp.arange(count, dtype=jnp.int32)) % count
     return jnp.stack(got)[order]
 
@@ -151,7 +153,7 @@
     )
     grad_tiles = jnp.stack([key_part, value_part], axis=2)
     remote_grad = grad_tiles[:, 1:].astype(jnp.bfloat16).reshape(my_entries, head_count, part_rows, HD)
-    back = head_exchange(jnp.transpose(remote_grad, (1, 0, 2, 3)), head_idx, head_count).reshape(
+    back = head_exchange(jnp.transpose(remote_grad, (1, 0, 2, 3)), head_idx, head_count, False).reshape(
         entry_count, part_rows, HD
     )
     slot_entry = (
@@ -160,7 +162,9 @@
         .set(jnp.arange(entry_count, dtype=jnp.int32))[:total_slots]
     )
     back = jnp.concatenate([back, jnp.zeros((1, part_rows, HD), back.dtype)], axis=0)
-    outgoing_part = back[slot_entry]
+    source_group = slot_entry // my_entries
+    by_shift = ((head_idx - source_group) % head_count) * my_entries + slot_entry % my_entries
+    outgoing_part = back[jnp.where(slot_entry < entry_count, by_shift, entry_count)]
     returned = lax.all_to_all(
         outgoing_part.reshape(pair_count, capacity, part_rows, HD),
         "ctx",

time: 167 us -> 165 us (0.988)
  other arithmetic: 21.4 us -> 19.4 us
  local copies, waits for them, and re-layouts: 26.9 us -> 24.9 us
  waiting for transfers between devices: 63.7 us -> 65.7 us
    ppermute x15, waiting for transfers between devices: 46.8 us -> 48.5 us  [head_exchange(): lax.ppermute(ahead[k], 'head', [(j, (j + k) % count) for j in range(count)])]
    gather x5 -> x4, local copies, waits for them, and re-layouts: 4.97 us -> 3.49 us  [head_exchange(): return jnp.stack(got)[order]]
  transfers between devices with their start and end apart: 18 -> 18, of which waited for: 16 -> 16; matrix products, arithmetic and copies ran while one was open for 14% -> 13% of each run, Pallas kernels for 0% -> 0%
where the time goes in v5:
time: 165 us
  waiting for transfers between devices  65.7 us (40%)
  starting transfers between devices  40.1 us (24%)
  local copies, waits for them, and re-layouts  24.9 us (15%)
  other arithmetic  19.4 us (12%)
  matrix products  13.5 us (8%)
    ppermute x15, waiting for transfers between devices, head_exchange(): lax.ppermute(ahead[k], 'head', [(j, (j + k) % count) for j in range(count)])  48.5 us
    ppermute x15, starting transfers between devices, head_exchange(): lax.ppermute(ahead[k], 'head', [(j, (j + k) % count) for j in range(count)])  15.8 us
    all_to_all x1, starting transfers between devices, on_device(): lax.all_to_all(req_table.reshape(pair_count, capacity), 'ctx', split_axis...  12.1 us
    all_to_all x1, waiting for transfers between devices, on_device(): lax.all_to_all(send_parts, 'ctx', split_axis=0, concat_axis=0, tiled=True)  8.1 us
    all_to_all x1, starting transfers between devices, on_device(): lax.all_to_all(outgoing_part.reshape(pair_count, capacity, part_rows, HD)...  6.64 us
    all_to_all x1, starting transfers between devices, on_device(): lax.all_to_all(send_parts, 'ctx', split_axis=0, concat_axis=0, tiled=True)  5.55 us
    all_to_all x1, waiting for transfers between devices, on_device(): lax.all_to_all(req_table.reshape(pair_count, capacity), 'ctx', split_axis...  5.48 us
    scatter-add x1, other arithmetic, on_device(): returned_sum = jnp.zeros((QB + 1, part_rows, HD), jnp.float32).at[target]...  3.75 us
  transfers between devices with their start and end apart: 18, of which 16 were waited for; matrix products, arithmetic and copies ran while one was open for 13% of the time, Pallas kernels for 0%

profile of v5, /device:TPU:8, one launch (start us, length us, event | category | flops | bytes accessed | tf_op | source)
XLA Modules:
  0.0 164.9 jit_solution(16483135827940379154)
XLA Ops:
  0.7 0.8 compare_and_fusion.1
  1.5 0.8 fusion.44
  3.2 0.8 scatter_custom_fusion
  4.0 0.7 copy.79
  4.7 12.1 %all-to-all-start = ((s32[64,1,1]{2,1,0:T(1,128)}), s32[64,1,1]{2,1,0:T(1,128)S(1)}, u32[]{:S(2)}, u32[]{:S(2)}) async-start(s32[64,1,1]{2,1,0:T(1,128)} %copy.79), calls=%async_computation | async-start | bytes 65536 | tf_op jit(solution)/shard_map/all_to_all | solution.py:67
  16.9 1.3 pad_maximum_fusion.1
  18.2 1.1 pad_maximum_fusion.6
  19.9 5.5 %all-to-all-done = s32[64,1,1]{2,1,0:T(1,128)S(1)} async-done(((s32[64,1,1]{2,1,0:T(1,128)}), s32[64,1,1]{2,1,0:T(1,128)S(1)}, u32[]{:S(2)}, u32[]{:S(2)}) %all-to-all-start) | async-done | bytes 288 | tf_op jit(solution)/shard_map/all_to_all | solution.py:67
  25.4 2.4 %fusion.72 = (s32[64]{0:T(128)S(1)}, s32[64]{0:T(128)S(1)}) fusion(s32[64,1,1]{2,1,0:T(1,128)S(1)} %all-to-all-done), kind=kLoop, calls=%fused_computation.166 | loop fusion | flops 64 | bytes 768 | tf_op jit(solution)/shard_map/all_to_all | solution.py:67
  27.8 1.7 %gather_fusion = bf16[64,64,128]{2,1,0:T(8,128)(2,1)} fusion(bf16[8,64,128]{2,1,0:T(8,128)(2,1)S(1)} %dynamic-slice_bitcast_fusion, s32[1024]{0:T(1024)S(1)} %pad_clamp_fusion.4), kind=kCustom, calls=%fused_computation | custom fusion | bytes 2097408 | tf_op jit(solution)/shard_map/gather | solution.py:86
  29.4 5.5 %all-to-all-start.1 = ((bf16[64,1,64,128]{3,2,1,0:T(8,128)(2,1)}), bf16[64,1,64,128]{3,2,1,0:T(8,128)(2,1)S(1)}, u32[]{:S(2)}, u32[]{:S(2)}) async-start(bf16[64,1,64,128]{3,2,1,0:T(8,128)(2,1)} %bitcast.8), calls=%async_computation.1 | async-start | bytes 2097152 | tf_op jit(solution)/shard_map/all_to_all | solution.py:87
  35.0 0.9 fusion.76
  35.9 2.8 %collective-permute-start.5 = (bf16[2,256,256]{2,1,0:T(8,128)(2,1)}, bf16[2,256,256]{2,1,0:T(8,128)(2,1)S(1)}, u32[]{:S(2)}, u32[]{:S(2)}) collective-permute-start(bf16[2,256,256]{2,1,0:T(8,128)(2,1)} %get-tuple-element.21), channel_id=1, source_target_pairs={{0,3},{1,0},{2,1},{3,2},{4,7},{5,4},{6,5},{7,6},{8,11},{9,8},{10,9... | collective-permute-start | bytes 786440 | tf_op jit(solution)/shard_map/ppermute | solution.py:41
  38.7 0.8 collective-permute-start.4
  39.5 0.9 collective-permute-start.3
  41.1 1.2 scatter_custom_fusion.1
  42.8 7.7 %collective-permute-done.5 = bf16[2,256,256]{2,1,0:T(8,128)(2,1)S(1)} collective-permute-done((bf16[2,256,256]{2,1,0:T(8,128)(2,1)}, bf16[2,256,256]{2,1,0:T(8,128)(2,1)S(1)}, u32[]{:S(2)}, u32[]{:S(2)}) %collective-permute-start.5) | collective-permute-done | bytes 262176 | tf_op jit(solution)/shard_map/ppermute | solution.py:41
  50.5 3.6 %collective-permute-done.3 = bf16[2,256,256]{2,1,0:T(8,128)(2,1)S(1)} collective-permute-done((bf16[2,256,256]{2,1,0:T(8,128)(2,1)S(1)}, bf16[2,256,256]{2,1,0:T(8,128)(2,1)S(1)}, u32[]{:S(2)}, u32[]{:S(2)}) %collective-permute-start.3) | collective-permute-done | bytes 262176 | tf_op jit(solution)/shard_map/ppermute | solution.py:41
  54.0 1.1 pad_maximum_fusion.2
  55.8 8.1 %all-to-all-done.1 = bf16[64,1,64,128]{3,2,1,0:T(8,128)(2,1)S(1)} async-done(((bf16[64,1,64,128]{3,2,1,0:T(8,128)(2,1)}), bf16[64,1,64,128]{3,2,1,0:T(8,128)(2,1)S(1)}, u32[]{:S(2)}, u32[]{:S(2)}) %all-to-all-start.1) | async-done | bytes 1048608 | tf_op jit(solution)/shard_map/all_to_all | solution.py:87
  63.9 0.7 gather_fusion.1
  64.6 0.7 gather_fusion.2
  65.3 0.9 fusion.78
  66.2 2.8 %collective-permute-start.2 = (bf16[14,64,128]{2,1,0:T(8,128)(2,1)}, bf16[14,64,128]{2,1,0:T(8,128)(2,1)}, u32[]{:S(2)}, u32[]{:S(2)}) collective-permute-start(bf16[14,64,128]{2,1,0:T(8,128)(2,1)} %get-tuple-element.29), channel_id=1, source_target_pairs={{0,3},{1,0},{2,1},{3,2},{4,7},{5,4},{6,5},{7,6},{8,11},{9,8},{10,9... | collective-permute-start | bytes 688136 | tf_op jit(solution)/shard_map/ppermute | solution.py:41
  69.0 0.8 collective-permute-start.1
  69.8 0.9 collective-permute-start
  72.0 1.1 copy.89
  73.1 5.0 %collective-permute-done.2 = bf16[14,64,128]{2,1,0:T(8,128)(2,1)} collective-permute-done((bf16[14,64,128]{2,1,0:T(8,128)(2,1)}, bf16[14,64,128]{2,1,0:T(8,128)(2,1)}, u32[]{:S(2)}, u32[]{:S(2)}) %collective-permute-start.2) | collective-permute-done | bytes 229408 | tf_op jit(solution)/shard_map/ppermute | solution.py:41
  78.2 1.1 collective-permute-done.1
  79.3 2.5 %collective-permute-done = bf16[14,64,128]{2,1,0:T(8,128)(2,1)} collective-permute-done((bf16[14,64,128]{2,1,0:T(8,128)(2,1)}, bf16[14,64,128]{2,1,0:T(8,128)(2,1)}, u32[]{:S(2)}, u32[]{:S(2)}) %collective-permute-start) | collective-permute-done | bytes 229408 | tf_op jit(solution)/shard_map/ppermute | solution.py:41
  81.8 1.4 pad_maximum_fusion.4
  83.2 0.7 gather_fusion.3
  84.1 1.3 fusion.5
  85.4 1.8 %fusion.2 = f32[2,8,128]{2,1,0:T(8,128)S(1)} fusion(f32[2,8,128,128,8]{3,2,4,1,0:T(8,128)S(1)} %get-tuple-element.40, f32[2,8,128]{2,1,0:T(8,128)S(1)} %get-tuple-element.39, pred[2,128,8,128]{1,3,2,0:T(8,128)(4,1)S(1)} %compare_and_fusion), kind=kLoop, calls=%fused_computation.21 | loop fusion | flops 8386560 | bytes 8667136 | tf_op jit(solution)/shard_map/reduce_sum | solution.py:121
  87.2 2.9 %multiply_reduce_fusion = (f32[2,128,8]{1,2,0:T(8,128)S(1)}, bf16[2,128,8,128]{1,3,2,0:T(8,128)(2,1)}) fusion(bf16[2,128,8,128]{1,3,2,0:T(8,128)(2,1)S(1)} %copy-done.6, f32[2,128,8]{1,2,0:T(8,128)S(1)} %bitcast.250, f32[2,8,128,128,8]{3,2,4,1,0:T(8,128)S(1)} %get-tuple-element.40, f32[2,8,128]{2,1,0:T(8,128)S(1)} %get-tuple-element.39, ...), kind=kOutput, calls=%fused_computation.49 | convolution fusion | flops 547878912 | bytes 10772480 | tf_op jit(solution)/shard_map/qhisj,qsjd->qihd/dot_general | solution.py:122
  90.2 2.0 %fusion.16 = f32[2,8,1,128,128]{4,3,1,0,2:T(8,128)S(1)} fusion(f32[2,8,128,128,8]{3,2,4,1,0:T(8,128)S(1)} %get-tuple-element.40, f32[2,8,128]{2,1,0:T(8,128)S(1)} %log_add_fusion, pred[2,128,8,128]{1,3,2,0:T(8,128)(4,1)S(1)} %compare_and_fusion, bf16[2,128,8,128,1]{3,2,1,0,4:T(8,128)(2,1)S(1)} %bitcast.216), kind=kOutput, calls=%fused_computation.34 | convolution fusion | flops 545259520 | bytes 10231808 | tf_op jit(solution)/shard_map/qhisj,qihd->qsjd/dot_general | solution.py:148
  92.2 2.8 %fusion.1 = bf16[2,8,128,8,128]{2,4,1,3,0:T(8,128)(2,1)S(1)} fusion(f32[2,8,128,128,8]{3,2,4,1,0:T(8,128)S(1)} %get-tuple-element.40, f32[2,8,128]{2,1,0:T(8,128)S(1)} %bitcast.251, f32[2,8,128]{2,1,0:T(8,128)S(1)} %log_add_fusion, pred[2,128,8,128]{1,3,2,0:T(8,128)(4,1)S(1)} %compare_and_fusion, bf16[2,128,8,128,1]{3,2,1,0,4:T(8,128)(2,1)S(1)} %bitcast.217, ...), kind=kOutput, calls=%fused_computation.17 | convolution fusion | flops 550502400 | bytes 14434304 | tf_op jit(solution)/shard_map/qihd,qsjd->qhisj/dot_general | solution.py:134
  95.0 1.3 fusion.21
  97.0 0.7 gather_fusion.8
  97.9 0.7 collective-permute-start.11
  98.6 0.8 collective-permute-start.10
  99.3 0.8 collective-permute-start.9
  100.2 6.2 %collective-permute-done.11 = bf16[14,64,128]{2,1,0:T(8,128)(2,1)S(1)} collective-permute-done((bf16[14,64,128]{2,1,0:T(8,128)(2,1)S(1)}, bf16[14,64,128]{2,1,0:T(8,128)(2,1)S(1)}, u32[]{:S(2)}, u32[]{:S(2)}) %collective-permute-start.11) | collective-permute-done | bytes 229408 | tf_op jit(solution)/shard_map/ppermute | solution.py:41
  106.4 2.2 %collective-permute-done.10 = bf16[14,64,128]{2,1,0:T(8,128)(2,1)S(1)} collective-permute-done((bf16[14,64,128]{2,1,0:T(8,128)(2,1)S(1)}, bf16[14,64,128]{2,1,0:T(8,128)(2,1)S(1)}, u32[]{:S(2)}, u32[]{:S(2)}) %collective-permute-start.10) | collective-permute-done | bytes 229408 | tf_op jit(solution)/shard_map/ppermute | solution.py:41
  108.6 3.5 %collective-permute-done.9 = bf16[14,64,128]{2,1,0:T(8,128)(2,1)S(1)} collective-permute-done((bf16[14,64,128]{2,1,0:T(8,128)(2,1)S(1)}, bf16[14,64,128]{2,1,0:T(8,128)(2,1)S(1)}, u32[]{:S(2)}, u32[]{:S(2)}) %collective-permute-start.9) | collective-permute-done | bytes 229408 | tf_op jit(solution)/shard_map/ppermute | solution.py:41
  112.3 1.7 %gather_fusion.9 = bf16[64,64,128]{2,1,0:T(8,128)(2,1)} fusion(bf16[57,64,128]{2,1,0:T(8,128)(2,1)S(1)} %concatenate.8, s32[1024]{0:T(1024)S(1)} %pad_clamp_fusion), kind=kCustom, calls=%fused_computation.9 | custom fusion | bytes 2097408 | tf_op jit(solution)/shard_map/gather | solution.py:167
  114.0 6.6 %all-to-all-start.2 = ((bf16[64,1,64,128]{3,2,1,0:T(8,128)(2,1)}), bf16[64,1,64,128]{3,2,1,0:T(8,128)(2,1)}, u32[]{:S(2)}, u32[]{:S(2)}) async-start(bf16[64,1,64,128]{3,2,1,0:T(8,128)(2,1)} %bitcast.78), calls=%async_computation.2 | async-start | bytes 2097152 | tf_op jit(solution)/shard_map/all_to_all | solution.py:168
  120.6 3.1 %fusion.23 = bf16[2,128,8,128]{1,3,2,0:T(8,128)(2,1)S(1)} fusion(bf16[2,8,128,8,128]{2,4,1,3,0:T(8,128)(2,1)} %copy-done.1, bf16[2,1,2,128,128]{4,3,1,0,2:T(8,128)(2,1)S(1)} %copy_bitcast_fusion, bf16[2,7,2,128,128]{4,3,2,1,0:T(8,128)(2,1)} %bitcast.230), kind=kOutput, calls=%fused_computation.41 | convolution fusion | flops 538443776 | bytes 5767168 | tf_op jit(solution)/shard_map/qhisj,qsjd->qihd/dot_general | solution.py:141
  124.4 0.9 copy.94
  126.0 1.1 maximum_bitcast_fusion
  127.9 0.9 collective-permute-start.8
  129.4 0.8 collective-permute-start.6
  130.2 6.9 %collective-permute-done.8 = bf16[2,256,256]{2,1,0:T(8,128)(2,1)S(1)} collective-permute-done((bf16[2,256,256]{2,1,0:T(8,128)(2,1)S(1)}, bf16[2,256,256]{2,1,0:T(8,128)(2,1)S(1)}, u32[]{:S(2)}, u32[]{:S(2)}) %collective-permute-start.8) | collective-permute-done | bytes 262176 | tf_op jit(solution)/shard_map/ppermute | solution.py:41
  137.1 2.4 %collective-permute-done.7 = bf16[2,256,256]{2,1,0:T(8,128)(2,1)S(1)} collective-permute-done((bf16[2,256,256]{2,1,0:T(8,128)(2,1)S(1)}, bf16[2,256,256]{2,1,0:T(8,128)(2,1)S(1)}, u32[]{:S(2)}, u32[]{:S(2)}) %collective-permute-start.7) | collective-permute-done | bytes 262176 | tf_op jit(solution)/shard_map/ppermute | solution.py:41
  139.5 4.4 %collective-permute-done.6 = bf16[2,256,256]{2,1,0:T(8,128)(2,1)S(1)} collective-permute-done((bf16[2,256,256]{2,1,0:T(8,128)(2,1)S(1)}, bf16[2,256,256]{2,1,0:T(8,128)(2,1)S(1)}, u32[]{:S(2)}, u32[]{:S(2)}) %collective-permute-start.6) | collective-permute-done | bytes 262176 | tf_op jit(solution)/shard_map/ppermute | solution.py:41
  144.1 1.6 gather_fusion.7
  145.7 3.6 %all-to-all-done.2 = bf16[64,1,64,128]{3,2,1,0:T(8,128)(2,1)} async-done(((bf16[64,1,64,128]{3,2,1,0:T(8,128)(2,1)}), bf16[64,1,64,128]{3,2,1,0:T(8,128)(2,1)}, u32[]{:S(2)}, u32[]{:S(2)}) %all-to-all-start.2) | async-done | bytes 1048608 | tf_op jit(solution)/shard_map/all_to_all | solution.py:168
  149.3 1.5 bitcast_convert_fusion
  150.8 3.8 %scatter_fusion = f32[9,64,128]{2,1,0:T(8,128)S(1)} fusion(f32[9,64,128]{2,1,0:T(8,128)S(1)} %broadcast_in_dim.31, s32[64]{0:T(128)S(1)} %fusion.59, f32[64,64,128]{2,1,0:T(8,128)S(1)} %bitcast_convert_fusion), kind=kCustom, calls=%fused_computation.14 | custom fusion | flops 524288 | bytes 6291712 | tf_op jit(solution)/shard_map/scatter-add | solution.py:179
  155.2 0.9 collective-permute-start.14
  156.7 0.8 collective-permute-start.12
  157.5 2.2 %fusion.73 = (bf16[4,1,256,256]{3,2,1,0:T(8,128)(2,1)}, bf16[4,1,256,256]{3,2,1,0:T(8,128)(2,1)}) fusion(bf16[4,2,256,256]{3,2,1,0:T(8,128)(2,1)} %gather_fusion.7), kind=kLoop, calls=%fused_computation.167 | loop fusion | bytes 2097152 | tf_op jit(solution)/shard_map/slice | solution.py:192
  159.8 2.2 %collective-permute-done.13 = f32[2,64,128]{2,1,0:T(8,128)S(1)} collective-permute-done((f32[2,64,128]{2,1,0:T(8,128)S(1)}, f32[2,64,128]{2,1,0:T(8,128)S(1)}, u32[]{:S(2)}, u32[]{:S(2)}) %collective-permute-start.13) | collective-permute-done | bytes 65568 | tf_op jit(solution)/shard_map/ppermute | solution.py:41
  163.2 1.0 fusion.37
  (92 shorter events, 11.6 us)
Async XLA Ops:
  0.6 40.2 %copy-start.7 = (s32[8,8]{1,0:T(8,128)S(1)}, s32[8,8]{1,0:T(8,128)}, u32[]{:S(2)}) copy-start(s32[8,8]{1,0:T(8,128)} %param.9) | copy-start | bytes 772
  0.6 40.2 %copy-start.2 = (bf16[1024,128]{1,0:T(8,128)(2,1)S(1)}, bf16[1024,128]{1,0:T(8,128)(2,1)}, u32[]{:S(2)}) copy-start(bf16[1024,128]{1,0:T(8,128)(2,1)} %param.6) | copy-start | bytes 786436
  0.7 40.2 %copy-start.3 = (bf16[1024,128]{1,0:T(8,128)(2,1)S(1)}, bf16[1024,128]{1,0:T(8,128)(2,1)}, u32[]{:S(2)}) copy-start(bf16[1024,128]{1,0:T(8,128)(2,1)} %param.7) | copy-start | bytes 786436
  4.7 20.7 %all-to-all-start = ((s32[64,1,1]{2,1,0:T(1,128)}), s32[64,1,1]{2,1,0:T(1,128)S(1)}, u32[]{:S(2)}, u32[]{:S(2)}) async-start(s32[64,1,1]{2,1,0:T(1,128)} %copy.79), calls=%async_computation | async-start | bytes 65536 | tf_op jit(solution)/shard_map/all_to_all | solution.py:67
  29.4 34.4 %all-to-all-start.1 = ((bf16[64,1,64,128]{3,2,1,0:T(8,128)(2,1)}), bf16[64,1,64,128]{3,2,1,0:T(8,128)(2,1)S(1)}, u32[]{:S(2)}, u32[]{:S(2)}) async-start(bf16[64,1,64,128]{3,2,1,0:T(8,128)(2,1)} %bitcast.8), calls=%async_computation.1 | async-start | bytes 2097152 | tf_op jit(solution)/shard_map/all_to_all | solution.py:87
  35.9 14.6 %collective-permute-start.5 = (bf16[2,256,256]{2,1,0:T(8,128)(2,1)}, bf16[2,256,256]{2,1,0:T(8,128)(2,1)S(1)}, u32[]{:S(2)}, u32[]{:S(2)}) collective-permute-start(bf16[2,256,256]{2,1,0:T(8,128)(2,1)} %get-tuple-element.21), channel_id=1, source_target_pairs={{0,3},{1,0},{2,1},{3,2},{4,7},{5,4},{6,5},{7,6},{8,11},{9,8},{10,9... | collective-permute-start | bytes 786440 | tf_op jit(solution)/shard_map/ppermute | solution.py:41
  38.7 11.8 %collective-permute-start.4 = (bf16[2,256,256]{2,1,0:T(8,128)(2,1)}, bf16[2,256,256]{2,1,0:T(8,128)(2,1)S(1)}, u32[]{:S(2)}, u32[]{:S(2)}) collective-permute-start(bf16[2,256,256]{2,1,0:T(8,128)(2,1)} %get-tuple-element.19), channel_id=1, source_target_pairs={{0,2},{1,3},{2,0},{3,1},{4,6},{5,7},{6,4},{7,5},{8,10},{9,11},{10,... | collective-permute-start | bytes 786440 | tf_op jit(solution)/shard_map/ppermute | solution.py:41
  39.5 14.6 %collective-permute-start.3 = (bf16[2,256,256]{2,1,0:T(8,128)(2,1)S(1)}, bf16[2,256,256]{2,1,0:T(8,128)(2,1)S(1)}, u32[]{:S(2)}, u32[]{:S(2)}) collective-permute-start(bf16[2,256,256]{2,1,0:T(8,128)(2,1)S(1)} %get-tuple-element.20), channel_id=1, source_target_pairs={{0,1},{1,2},{2,3},{3,0},{4,5},{5,6},{6,7},{7,4},{8,9},{9,10},{10,1... | collective-permute-start | bytes 786440 | tf_op jit(solution)/shard_map/ppermute | solution.py:41
  66.2 11.9 %collective-permute-start.2 = (bf16[14,64,128]{2,1,0:T(8,128)(2,1)}, bf16[14,64,128]{2,1,0:T(8,128)(2,1)}, u32[]{:S(2)}, u32[]{:S(2)}) collective-permute-start(bf16[14,64,128]{2,1,0:T(8,128)(2,1)} %get-tuple-element.29), channel_id=1, source_target_pairs={{0,3},{1,0},{2,1},{3,2},{4,7},{5,4},{6,5},{7,6},{8,11},{9,8},{10,9... | collective-permute-start | bytes 688136 | tf_op jit(solution)/shard_map/ppermute | solution.py:41
  69.0 10.3 %collective-permute-start.1 = (bf16[14,64,128]{2,1,0:T(8,128)(2,1)}, bf16[14,64,128]{2,1,0:T(8,128)(2,1)}, u32[]{:S(2)}, u32[]{:S(2)}) collective-permute-start(bf16[14,64,128]{2,1,0:T(8,128)(2,1)} %get-tuple-element.27), channel_id=1, source_target_pairs={{0,2},{1,3},{2,0},{3,1},{4,6},{5,7},{6,4},{7,5},{8,10},{9,11},{10,... | collective-permute-start | bytes 688136 | tf_op jit(solution)/shard_map/ppermute | solution.py:41
  69.8 12.0 %collective-permute-start = (bf16[14,64,128]{2,1,0:T(8,128)(2,1)}, bf16[14,64,128]{2,1,0:T(8,128)(2,1)}, u32[]{:S(2)}, u32[]{:S(2)}) collective-permute-start(bf16[14,64,128]{2,1,0:T(8,128)(2,1)} %get-tuple-element.28), channel_id=1, source_target_pairs={{0,1},{1,2},{2,3},{3,0},{4,5},{5,6},{6,7},{7,4},{8,9},{9,10},{10,1... | collective-permute-start | bytes 688136 | tf_op jit(solution)/shard_map/ppermute | solution.py:41
  84.0 8.1 %copy-start.4 = (bf16[14,4,64,128]{3,2,1,0:T(8,128)(2,1)}, bf16[14,4,64,128]{3,2,1,0:T(8,128)(2,1)S(1)}, u32[]{:S(2)}) copy-start(bf16[14,4,64,128]{3,2,1,0:T(8,128)(2,1)S(1)} %copy.80) | copy-start | bytes 2752516
  84.1 3.2 %copy-start.6 = (bf16[2,128,8,128]{1,3,2,0:T(8,128)(2,1)S(1)}, bf16[2,128,8,128]{1,3,2,0:T(8,128)(2,1)}, u32[]{:S(2)}) copy-start(bf16[2,128,8,128]{1,3,2,0:T(8,128)(2,1)} %copy.89) | copy-start | bytes 1572868
  92.2 4.1 %copy-start = (f32[2,8,1,128,128]{4,3,1,0,2:T(8,128)}, f32[2,8,1,128,128]{4,3,1,0,2:T(8,128)S(1)}, u32[]{:S(2)}) copy-start(f32[2,8,1,128,128]{4,3,1,0,2:T(8,128)S(1)} %fusion.16) | copy-start | bytes 3145732
  95.0 2.0 %copy-start.1 = (bf16[2,8,128,8,128]{2,4,1,3,0:T(8,128)(2,1)}, bf16[2,8,128,8,128]{2,4,1,3,0:T(8,128)(2,1)S(1)}, u32[]{:S(2)}) copy-start(bf16[2,8,128,8,128]{2,4,1,3,0:T(8,128)(2,1)S(1)} %fusion.1) | copy-start | bytes 12582916
  95.0 5.1 %copy-start.8 = (s32[65]{0:T(128)S(1)}, s32[65]{0:T(128)}, u32[]{:S(2)}) copy-start(s32[65]{0:T(128)} %scatter_custom_fusion.1) | copy-start | bytes 784
  97.9 8.6 %collective-permute-start.11 = (bf16[14,64,128]{2,1,0:T(8,128)(2,1)S(1)}, bf16[14,64,128]{2,1,0:T(8,128)(2,1)S(1)}, u32[]{:S(2)}, u32[]{:S(2)}) collective-permute-start(bf16[14,64,128]{2,1,0:T(8,128)(2,1)S(1)} %get-tuple-element.25), channel_id=1, source_target_pairs={{0,3},{1,0},{2,1},{3,2},{4,7},{5,4},{6,5},{7,6},{8,11},{9,8},{10,9... | collective-permute-start | bytes 688136 | tf_op jit(solution)/shard_map/ppermute | solution.py:41
  98.6 10.0 %collective-permute-start.10 = (bf16[14,64,128]{2,1,0:T(8,128)(2,1)S(1)}, bf16[14,64,128]{2,1,0:T(8,128)(2,1)S(1)}, u32[]{:S(2)}, u32[]{:S(2)}) collective-permute-start(bf16[14,64,128]{2,1,0:T(8,128)(2,1)S(1)} %get-tuple-element.23), channel_id=1, source_target_pairs={{0,2},{1,3},{2,0},{3,1},{4,6},{5,7},{6,4},{7,5},{8,10},{9,11},{10,... | collective-permute-start | bytes 688136 | tf_op jit(solution)/shard_map/ppermute | solution.py:41
  99.3 12.8 %collective-permute-start.9 = (bf16[14,64,128]{2,1,0:T(8,128)(2,1)S(1)}, bf16[14,64,128]{2,1,0:T(8,128)(2,1)S(1)}, u32[]{:S(2)}, u32[]{:S(2)}) collective-permute-start(bf16[14,64,128]{2,1,0:T(8,128)(2,1)S(1)} %get-tuple-element.24), channel_id=1, source_target_pairs={{0,1},{1,2},{2,3},{3,0},{4,5},{5,6},{6,7},{7,4},{8,9},{9,10},{10,1... | collective-permute-start | bytes 688136 | tf_op jit(solution)/shard_map/ppermute | solution.py:41
  112.1 13.2 %copy-start.5 = (bf16[2,128,8,128]{1,3,2,0:T(8,128)(2,1)S(1)}, bf16[2,128,8,128]{1,3,2,0:T(8,128)(2,1)}, u32[]{:S(2)}) copy-start(bf16[2,128,8,128]{1,3,2,0:T(8,128)(2,1)} %get-tuple-element.42) | copy-start | bytes 1572868
  114.0 35.3 %all-to-all-start.2 = ((bf16[64,1,64,128]{3,2,1,0:T(8,128)(2,1)}), bf16[64,1,64,128]{3,2,1,0:T(8,128)(2,1)}, u32[]{:S(2)}, u32[]{:S(2)}) async-start(bf16[64,1,64,128]{3,2,1,0:T(8,128)(2,1)} %bitcast.78), calls=%async_computation.2 | async-start | bytes 2097152 | tf_op jit(solution)/shard_map/all_to_all | solution.py:168
  127.9 9.3 %collective-permute-start.8 = (bf16[2,256,256]{2,1,0:T(8,128)(2,1)S(1)}, bf16[2,256,256]{2,1,0:T(8,128)(2,1)S(1)}, u32[]{:S(2)}, u32[]{:S(2)}) collective-permute-start(bf16[2,256,256]{2,1,0:T(8,128)(2,1)S(1)} %get-tuple-element.15), channel_id=1, source_target_pairs={{0,3},{1,0},{2,1},{3,2},{4,7},{5,4},{6,5},{7,6},{8,11},{9,8},{10,9... | collective-permute-start | bytes 786440 | tf_op jit(solution)/shard_map/ppermute | solution.py:41
  128.8 10.7 %collective-permute-start.7 = (bf16[2,256,256]{2,1,0:T(8,128)(2,1)S(1)}, bf16[2,256,256]{2,1,0:T(8,128)(2,1)S(1)}, u32[]{:S(2)}, u32[]{:S(2)}) collective-permute-start(bf16[2,256,256]{2,1,0:T(8,128)(2,1)S(1)} %get-tuple-element.13), channel_id=1, source_target_pairs={{0,2},{1,3},{2,0},{3,1},{4,6},{5,7},{6,4},{7,5},{8,10},{9,11},{10,... | collective-permute-start | bytes 786440 | tf_op jit(solution)/shard_map/ppermute | solution.py:41
  129.4 14.6 %collective-permute-start.6 = (bf16[2,256,256]{2,1,0:T(8,128)(2,1)S(1)}, bf16[2,256,256]{2,1,0:T(8,128)(2,1)S(1)}, u32[]{:S(2)}, u32[]{:S(2)}) collective-permute-start(bf16[2,256,256]{2,1,0:T(8,128)(2,1)S(1)} %get-tuple-element.14), channel_id=1, source_target_pairs={{0,1},{1,2},{2,3},{3,0},{4,5},{5,6},{6,7},{7,4},{8,9},{9,10},{10,1... | collective-permute-start | bytes 786440 | tf_op jit(solution)/shard_map/ppermute | solution.py:41
  155.2 4.5 %collective-permute-start.14 = (f32[2,64,128]{2,1,0:T(8,128)S(1)}, f32[2,64,128]{2,1,0:T(8,128)S(1)}, u32[]{:S(2)}, u32[]{:S(2)}) collective-permute-start(f32[2,64,128]{2,1,0:T(8,128)S(1)} %get-tuple-element.33), channel_id=1, source_target_pairs={{0,3},{1,0},{2,1},{3,2},{4,7},{5,4},{6,5},{7,6},{8,11},{9,8},{10,9... | collective-permute-start | bytes 196616 | tf_op jit(solution)/shard_map/ppermute | solution.py:41
  156.1 5.8 %collective-permute-start.13 = (f32[2,64,128]{2,1,0:T(8,128)S(1)}, f32[2,64,128]{2,1,0:T(8,128)S(1)}, u32[]{:S(2)}, u32[]{:S(2)}) collective-permute-start(f32[2,64,128]{2,1,0:T(8,128)S(1)} %get-tuple-element.31), channel_id=1, source_target_pairs={{0,2},{1,3},{2,0},{3,1},{4,6},{5,7},{6,4},{7,5},{8,10},{9,11},{10,... | collective-permute-start | bytes 196616 | tf_op jit(solution)/shard_map/ppermute | solution.py:41
  156.7 5.9 %collective-permute-start.12 = (f32[2,64,128]{2,1,0:T(8,128)S(1)}, f32[2,64,128]{2,1,0:T(8,128)S(1)}, u32[]{:S(2)}, u32[]{:S(2)}) collective-permute-start(f32[2,64,128]{2,1,0:T(8,128)S(1)} %get-tuple-element.32), channel_id=1, source_target_pairs={{0,1},{1,2},{2,3},{3,0},{4,5},{5,6},{6,7},{7,4},{8,9},{9,10},{10,1... | collective-permute-start | bytes 196616 | tf_op jit(solution)/shard_map/ppermute | solution.py:41
